TPU v7x, 32 devices: a whole 2x2x4 slice. The times are simulated.
32 devices in a mesh: stratum: 4 (over y, x), user: 8 (over z, core).
Axes of the slice: x: 2, y: 2, z: 4, core: 2. Of those that a mesh axis runs over, the one named last changes fastest.
Arguments:
- users: bfloat16 [32768, 512], P(('stratum', 'user')), may hold values from -6 to 6
- items: float32 [256, 512], P(('stratum', 'user')), may hold values from -6 to 6
- momentum: float32 [256, 512], P(('stratum', 'user')), may hold values from -30 to 30
- ratings: bfloat16 [32768, 4, 64], P(('stratum', 'user')), may hold values from -6.25 to 6.25, as said below
Outputs:
- new_users: bfloat16 [32768, 512], P(('stratum', 'user'))
- new_items: float32 [256, 512], P(('stratum', 'user'))
- new_momentum: float32 [256, 512], P(('stratum', 'user'))
Inputs may be any that keep to these rules, and one draw needn't show every extreme that they name: `ratings`: an entry equal to zero marks an unobserved rating; every observed rating has magnitude 0.25 or more.
All inputs are finite; a program needn't handle non-finite values.
Results may differ from a plain program's by a relative error of at most 0.013.
The roundings to bfloat16 on the way count: a program that leaves them out, or rounds other values in their place, can miss the bound.
Values may be sent and summed in bfloat16 or wider, within the bound.
No kernel may reach another device: no remote copies, remote signals or barrier semaphores. Data moves between devices by JAX's collectives and lax.ppermute only.
A program may use at most 64 MiB of HBM per device.

v0:
```python
import jax
import jax.numpy as jnp
from jax import lax
from jax.sharding import PartitionSpec as P


AXES = ("stratum", "user")
user_rate = 1.0
item_rate = 0.04
inertia = 0.6


def wide(block):
    return block.astype(jnp.float32)


def narrow(block):
    return block.astype(jnp.bfloat16)


def route(block, target):
    strata, users = lax.axis_size("stratum"), lax.axis_size("user")
    pairs = []
    for s in range(strata):
        for u in range(users):
            there, who = target(s, u)
            pairs.append((s * users + u, there % strata * users + who))
    return lax.ppermute(block, AXES, pairs)


def swap(block, bits):
    return route(block, lambda s, u: (s, u ^ bits))


def even_to_odd(block, bits):
    return route(block, lambda s, u: (s, u ^ 1) if u % 2 else (s, u ^ bits ^ 1))


def odd_to_even_back(block, bits):
    return route(block, lambda s, u: (s - 1, u ^ bits ^ 1) if u % 2 else (s, u ^ 1))


def local(users, items, momentum, ratings):
    steps, rank = ratings.shape[1], users.shape[1]
    factor = rank ** (-0.5)
    own = items.shape[0]
    n = lax.axis_size("user")
    slices = n // 2
    top = n // 2
    me = lax.axis_index("user")
    core, place = me % 2, me // 2

    def in_order(mine, other, late):
        return jnp.concatenate(
            [jnp.where(late == 0, mine, other), jnp.where(late == 0, other, mine)], axis=0
        )

    def chip_rows(block):
        return lax.dynamic_slice_in_dim(block, place * 2 * own, 2 * own, 0)

    mine = narrow(items)
    block, bit = mine, 1
    while bit < top // 2:
        block = in_order(block, swap(block, bit), me // bit % 2)
        bit *= 2
    block = in_order(block, even_to_odd(block, bit), me // bit % 2)
    far = route(block, lambda s, u: (s, u ^ top ^ 1) if u % 2 else (s, u ^ 1))
    block = in_order(swap(block, 1), far, me // top)
    whole = jnp.where(core == 0, block, swap(block, 1))
    tiles = [ratings[:, step, :] for step in range(steps)]
    tiles[0] = lax.optimization_barrier(tiles[0])

    owner = lax.broadcasted_iota(jnp.int32, (n, own, rank), 0)
    share = jnp.where(owner == me, inertia * momentum[None], 0.0).reshape(-1, rank)
    for step in range(steps):
        last = step == steps - 1
        score = lax.dot_general(
            users, whole, (((1,), (1,)), ((), ())), preferred_element_type=jnp.float32
        )
        resid = narrow(jnp.where(tiles[step] != 0, score * factor - wide(tiles[step]), 0.0))
        grads = lax.dot_general(
            resid, users, (((0,), (0,)), ((), ())), preferred_element_type=jnp.float32
        )
        grads = factor * grads + share
        total = narrow(grads + wide(swap(narrow(grads), 1)))
        bit = 4
        while bit < top:
            total = narrow(wide(total) + wide(swap(total, bit)))
            bit *= 2
        value = chip_rows(whole) if last else whole
        other = even_to_odd(total, 2)
        value, _ = lax.optimization_barrier((value, total))
        value = odd_to_even_back(value, 0)
        total = narrow(wide(total) + wide(other))
        far, near = total, total
        if last:
            far = lax.dynamic_slice_in_dim(total, (place ^ (top // 2)) * 2 * own, 2 * own, 0)
            near = chip_rows(total)
        far = odd_to_even_back(far, top)
        near = odd_to_even_back(near, 0)
        change = jnp.dot(resid, whole, preferred_element_type=jnp.float32)
        users = narrow(wide(users) - user_rate * factor * change)
        moment = wide(near) + wide(far)
        fresh = wide(value) - item_rate * moment
        if last:
            both = jnp.concatenate([fresh, moment], axis=0).reshape(2, 2, own, rank)
            got = swap(both[:, 1], 1)
            fresh, moment = jnp.where(core == 0, both[:, 0], got)
        else:
            fresh = narrow(fresh)
            whole = jnp.where(core == 0, fresh, swap(fresh, 1))
            share = jnp.where(core == 0, (inertia / slices) * moment, 0.0)
    return users, fresh, moment


def solution(mesh):
    rows = P(AXES, None)
    return jax.shard_map(
        local,
        mesh=mesh,
        in_specs=(rows, rows, rows, P(AXES, None, None)),
        out_specs=(rows, rows, rows),
        check_vma=False,
    )
```

profile of v0, /device:TPU:0, one launch (start us, length us, event | category | flops | bytes accessed | tf_op | source)
XLA Modules:
  0.0 70.3 jit_solution(10496869753910110370)
XLA Ops:
  3.5 2.7 %collective-permute-start.1 = (bf16[16,512]{1,0:T(8,128)(2,1)S(1)}, bf16[16,512]{1,0:T(8,128)(2,1)S(1)}, u32[]{:S(2)}, u32[]{:S(2)}) collective-permute-start(bf16[16,512]{1,0:T(8,128)(2,1)S(1)} %pad_maximum_fusion.3), channel_id=1, source_target_pairs={{0,3},{1,0},{2,1},{3,2},{4,7},{5,4},{6,5},{7,6},{8,11},{9,8},{10,9... | collective-permute-start | bytes 49160 | tf_op jit(solution)/shard_map/ppermute | solution.py:28
  8.9 3.3 %collective-permute-done.3 = bf16[32,512]{1,0:T(8,128)(2,1)S(1)} collective-permute-done((bf16[32,512]{1,0:T(8,128)(2,1)S(1)}, bf16[32,512]{1,0:T(8,128)(2,1)S(1)}, u32[]{:S(2)}, u32[]{:S(2)}) %collective-permute-start.3) | collective-permute-done | bytes 32800 | tf_op jit(solution)/shard_map/ppermute | solution.py:28
  14.6 1.1 %collective-permute-done.5 = bf16[64,512]{1,0:T(8,128)(2,1)S(1)} collective-permute-done((bf16[64,512]{1,0:T(8,128)(2,1)S(1)}, bf16[64,512]{1,0:T(8,128)(2,1)S(1)}, u32[]{:S(2)}, u32[]{:S(2)}) %collective-permute-start.5) | collective-permute-done | bytes 65568 | tf_op jit(solution)/shard_map/ppermute | solution.py:28
  15.7 1.6 %collective-permute-start.7 = (bf16[64,512]{1,0:T(8,128)(2,1)S(1)}, bf16[64,512]{1,0:T(8,128)(2,1)S(1)}, u32[]{:S(2)}, u32[]{:S(2)}) collective-permute-start(bf16[64,512]{1,0:T(8,128)(2,1)S(1)} %add_convert_fusion.7), channel_id=1, source_target_pairs={{0,3},{1,0},{2,1},{3,2},{4,7},{5,4},{6,5},{7,6},{8,11},{9,8},{10,9... | collective-permute-start | bytes 196616 | tf_op jit(solution)/shard_map/ppermute | solution.py:28
  17.4 1.9 %collective-permute-done.7 = bf16[64,512]{1,0:T(8,128)(2,1)S(1)} collective-permute-done((bf16[64,512]{1,0:T(8,128)(2,1)S(1)}, bf16[64,512]{1,0:T(8,128)(2,1)S(1)}, u32[]{:S(2)}, u32[]{:S(2)}) %collective-permute-start.7) | collective-permute-done | bytes 65568 | tf_op jit(solution)/shard_map/ppermute | solution.py:28
  20.0 1.9 %collective-permute-start.9 = (bf16[64,512]{1,0:T(8,128)(2,1)S(1)}, bf16[64,512]{1,0:T(8,128)(2,1)S(1)}, u32[]{:S(2)}, u32[]{:S(2)}) collective-permute-start(bf16[64,512]{1,0:T(8,128)(2,1)S(1)} %add_convert_fusion.6), channel_id=1, source_target_pairs={{0,1},{1,28},{2,3},{3,30},{4,5},{5,24},{6,7},{7,26},{8,9},{9,4},{1... | collective-permute-start | bytes 196616 | tf_op jit(solution)/shard_map/ppermute | solution.py:28
  21.9 1.1 %collective-permute-done.8 = bf16[64,512]{1,0:T(8,128)(2,1)S(1)} collective-permute-done((bf16[64,512]{1,0:T(8,128)(2,1)S(1)}, bf16[64,512]{1,0:T(8,128)(2,1)S(1)}, u32[]{:S(2)}, u32[]{:S(2)}) %collective-permute-start.8) | collective-permute-done | bytes 65568 | tf_op jit(solution)/shard_map/ppermute | solution.py:28
  23.0 2.5 %collective-permute-done.9 = bf16[64,512]{1,0:T(8,128)(2,1)S(1)} collective-permute-done((bf16[64,512]{1,0:T(8,128)(2,1)S(1)}, bf16[64,512]{1,0:T(8,128)(2,1)S(1)}, u32[]{:S(2)}, u32[]{:S(2)}) %collective-permute-start.9) | collective-permute-done | bytes 65568 | tf_op jit(solution)/shard_map/ppermute | solution.py:28
  29.0 2.1 %collective-permute-start.13 = (bf16[64,512]{1,0:T(8,128)(2,1)S(1)}, bf16[64,512]{1,0:T(8,128)(2,1)S(1)}, u32[]{:S(2)}, u32[]{:S(2)}) collective-permute-start(bf16[64,512]{1,0:T(8,128)(2,1)S(1)} %add_convert_fusion.5), channel_id=1, source_target_pairs={{0,3},{1,0},{2,1},{3,2},{4,7},{5,4},{6,5},{7,6},{8,11},{9,8},{10,9... | collective-permute-start | bytes 196616 | tf_op jit(solution)/shard_map/ppermute | solution.py:28
  31.1 1.9 %collective-permute-done.13 = bf16[64,512]{1,0:T(8,128)(2,1)S(1)} collective-permute-done((bf16[64,512]{1,0:T(8,128)(2,1)S(1)}, bf16[64,512]{1,0:T(8,128)(2,1)S(1)}, u32[]{:S(2)}, u32[]{:S(2)}) %collective-permute-start.13) | collective-permute-done | bytes 65568 | tf_op jit(solution)/shard_map/ppermute | solution.py:28
  33.8 1.9 %collective-permute-start.15 = (bf16[64,512]{1,0:T(8,128)(2,1)S(1)}, bf16[64,512]{1,0:T(8,128)(2,1)S(1)}, u32[]{:S(2)}, u32[]{:S(2)}) collective-permute-start(bf16[64,512]{1,0:T(8,128)(2,1)S(1)} %add_convert_fusion.4), channel_id=1, source_target_pairs={{0,1},{1,28},{2,3},{3,30},{4,5},{5,24},{6,7},{7,26},{8,9},{9,4},{1... | collective-permute-start | bytes 196616 | tf_op jit(solution)/shard_map/ppermute | solution.py:28
  35.7 1.1 %collective-permute-done.14 = bf16[64,512]{1,0:T(8,128)(2,1)S(1)} collective-permute-done((bf16[64,512]{1,0:T(8,128)(2,1)S(1)}, bf16[64,512]{1,0:T(8,128)(2,1)S(1)}, u32[]{:S(2)}, u32[]{:S(2)}) %collective-permute-start.14) | collective-permute-done | bytes 65568 | tf_op jit(solution)/shard_map/ppermute | solution.py:28
  36.8 2.5 %collective-permute-done.15 = bf16[64,512]{1,0:T(8,128)(2,1)S(1)} collective-permute-done((bf16[64,512]{1,0:T(8,128)(2,1)S(1)}, bf16[64,512]{1,0:T(8,128)(2,1)S(1)}, u32[]{:S(2)}, u32[]{:S(2)}) %collective-permute-start.15) | collective-permute-done | bytes 65568 | tf_op jit(solution)/shard_map/ppermute | solution.py:28
  43.2 2.1 %collective-permute-start.19 = (bf16[64,512]{1,0:T(8,128)(2,1)S(1)}, bf16[64,512]{1,0:T(8,128)(2,1)S(1)}, u32[]{:S(2)}, u32[]{:S(2)}) collective-permute-start(bf16[64,512]{1,0:T(8,128)(2,1)S(1)} %add_convert_fusion.3), channel_id=1, source_target_pairs={{0,3},{1,0},{2,1},{3,2},{4,7},{5,4},{6,5},{7,6},{8,11},{9,8},{10,9... | collective-permute-start | bytes 196616 | tf_op jit(solution)/shard_map/ppermute | solution.py:28
  45.3 1.9 %collective-permute-done.19 = bf16[64,512]{1,0:T(8,128)(2,1)S(1)} collective-permute-done((bf16[64,512]{1,0:T(8,128)(2,1)S(1)}, bf16[64,512]{1,0:T(8,128)(2,1)S(1)}, u32[]{:S(2)}, u32[]{:S(2)}) %collective-permute-start.19) | collective-permute-done | bytes 65568 | tf_op jit(solution)/shard_map/ppermute | solution.py:28
  47.7 1.9 %collective-permute-start.21 = (bf16[64,512]{1,0:T(8,128)(2,1)S(1)}, bf16[64,512]{1,0:T(8,128)(2,1)S(1)}, u32[]{:S(2)}, u32[]{:S(2)}) collective-permute-start(bf16[64,512]{1,0:T(8,128)(2,1)S(1)} %add_convert_fusion.2), channel_id=1, source_target_pairs={{0,1},{1,28},{2,3},{3,30},{4,5},{5,24},{6,7},{7,26},{8,9},{9,4},{1... | collective-permute-start | bytes 196616 | tf_op jit(solution)/shard_map/ppermute | solution.py:28
  49.6 1.4 %collective-permute-done.20 = bf16[64,512]{1,0:T(8,128)(2,1)S(1)} collective-permute-done((bf16[64,512]{1,0:T(8,128)(2,1)S(1)}, bf16[64,512]{1,0:T(8,128)(2,1)S(1)}, u32[]{:S(2)}, u32[]{:S(2)}) %collective-permute-start.20) | collective-permute-done | bytes 65568 | tf_op jit(solution)/shard_map/ppermute | solution.py:28
  51.0 2.6 %collective-permute-done.21 = bf16[64,512]{1,0:T(8,128)(2,1)S(1)} collective-permute-done((bf16[64,512]{1,0:T(8,128)(2,1)S(1)}, bf16[64,512]{1,0:T(8,128)(2,1)S(1)}, u32[]{:S(2)}, u32[]{:S(2)}) %collective-permute-start.21) | collective-permute-done | bytes 65568 | tf_op jit(solution)/shard_map/ppermute | solution.py:28
  57.4 2.1 %collective-permute-start.25 = (bf16[64,512]{1,0:T(8,128)(2,1)S(1)}, bf16[64,512]{1,0:T(8,128)(2,1)S(1)}, u32[]{:S(2)}, u32[]{:S(2)}) collective-permute-start(bf16[64,512]{1,0:T(8,128)(2,1)S(1)} %add_convert_fusion.1), channel_id=1, source_target_pairs={{0,3},{1,0},{2,1},{3,2},{4,7},{5,4},{6,5},{7,6},{8,11},{9,8},{10,9... | collective-permute-start | bytes 196616 | tf_op jit(solution)/shard_map/ppermute | solution.py:28
  59.5 1.9 %collective-permute-done.25 = bf16[64,512]{1,0:T(8,128)(2,1)S(1)} collective-permute-done((bf16[64,512]{1,0:T(8,128)(2,1)S(1)}, bf16[64,512]{1,0:T(8,128)(2,1)S(1)}, u32[]{:S(2)}, u32[]{:S(2)}) %collective-permute-start.25) | collective-permute-done | bytes 65568 | tf_op jit(solution)/shard_map/ppermute | solution.py:28
  61.7 1.8 %collective-permute-start.27 = (bf16[16,512]{1,0:T(8,128)(2,1)S(1)}, bf16[16,512]{1,0:T(8,128)(2,1)S(1)}, u32[]{:S(2)}, u32[]{:S(2)}) collective-permute-start(bf16[16,512]{1,0:T(8,128)(2,1)S(1)} %get-tuple-element.12), channel_id=1, source_target_pairs={{0,1},{1,28},{2,3},{3,30},{4,5},{5,24},{6,7},{7,26},{8,9},{9,4},{1... | collective-permute-start | bytes 49160 | tf_op jit(solution)/shard_map/ppermute | solution.py:28
  63.5 2.1 %collective-permute-done.26 = bf16[16,512]{1,0:T(8,128)(2,1)S(1)} collective-permute-done((bf16[16,512]{1,0:T(8,128)(2,1)S(1)}, bf16[16,512]{1,0:T(8,128)(2,1)S(1)}, u32[]{:S(2)}, u32[]{:S(2)}) %collective-permute-start.26) | collective-permute-done | bytes 16416 | tf_op jit(solution)/shard_map/ppermute | solution.py:28
  65.6 1.6 %collective-permute-done.27 = bf16[16,512]{1,0:T(8,128)(2,1)S(1)} collective-permute-done((bf16[16,512]{1,0:T(8,128)(2,1)S(1)}, bf16[16,512]{1,0:T(8,128)(2,1)S(1)}, u32[]{:S(2)}, u32[]{:S(2)}) %collective-permute-start.27) | collective-permute-done | bytes 16416 | tf_op jit(solution)/shard_map/ppermute | solution.py:28
  68.2 1.4 %subtract_convert_fusion = bf16[1024,512]{1,0:T(8,128)(2,1)} fusion(bf16[1024,512]{1,0:T(8,128)(2,1)S(1)} %subtract_convert_fusion.1, bf16[1024,64]{0,1:T(8,128)(2,1)S(1)} %fusion.12, bf16[64,512]{1,0:T(8,128)(2,1)S(1)} %broadcast_select_fusion), kind=kOutput, calls=%fused_computation | convolution fusion | flops 69206016 | bytes 2293760 | tf_op jit(solution)/shard_map/dot_general | solution.py:101
  (84 shorter events, 23.0 us)
Async XLA Ops:
  1.4 1.3 %collective-permute-start = (bf16[8,512]{1,0:T(8,128)(2,1)S(1)}, bf16[8,512]{1,0:T(8,128)(2,1)S(1)}, u32[]{:S(2)}, u32[]{:S(2)}) collective-permute-start(bf16[8,512]{1,0:T(8,128)(2,1)S(1)} %convert_element_type.178), channel_id=1, source_target_pairs={{0,1},{1,0},{2,3},{3,2},{4,5},{5,4},{6,7},{7,6},{8,9},{9,8},{10,11... | collective-permute-start | bytes 24584 | tf_op jit(solution)/shard_map/ppermute | solution.py:28
  3.5 4.1 %collective-permute-start.1 = (bf16[16,512]{1,0:T(8,128)(2,1)S(1)}, bf16[16,512]{1,0:T(8,128)(2,1)S(1)}, u32[]{:S(2)}, u32[]{:S(2)}) collective-permute-start(bf16[16,512]{1,0:T(8,128)(2,1)S(1)} %pad_maximum_fusion.3), channel_id=1, source_target_pairs={{0,3},{1,0},{2,1},{3,2},{4,7},{5,4},{6,5},{7,6},{8,11},{9,8},{10,9... | collective-permute-start | bytes 49160 | tf_op jit(solution)/shard_map/ppermute | solution.py:28
  8.0 4.2 %collective-permute-start.3 = (bf16[32,512]{1,0:T(8,128)(2,1)S(1)}, bf16[32,512]{1,0:T(8,128)(2,1)S(1)}, u32[]{:S(2)}, u32[]{:S(2)}) collective-permute-start(bf16[32,512]{1,0:T(8,128)(2,1)S(1)} %pad_maximum_fusion.2), channel_id=1, source_target_pairs={{0,1},{1,4},{2,3},{3,6},{4,5},{5,0},{6,7},{7,2},{8,9},{9,12},{10,1... | collective-permute-start | bytes 98312 | tf_op jit(solution)/shard_map/ppermute | solution.py:28
  15.7 3.5 %collective-permute-start.7 = (bf16[64,512]{1,0:T(8,128)(2,1)S(1)}, bf16[64,512]{1,0:T(8,128)(2,1)S(1)}, u32[]{:S(2)}, u32[]{:S(2)}) collective-permute-start(bf16[64,512]{1,0:T(8,128)(2,1)S(1)} %add_convert_fusion.7), channel_id=1, source_target_pairs={{0,3},{1,0},{2,1},{3,2},{4,7},{5,4},{6,5},{7,6},{8,11},{9,8},{10,9... | collective-permute-start | bytes 196616 | tf_op jit(solution)/shard_map/ppermute | solution.py:28
  17.4 4.5 %collective-permute-start.6 = (bf16[64,512]{1,0:T(8,128)(2,1)S(1)}, bf16[64,512]{1,0:T(8,128)(2,1)S(1)}, u32[]{:S(2)}, u32[]{:S(2)}) collective-permute-start(bf16[64,512]{1,0:T(8,128)(2,1)S(1)} %broadcast_select_fusion.3), channel_id=1, source_target_pairs={{0,1},{1,24},{2,3},{3,26},{4,5},{5,28},{6,7},{7,30},{8,9},{9,0},{1... | collective-permute-start | bytes 196616 | tf_op jit(solution)/shard_map/ppermute | solution.py:28
  19.3 3.7 %collective-permute-start.8 = (bf16[64,512]{1,0:T(8,128)(2,1)S(1)}, bf16[64,512]{1,0:T(8,128)(2,1)S(1)}, u32[]{:S(2)}, u32[]{:S(2)}) collective-permute-start(bf16[64,512]{1,0:T(8,128)(2,1)S(1)} %add_convert_fusion.6), channel_id=1, source_target_pairs={{0,1},{1,24},{2,3},{3,26},{4,5},{5,28},{6,7},{7,30},{8,9},{9,0},{1... | collective-permute-start | bytes 196616 | tf_op jit(solution)/shard_map/ppermute | solution.py:28
  20.0 5.5 %collective-permute-start.9 = (bf16[64,512]{1,0:T(8,128)(2,1)S(1)}, bf16[64,512]{1,0:T(8,128)(2,1)S(1)}, u32[]{:S(2)}, u32[]{:S(2)}) collective-permute-start(bf16[64,512]{1,0:T(8,128)(2,1)S(1)} %add_convert_fusion.6), channel_id=1, source_target_pairs={{0,1},{1,28},{2,3},{3,30},{4,5},{5,24},{6,7},{7,26},{8,9},{9,4},{1... | collective-permute-start | bytes 196616 | tf_op jit(solution)/shard_map/ppermute | solution.py:28
  25.5 1.4 %collective-permute-start.10 = (bf16[64,512]{1,0:T(8,128)(2,1)S(1)}, bf16[64,512]{1,0:T(8,128)(2,1)S(1)}, u32[]{:S(2)}, u32[]{:S(2)}) collective-permute-start(bf16[64,512]{1,0:T(8,128)(2,1)S(1)} %subtract_convert_fusion.6), channel_id=1, source_target_pairs={{0,1},{1,0},{2,3},{3,2},{4,5},{5,4},{6,7},{7,6},{8,9},{9,8},{10,11... | collective-permute-start | bytes 196616 | tf_op jit(solution)/shard_map/ppermute | solution.py:28
  29.0 4.0 %collective-permute-start.13 = (bf16[64,512]{1,0:T(8,128)(2,1)S(1)}, bf16[64,512]{1,0:T(8,128)(2,1)S(1)}, u32[]{:S(2)}, u32[]{:S(2)}) collective-permute-start(bf16[64,512]{1,0:T(8,128)(2,1)S(1)} %add_convert_fusion.5), channel_id=1, source_target_pairs={{0,3},{1,0},{2,1},{3,2},{4,7},{5,4},{6,5},{7,6},{8,11},{9,8},{10,9... | collective-permute-start | bytes 196616 | tf_op jit(solution)/shard_map/ppermute | solution.py:28
  31.1 4.6 %collective-permute-start.12 = (bf16[64,512]{1,0:T(8,128)(2,1)S(1)}, bf16[64,512]{1,0:T(8,128)(2,1)S(1)}, u32[]{:S(2)}, u32[]{:S(2)}) collective-permute-start(bf16[64,512]{1,0:T(8,128)(2,1)S(1)} %broadcast_select_fusion.2), channel_id=1, source_target_pairs={{0,1},{1,24},{2,3},{3,26},{4,5},{5,28},{6,7},{7,30},{8,9},{9,0},{1... | collective-permute-start | bytes 196616 | tf_op jit(solution)/shard_map/ppermute | solution.py:28
  33.0 3.8 %collective-permute-start.14 = (bf16[64,512]{1,0:T(8,128)(2,1)S(1)}, bf16[64,512]{1,0:T(8,128)(2,1)S(1)}, u32[]{:S(2)}, u32[]{:S(2)}) collective-permute-start(bf16[64,512]{1,0:T(8,128)(2,1)S(1)} %add_convert_fusion.4), channel_id=1, source_target_pairs={{0,1},{1,24},{2,3},{3,26},{4,5},{5,28},{6,7},{7,30},{8,9},{9,0},{1... | collective-permute-start | bytes 196616 | tf_op jit(solution)/shard_map/ppermute | solution.py:28
  33.8 5.5 %collective-permute-start.15 = (bf16[64,512]{1,0:T(8,128)(2,1)S(1)}, bf16[64,512]{1,0:T(8,128)(2,1)S(1)}, u32[]{:S(2)}, u32[]{:S(2)}) collective-permute-start(bf16[64,512]{1,0:T(8,128)(2,1)S(1)} %add_convert_fusion.4), channel_id=1, source_target_pairs={{0,1},{1,28},{2,3},{3,30},{4,5},{5,24},{6,7},{7,26},{8,9},{9,4},{1... | collective-permute-start | bytes 196616 | tf_op jit(solution)/shard_map/ppermute | solution.py:28
  39.4 1.7 %collective-permute-start.16 = (bf16[64,512]{1,0:T(8,128)(2,1)S(1)}, bf16[64,512]{1,0:T(8,128)(2,1)S(1)}, u32[]{:S(2)}, u32[]{:S(2)}) collective-permute-start(bf16[64,512]{1,0:T(8,128)(2,1)S(1)} %subtract_convert_fusion.5), channel_id=1, source_target_pairs={{0,1},{1,0},{2,3},{3,2},{4,5},{5,4},{6,7},{7,6},{8,9},{9,8},{10,11... | collective-permute-start | bytes 196616 | tf_op jit(solution)/shard_map/ppermute | solution.py:28
  41.9 1.3 %collective-permute-start.17 = (bf16[64,512]{1,0:T(8,128)(2,1)S(1)}, bf16[64,512]{1,0:T(8,128)(2,1)S(1)}, u32[]{:S(2)}, u32[]{:S(2)}) collective-permute-start(bf16[64,512]{1,0:T(8,128)(2,1)S(1)} %get-tuple-element.27), channel_id=1, source_target_pairs={{0,1},{1,0},{2,3},{3,2},{4,5},{5,4},{6,7},{7,6},{8,9},{9,8},{10,11... | collective-permute-start | bytes 196616 | tf_op jit(solution)/shard_map/ppermute | solution.py:28
  43.2 4.0 %collective-permute-start.19 = (bf16[64,512]{1,0:T(8,128)(2,1)S(1)}, bf16[64,512]{1,0:T(8,128)(2,1)S(1)}, u32[]{:S(2)}, u32[]{:S(2)}) collective-permute-start(bf16[64,512]{1,0:T(8,128)(2,1)S(1)} %add_convert_fusion.3), channel_id=1, source_target_pairs={{0,3},{1,0},{2,1},{3,2},{4,7},{5,4},{6,5},{7,6},{8,11},{9,8},{10,9... | collective-permute-start | bytes 196616 | tf_op jit(solution)/shard_map/ppermute | solution.py:28
  45.3 4.3 %collective-permute-start.18 = (bf16[64,512]{1,0:T(8,128)(2,1)S(1)}, bf16[64,512]{1,0:T(8,128)(2,1)S(1)}, u32[]{:S(2)}, u32[]{:S(2)}) collective-permute-start(bf16[64,512]{1,0:T(8,128)(2,1)S(1)} %broadcast_select_fusion.1), channel_id=1, source_target_pairs={{0,1},{1,24},{2,3},{3,26},{4,5},{5,28},{6,7},{7,30},{8,9},{9,0},{1... | collective-permute-start | bytes 196616 | tf_op jit(solution)/shard_map/ppermute | solution.py:28
  47.2 3.7 %collective-permute-start.20 = (bf16[64,512]{1,0:T(8,128)(2,1)S(1)}, bf16[64,512]{1,0:T(8,128)(2,1)S(1)}, u32[]{:S(2)}, u32[]{:S(2)}) collective-permute-start(bf16[64,512]{1,0:T(8,128)(2,1)S(1)} %add_convert_fusion.2), channel_id=1, source_target_pairs={{0,1},{1,24},{2,3},{3,26},{4,5},{5,28},{6,7},{7,30},{8,9},{9,0},{1... | collective-permute-start | bytes 196616 | tf_op jit(solution)/shard_map/ppermute | solution.py:28
  47.7 5.9 %collective-permute-start.21 = (bf16[64,512]{1,0:T(8,128)(2,1)S(1)}, bf16[64,512]{1,0:T(8,128)(2,1)S(1)}, u32[]{:S(2)}, u32[]{:S(2)}) collective-permute-start(bf16[64,512]{1,0:T(8,128)(2,1)S(1)} %add_convert_fusion.2), channel_id=1, source_target_pairs={{0,1},{1,28},{2,3},{3,30},{4,5},{5,24},{6,7},{7,26},{8,9},{9,4},{1... | collective-permute-start | bytes 196616 | tf_op jit(solution)/shard_map/ppermute | solution.py:28
  53.6 1.7 %collective-permute-start.22 = (bf16[64,512]{1,0:T(8,128)(2,1)S(1)}, bf16[64,512]{1,0:T(8,128)(2,1)S(1)}, u32[]{:S(2)}, u32[]{:S(2)}) collective-permute-start(bf16[64,512]{1,0:T(8,128)(2,1)S(1)} %subtract_convert_fusion.4), channel_id=1, source_target_pairs={{0,1},{1,0},{2,3},{3,2},{4,5},{5,4},{6,7},{7,6},{8,9},{9,8},{10,11... | collective-permute-start | bytes 196616 | tf_op jit(solution)/shard_map/ppermute | solution.py:28
  57.4 4.0 %collective-permute-start.25 = (bf16[64,512]{1,0:T(8,128)(2,1)S(1)}, bf16[64,512]{1,0:T(8,128)(2,1)S(1)}, u32[]{:S(2)}, u32[]{:S(2)}) collective-permute-start(bf16[64,512]{1,0:T(8,128)(2,1)S(1)} %add_convert_fusion.1), channel_id=1, source_target_pairs={{0,3},{1,0},{2,1},{3,2},{4,7},{5,4},{6,5},{7,6},{8,11},{9,8},{10,9... | collective-permute-start | bytes 196616 | tf_op jit(solution)/shard_map/ppermute | solution.py:28
  59.5 4.0 %collective-permute-start.24 = (bf16[16,512]{1,0:T(8,128)(2,1)S(1)}, bf16[16,512]{1,0:T(8,128)(2,1)S(1)}, u32[]{:S(2)}, u32[]{:S(2)}) collective-permute-start(bf16[16,512]{1,0:T(8,128)(2,1)S(1)} %constant_dynamic-slice_fusion.2), channel_id=1, source_target_pairs={{0,1},{1,24},{2,3},{3,26},{4,5},{5,28},{6,7},{7,30},{8,9},{9,0},{1... | collective-permute-start | bytes 49160 | tf_op jit(solution)/shard_map/ppermute | solution.py:28
  61.5 4.1 %collective-permute-start.26 = (bf16[16,512]{1,0:T(8,128)(2,1)S(1)}, bf16[16,512]{1,0:T(8,128)(2,1)S(1)}, u32[]{:S(2)}, u32[]{:S(2)}) collective-permute-start(bf16[16,512]{1,0:T(8,128)(2,1)S(1)} %get-tuple-element.11), channel_id=1, source_target_pairs={{0,1},{1,24},{2,3},{3,26},{4,5},{5,28},{6,7},{7,30},{8,9},{9,0},{1... | collective-permute-start | bytes 49160 | tf_op jit(solution)/shard_map/ppermute | solution.py:28
  61.7 5.5 %collective-permute-start.27 = (bf16[16,512]{1,0:T(8,128)(2,1)S(1)}, bf16[16,512]{1,0:T(8,128)(2,1)S(1)}, u32[]{:S(2)}, u32[]{:S(2)}) collective-permute-start(bf16[16,512]{1,0:T(8,128)(2,1)S(1)} %get-tuple-element.12), channel_id=1, source_target_pairs={{0,1},{1,28},{2,3},{3,30},{4,5},{5,24},{6,7},{7,26},{8,9},{9,4},{1... | collective-permute-start | bytes 49160 | tf_op jit(solution)/shard_map/ppermute | solution.py:28
  67.3 2.3 %collective-permute-start.28 = (f32[2,8,512]{2,1,0:T(8,128)S(1)}, f32[2,8,512]{2,1,0:T(8,128)S(1)}, u32[]{:S(2)}, u32[]{:S(2)}) collective-permute-start(f32[2,8,512]{2,1,0:T(8,128)S(1)} %slice_bitcast_fusion.1), channel_id=1, source_target_pairs={{0,1},{1,0},{2,3},{3,2},{4,5},{5,4},{6,7},{7,6},{8,9},{9,8},{10,11... | collective-permute-start | bytes 98312 | tf_op jit(solution)/shard_map/ppermute | solution.py:28
  (7 other events, 21.0 us)
where the time goes:
time: 70.8 us; the launch traced here: 70.3 us
  waiting for transfers between devices  33.3 us (47%)
  starting transfers between devices  25.9 us (37%)
  matrix products  5.8 us (8%)
  other arithmetic  2.59 us (4%)
  local copies, waits for them, and re-layouts  1.72 us (2%)
  between operations  0.9 us (1%)
    ppermute x29, waiting for transfers between devices, route(): return lax.ppermute(block, AXES, pairs)  33.3 us
    ppermute x29, starting transfers between devices, route(): return lax.ppermute(block, AXES, pairs)  25.9 us
    dot_general x4, matrix products, local(): change = jnp.dot(resid, whole, preferred_element_type=jnp.float32)  2.81 us
    dot_general x4, matrix products, local(): lax.dot_general(users, whole, (((1,), (1,)), ((), ())), preferred_element...  1.77 us
  transfers between devices with their start and end apart: 29, of which 23 were waited for; matrix products, arithmetic and copies ran while one was open for 7% of the time, Pallas kernels for 0%

commit v1 on v0

v1 whole, which is shorter than its diff:
```python
import jax
import jax.numpy as jnp
from jax import lax
from jax.sharding import PartitionSpec as P


AXES = ("stratum", "user")
user_rate = 1.0
item_rate = 0.04
inertia = 0.6


def wide(block):
    return block.astype(jnp.float32)


def narrow(block):
    return block.astype(jnp.bfloat16)


def route(block, target):
    strata, users = lax.axis_size("stratum"), lax.axis_size("user")
    pairs = []
    for s in range(strata):
        for u in range(users):
            there, who = target(s, u)
            pairs.append((s * users + u, there % strata * users + who))
    return lax.ppermute(block, AXES, pairs)


def swap(block, bits):
    return route(block, lambda s, u: (s, u ^ bits))


def back(block, even, odd):
    return route(block, lambda s, u: (s - 1, u ^ (odd if u % 2 else even)))


def local(users, items, momentum, ratings):
    steps, rank = ratings.shape[1], users.shape[1]
    factor = rank ** (-0.5)
    own = items.shape[0]
    n = lax.axis_size("user")
    top = n // 2
    me = lax.axis_index("user")
    core, place = me % 2, me // 2

    def in_order(mine, other, late):
        return jnp.concatenate(
            [jnp.where(late == 0, mine, other), jnp.where(late == 0, other, mine)], axis=0
        )

    def rows_of(block, start, count):
        return lax.dynamic_slice_in_dim(block, start, count, 0)

    mine = lax.optimization_barrier(narrow(items))
    block, bit = mine, 1
    while bit < top // 2:
        block = in_order(block, swap(block, bit), me // bit % 2)
        bit *= 2
    near, far, cross = swap(block, bit), swap(block, top), swap(block, bit + top)
    side, end = me // bit % 2, me // top
    whole = in_order(in_order(block, near, side), in_order(far, cross, side), end)
    tiles = [ratings[:, step, :] for step in range(steps)]
    tiles[0] = lax.optimization_barrier(tiles[0])

    owner = lax.broadcasted_iota(jnp.int32, (n, own, rank), 0)
    share = jnp.where(owner == me, inertia * momentum[None], 0.0).reshape(-1, rank)
    for step in range(steps):
        last = step == steps - 1
        score = lax.dot_general(
            users, whole, (((1,), (1,)), ((), ())), preferred_element_type=jnp.float32
        )
        resid = narrow(jnp.where(tiles[step] != 0, score * factor - wide(tiles[step]), 0.0))
        grads = lax.dot_general(
            resid, users, (((0,), (0,)), ((), ())), preferred_element_type=jnp.float32
        )
        grads = factor * grads + share
        total, bit = narrow(grads), 1
        while bit < top // 2:
            grads = grads + wide(swap(total, bit))
            total = narrow(grads)
            bit *= 2
        first = (bit, top)
        second = (0, bit + top)

        def part(flip):
            return rows_of(total, (place ^ flip // 2) * 2 * own, 2 * own)

        def picked(flips):
            if not last:
                return total
            return jnp.where(core == 0, part(flips[0]), part(flips[1]))

        one = back(picked(first), *first)
        two = back(picked(second), *second)
        if last:
            value = rows_of(whole, me * own, own)
        else:
            value = rows_of(whole, core * (n // 2 * own), n // 2 * own)
        value = back(value, 0, 0)
        change = jnp.dot(resid, whole, preferred_element_type=jnp.float32)
        users = narrow(wide(users) - user_rate * factor * change)
        moment = wide(one) + wide(two)
        if last:
            give = rows_of(moment, (1 - core) * own, own)
            moment = rows_of(moment, core * own, own) + wide(swap(narrow(give), 1))
        else:
            moment = narrow(moment)
            moment = wide(moment) + wide(swap(moment, 1))
            value = in_order(value, swap(value, 1), core)
        fresh = wide(value) - item_rate * moment
        whole = narrow(fresh)
        share = (inertia / n) * moment
    return users, fresh, moment


def solution(mesh):
    rows = P(AXES, None)
    return jax.shard_map(
        local,
        mesh=mesh,
        in_specs=(rows, rows, rows, P(AXES, None, None)),
        out_specs=(rows, rows, rows),
        check_vma=False,
    )
```

time: 70.8 us -> 63 us (0.89)
  waiting for transfers between devices: 33.3 us -> 20.7 us
  starting transfers between devices: 25.9 us -> 30.5 us
  matrix products: 5.8 us -> 7.01 us
    ppermute x29 -> x27, waiting for transfers between devices: 33.3 us -> 20.7 us  [route(): return lax.ppermute(block, AXES, pairs)]
    ppermute x29 -> x27, starting transfers between devices: 25.9 us -> 30.5 us  [route(): return lax.ppermute(block, AXES, pairs)]
    dot_general x4, matrix products: 1.77 us -> 3 us  [local(): lax.dot_general(users, whole, (((1,), (1,)), ((), ())), preferred_element...]
  transfers between devices with their start and end apart: 29 -> 27, of which waited for: 23 -> 14; matrix products, arithmetic and copies ran while one was open for 7% -> 8% of each run, Pallas kernels for 0% -> 0%
where the time goes in v1:
time: 63 us; the launch traced here: 62.6 us
  starting transfers between devices  30.5 us (48%)
  waiting for transfers between devices  20.7 us (33%)
  matrix products  7.01 us (11%)
  other arithmetic  2.43 us (4%)
  local copies, waits for them, and re-layouts  1.1 us (2%)
  between operations  0.85 us (1%)
    ppermute x27, starting transfers between devices, route(): return lax.ppermute(block, AXES, pairs)  30.5 us
    ppermute x27, waiting for transfers between devices, route(): return lax.ppermute(block, AXES, pairs)  20.7 us
    dot_general x4, matrix products, local(): lax.dot_general(users, whole, (((1,), (1,)), ((), ())), preferred_element...  3 us
    dot_general x4, matrix products, local(): change = jnp.dot(resid, whole, preferred_element_type=jnp.float32)  2.8 us
  transfers between devices with their start and end apart: 27, of which 14 were waited for; matrix products, arithmetic and copies ran while one was open for 8% of the time, Pallas kernels for 0%

profile of v1, /device:TPU:0, one launch (start us, length us, event | category | flops | bytes accessed | tf_op | source)
XLA Modules:
  0.0 62.6 jit_solution(2228457828800969368)
XLA Ops:
  3.5 2.7 %collective-permute-start.1 = (bf16[16,512]{1,0:T(8,128)(2,1)S(1)}, bf16[16,512]{1,0:T(8,128)(2,1)S(1)}, u32[]{:S(2)}, u32[]{:S(2)}) collective-permute-start(bf16[16,512]{1,0:T(8,128)(2,1)S(1)} %pad_maximum_fusion.5), channel_id=1, source_target_pairs={{0,2},{1,3},{2,0},{3,1},{4,6},{5,7},{6,4},{7,5},{8,10},{9,11},{10,... | collective-permute-start | bytes 49160 | tf_op jit(solution)/shard_map/ppermute | solution.py:28
  6.4 2.5 %collective-permute-start.3 = (bf16[16,512]{1,0:T(8,128)(2,1)S(1)}, bf16[16,512]{1,0:T(8,128)(2,1)S(1)}, u32[]{:S(2)}, u32[]{:S(2)}) collective-permute-start(bf16[16,512]{1,0:T(8,128)(2,1)S(1)} %pad_maximum_fusion.5), channel_id=1, source_target_pairs={{0,6},{1,7},{2,4},{3,5},{4,2},{5,3},{6,0},{7,1},{8,14},{9,15},{10,... | collective-permute-start | bytes 49160 | tf_op jit(solution)/shard_map/ppermute | solution.py:28
  9.1 2.9 %collective-permute-done.3 = bf16[16,512]{1,0:T(8,128)(2,1)S(1)} collective-permute-done((bf16[16,512]{1,0:T(8,128)(2,1)S(1)}, bf16[16,512]{1,0:T(8,128)(2,1)S(1)}, u32[]{:S(2)}, u32[]{:S(2)}) %collective-permute-start.3) | collective-permute-done | bytes 16416 | tf_op jit(solution)/shard_map/ppermute | solution.py:28
  12.0 1.6 %collective-permute-done.2 = bf16[16,512]{1,0:T(8,128)(2,1)S(1)} collective-permute-done((bf16[16,512]{1,0:T(8,128)(2,1)S(1)}, bf16[16,512]{1,0:T(8,128)(2,1)S(1)}, u32[]{:S(2)}, u32[]{:S(2)}) %collective-permute-start.2) | collective-permute-done | bytes 16416 | tf_op jit(solution)/shard_map/ppermute | solution.py:28
  13.6 1.7 %fusion.9 = bf16[1024,64]{0,1:T(8,128)(2,1)S(1)} fusion(bf16[1024,512]{1,0:T(8,128)(2,1)} %param.4, bf16[1024,64]{0,1:T(8,128)(2,1)S(1)} %slice_bitcast_fusion, bf16[32,512]{1,0:T(8,128)(2,1)S(1)} %get-tuple-element.14, bf16[32,512]{1,0:T(8,128)(2,1)S(1)} %get-tuple-element.13), kind=kOutput, calls=%fused_computation.17 | convolution fusion | flops 67633152 | bytes 1376256 | tf_op jit(solution)/shard_map/dot_general | solution.py:71
  15.7 2.5 %collective-permute-start.4 = (bf16[32,512]{1,0:T(8,128)(2,1)S(1)}, bf16[32,512]{1,0:T(8,128)(2,1)S(1)}, u32[]{:S(2)}, u32[]{:S(2)}) collective-permute-start(bf16[32,512]{1,0:T(8,128)(2,1)S(1)} %fusion.14), channel_id=1, source_target_pairs={{0,24},{1,25},{2,26},{3,27},{4,28},{5,29},{6,30},{7,31},{8,0},{9,1... | collective-permute-start | bytes 98312 | tf_op jit(solution)/shard_map/ppermute | solution.py:28
  18.2 1.2 %collective-permute-start.8 = (bf16[64,512]{1,0:T(8,128)(2,1)S(1)}, bf16[64,512]{1,0:T(8,128)(2,1)S(1)}, u32[]{:S(2)}, u32[]{:S(2)}) collective-permute-start(bf16[64,512]{1,0:T(8,128)(2,1)S(1)} %add_convert_fusion.6), channel_id=1, source_target_pairs={{0,24},{1,31},{2,26},{3,29},{4,28},{5,27},{6,30},{7,25},{8,0},{9,7... | collective-permute-start | bytes 196616 | tf_op jit(solution)/shard_map/ppermute | solution.py:28
  19.4 1.0 %collective-permute-start.7 = (bf16[64,512]{1,0:T(8,128)(2,1)S(1)}, bf16[64,512]{1,0:T(8,128)(2,1)S(1)}, u32[]{:S(2)}, u32[]{:S(2)}) collective-permute-start(bf16[64,512]{1,0:T(8,128)(2,1)S(1)} %add_convert_fusion.6), channel_id=1, source_target_pairs={{0,26},{1,29},{2,24},{3,31},{4,30},{5,25},{6,28},{7,27},{8,2},{9,5... | collective-permute-start | bytes 196616 | tf_op jit(solution)/shard_map/ppermute | solution.py:28
  21.5 1.1 %collective-permute-done.8 = bf16[64,512]{1,0:T(8,128)(2,1)S(1)} collective-permute-done((bf16[64,512]{1,0:T(8,128)(2,1)S(1)}, bf16[64,512]{1,0:T(8,128)(2,1)S(1)}, u32[]{:S(2)}, u32[]{:S(2)}) %collective-permute-start.8) | collective-permute-done | bytes 65568 | tf_op jit(solution)/shard_map/ppermute | solution.py:28
  22.5 2.9 %collective-permute-done.7 = bf16[64,512]{1,0:T(8,128)(2,1)S(1)} collective-permute-done((bf16[64,512]{1,0:T(8,128)(2,1)S(1)}, bf16[64,512]{1,0:T(8,128)(2,1)S(1)}, u32[]{:S(2)}, u32[]{:S(2)}) %collective-permute-start.7) | collective-permute-done | bytes 65568 | tf_op jit(solution)/shard_map/ppermute | solution.py:28
  28.2 1.8 %collective-permute-start.10 = (bf16[32,512]{1,0:T(8,128)(2,1)S(1)}, bf16[32,512]{1,0:T(8,128)(2,1)S(1)}, u32[]{:S(2)}, u32[]{:S(2)}) collective-permute-start(bf16[32,512]{1,0:T(8,128)(2,1)S(1)} %constant_dynamic-slice_fusion.2), channel_id=1, source_target_pairs={{0,24},{1,25},{2,26},{3,27},{4,28},{5,29},{6,30},{7,31},{8,0},{9,1... | collective-permute-start | bytes 98312 | tf_op jit(solution)/shard_map/ppermute | solution.py:28
  30.1 0.9 %collective-permute-start.14 = (bf16[64,512]{1,0:T(8,128)(2,1)S(1)}, bf16[64,512]{1,0:T(8,128)(2,1)S(1)}, u32[]{:S(2)}, u32[]{:S(2)}) collective-permute-start(bf16[64,512]{1,0:T(8,128)(2,1)S(1)} %add_convert_fusion.4), channel_id=1, source_target_pairs={{0,24},{1,31},{2,26},{3,29},{4,28},{5,27},{6,30},{7,25},{8,0},{9,7... | collective-permute-start | bytes 196616 | tf_op jit(solution)/shard_map/ppermute | solution.py:28
  31.0 1.6 %collective-permute-start.13 = (bf16[64,512]{1,0:T(8,128)(2,1)S(1)}, bf16[64,512]{1,0:T(8,128)(2,1)S(1)}, u32[]{:S(2)}, u32[]{:S(2)}) collective-permute-start(bf16[64,512]{1,0:T(8,128)(2,1)S(1)} %add_convert_fusion.4), channel_id=1, source_target_pairs={{0,26},{1,29},{2,24},{3,31},{4,30},{5,25},{6,28},{7,27},{8,2},{9,5... | collective-permute-start | bytes 196616 | tf_op jit(solution)/shard_map/ppermute | solution.py:28
  34.4 2.4 %collective-permute-done.13 = bf16[64,512]{1,0:T(8,128)(2,1)S(1)} collective-permute-done((bf16[64,512]{1,0:T(8,128)(2,1)S(1)}, bf16[64,512]{1,0:T(8,128)(2,1)S(1)}, u32[]{:S(2)}, u32[]{:S(2)}) %collective-permute-start.13) | collective-permute-done | bytes 65568 | tf_op jit(solution)/shard_map/ppermute | solution.py:28
  36.9 1.1 %collective-permute-start.15 = (bf16[64,512]{1,0:T(8,128)(2,1)S(1)}, bf16[64,512]{1,0:T(8,128)(2,1)S(1)}, u32[]{:S(2)}, u32[]{:S(2)}) collective-permute-start(bf16[64,512]{1,0:T(8,128)(2,1)S(1)} %add_convert_fusion.3), channel_id=1, source_target_pairs={{0,1},{1,0},{2,3},{3,2},{4,5},{5,4},{6,7},{7,6},{8,9},{9,8},{10,11... | collective-permute-start | bytes 196616 | tf_op jit(solution)/shard_map/ppermute | solution.py:28
  40.1 2.1 %collective-permute-start.16 = (bf16[32,512]{1,0:T(8,128)(2,1)S(1)}, bf16[32,512]{1,0:T(8,128)(2,1)S(1)}, u32[]{:S(2)}, u32[]{:S(2)}) collective-permute-start(bf16[32,512]{1,0:T(8,128)(2,1)S(1)} %constant_dynamic-slice_fusion.1), channel_id=1, source_target_pairs={{0,24},{1,25},{2,26},{3,27},{4,28},{5,29},{6,30},{7,31},{8,0},{9,1... | collective-permute-start | bytes 98312 | tf_op jit(solution)/shard_map/ppermute | solution.py:28
  43.1 1.1 %collective-permute-start.19 = (bf16[64,512]{1,0:T(8,128)(2,1)S(1)}, bf16[64,512]{1,0:T(8,128)(2,1)S(1)}, u32[]{:S(2)}, u32[]{:S(2)}) collective-permute-start(bf16[64,512]{1,0:T(8,128)(2,1)S(1)} %add_convert_fusion.2), channel_id=1, source_target_pairs={{0,26},{1,29},{2,24},{3,31},{4,30},{5,25},{6,28},{7,27},{8,2},{9,5... | collective-permute-start | bytes 196616 | tf_op jit(solution)/shard_map/ppermute | solution.py:28
  44.9 1.6 %collective-permute-done.20 = bf16[64,512]{1,0:T(8,128)(2,1)S(1)} collective-permute-done((bf16[64,512]{1,0:T(8,128)(2,1)S(1)}, bf16[64,512]{1,0:T(8,128)(2,1)S(1)}, u32[]{:S(2)}, u32[]{:S(2)}) %collective-permute-start.20) | collective-permute-done | bytes 65568 | tf_op jit(solution)/shard_map/ppermute | solution.py:28
  46.5 2.6 %collective-permute-done.19 = bf16[64,512]{1,0:T(8,128)(2,1)S(1)} collective-permute-done((bf16[64,512]{1,0:T(8,128)(2,1)S(1)}, bf16[64,512]{1,0:T(8,128)(2,1)S(1)}, u32[]{:S(2)}, u32[]{:S(2)}) %collective-permute-start.19) | collective-permute-done | bytes 65568 | tf_op jit(solution)/shard_map/ppermute | solution.py:28
  52.8 1.9 %collective-permute-start.24 = (bf16[16,512]{1,0:T(8,128)(2,1)S(1)}, bf16[16,512]{1,0:T(8,128)(2,1)S(1)}, u32[]{:S(2)}, u32[]{:S(2)}) collective-permute-start(bf16[16,512]{1,0:T(8,128)(2,1)S(1)} %get-tuple-element.5), channel_id=1, source_target_pairs={{0,26},{1,29},{2,24},{3,31},{4,30},{5,25},{6,28},{7,27},{8,2},{9,5... | collective-permute-start | bytes 49160 | tf_op jit(solution)/shard_map/ppermute | solution.py:28
  55.2 2.0 %collective-permute-start.22 = (bf16[8,512]{1,0:T(8,128)(2,1)S(1)}, bf16[8,512]{1,0:T(8,128)(2,1)S(1)}, u32[]{:S(2)}, u32[]{:S(2)}) collective-permute-start(bf16[8,512]{1,0:T(8,128)(2,1)S(1)} %constant_dynamic-slice_fusion), channel_id=1, source_target_pairs={{0,24},{1,25},{2,26},{3,27},{4,28},{5,29},{6,30},{7,31},{8,0},{9,1... | collective-permute-start | bytes 24584 | tf_op jit(solution)/shard_map/ppermute | solution.py:28
  57.5 1.0 %collective-permute-done.25 = bf16[16,512]{1,0:T(8,128)(2,1)S(1)} collective-permute-done((bf16[16,512]{1,0:T(8,128)(2,1)S(1)}, bf16[16,512]{1,0:T(8,128)(2,1)S(1)}, u32[]{:S(2)}, u32[]{:S(2)}) %collective-permute-start.25) | collective-permute-done | bytes 16416 | tf_op jit(solution)/shard_map/ppermute | solution.py:28
  58.5 2.1 %collective-permute-start.26 = (bf16[8,512]{1,0:T(8,128)(2,1)S(1)}, bf16[8,512]{1,0:T(8,128)(2,1)S(1)}, u32[]{:S(2)}, u32[]{:S(2)}) collective-permute-start(bf16[8,512]{1,0:T(8,128)(2,1)S(1)} %dynamic-slice_convert_fusion), channel_id=1, source_target_pairs={{0,1},{1,0},{2,3},{3,2},{4,5},{5,4},{6,7},{7,6},{8,9},{9,8},{10,11... | collective-permute-start | bytes 24584 | tf_op jit(solution)/shard_map/ppermute | solution.py:28
  60.6 1.4 %subtract_convert_fusion = bf16[1024,512]{1,0:T(8,128)(2,1)} fusion(bf16[1024,512]{1,0:T(8,128)(2,1)S(1)} %subtract_convert_fusion.1, bf16[1024,64]{0,1:T(8,128)(2,1)S(1)} %fusion.12, bf16[64,512]{1,0:T(8,128)(2,1)S(1)} %subtract_convert_fusion.4), kind=kOutput, calls=%fused_computation | convolution fusion | flops 69206016 | bytes 2293760 | tf_op jit(solution)/shard_map/dot_general | solution.py:102
  (78 shorter events, 18.3 us)
Async XLA Ops:
  1.4 2.1 %collective-permute-start = (bf16[8,512]{1,0:T(8,128)(2,1)S(1)}, bf16[8,512]{1,0:T(8,128)(2,1)S(1)}, u32[]{:S(2)}, u32[]{:S(2)}) collective-permute-start(bf16[8,512]{1,0:T(8,128)(2,1)S(1)} %convert_element_type.175), channel_id=1, source_target_pairs={{0,1},{1,0},{2,3},{3,2},{4,5},{5,4},{6,7},{7,6},{8,9},{9,8},{10,11... | collective-permute-start | bytes 24584 | tf_op jit(solution)/shard_map/ppermute | solution.py:28
  3.5 5.6 %collective-permute-start.1 = (bf16[16,512]{1,0:T(8,128)(2,1)S(1)}, bf16[16,512]{1,0:T(8,128)(2,1)S(1)}, u32[]{:S(2)}, u32[]{:S(2)}) collective-permute-start(bf16[16,512]{1,0:T(8,128)(2,1)S(1)} %pad_maximum_fusion.5), channel_id=1, source_target_pairs={{0,2},{1,3},{2,0},{3,1},{4,6},{5,7},{6,4},{7,5},{8,10},{9,11},{10,... | collective-permute-start | bytes 49160 | tf_op jit(solution)/shard_map/ppermute | solution.py:28
  6.4 5.6 %collective-permute-start.3 = (bf16[16,512]{1,0:T(8,128)(2,1)S(1)}, bf16[16,512]{1,0:T(8,128)(2,1)S(1)}, u32[]{:S(2)}, u32[]{:S(2)}) collective-permute-start(bf16[16,512]{1,0:T(8,128)(2,1)S(1)} %pad_maximum_fusion.5), channel_id=1, source_target_pairs={{0,6},{1,7},{2,4},{3,5},{4,2},{5,3},{6,0},{7,1},{8,14},{9,15},{10,... | collective-permute-start | bytes 49160 | tf_op jit(solution)/shard_map/ppermute | solution.py:28
  8.9 4.6 %collective-permute-start.2 = (bf16[16,512]{1,0:T(8,128)(2,1)S(1)}, bf16[16,512]{1,0:T(8,128)(2,1)S(1)}, u32[]{:S(2)}, u32[]{:S(2)}) collective-permute-start(bf16[16,512]{1,0:T(8,128)(2,1)S(1)} %pad_maximum_fusion.5), channel_id=1, source_target_pairs={{0,4},{1,5},{2,6},{3,7},{4,0},{5,1},{6,2},{7,3},{8,12},{9,13},{10,... | collective-permute-start | bytes 49160 | tf_op jit(solution)/shard_map/ppermute | solution.py:28
  15.6 2.6 %collective-permute-start.6 = (bf16[64,512]{1,0:T(8,128)(2,1)S(1)}, bf16[64,512]{1,0:T(8,128)(2,1)S(1)}, u32[]{:S(2)}, u32[]{:S(2)}) collective-permute-start(bf16[64,512]{1,0:T(8,128)(2,1)S(1)} %get-tuple-element.21), channel_id=1, source_target_pairs={{0,1},{1,0},{2,3},{3,2},{4,5},{5,4},{6,7},{7,6},{8,9},{9,8},{10,11... | collective-permute-start | bytes 196616 | tf_op jit(solution)/shard_map/ppermute | solution.py:28
  15.7 5.2 %collective-permute-start.4 = (bf16[32,512]{1,0:T(8,128)(2,1)S(1)}, bf16[32,512]{1,0:T(8,128)(2,1)S(1)}, u32[]{:S(2)}, u32[]{:S(2)}) collective-permute-start(bf16[32,512]{1,0:T(8,128)(2,1)S(1)} %fusion.14), channel_id=1, source_target_pairs={{0,24},{1,25},{2,26},{3,27},{4,28},{5,29},{6,30},{7,31},{8,0},{9,1... | collective-permute-start | bytes 98312 | tf_op jit(solution)/shard_map/ppermute | solution.py:28
  18.2 4.3 %collective-permute-start.8 = (bf16[64,512]{1,0:T(8,128)(2,1)S(1)}, bf16[64,512]{1,0:T(8,128)(2,1)S(1)}, u32[]{:S(2)}, u32[]{:S(2)}) collective-permute-start(bf16[64,512]{1,0:T(8,128)(2,1)S(1)} %add_convert_fusion.6), channel_id=1, source_target_pairs={{0,24},{1,31},{2,26},{3,29},{4,28},{5,27},{6,30},{7,25},{8,0},{9,7... | collective-permute-start | bytes 196616 | tf_op jit(solution)/shard_map/ppermute | solution.py:28
  19.4 6.0 %collective-permute-start.7 = (bf16[64,512]{1,0:T(8,128)(2,1)S(1)}, bf16[64,512]{1,0:T(8,128)(2,1)S(1)}, u32[]{:S(2)}, u32[]{:S(2)}) collective-permute-start(bf16[64,512]{1,0:T(8,128)(2,1)S(1)} %add_convert_fusion.6), channel_id=1, source_target_pairs={{0,26},{1,29},{2,24},{3,31},{4,30},{5,25},{6,28},{7,27},{8,2},{9,5... | collective-permute-start | bytes 196616 | tf_op jit(solution)/shard_map/ppermute | solution.py:28
  20.9 5.2 %collective-permute-start.5 = (bf16[32,512]{1,0:T(8,128)(2,1)S(1)}, bf16[32,512]{1,0:T(8,128)(2,1)S(1)}, u32[]{:S(2)}, u32[]{:S(2)}) collective-permute-start(bf16[32,512]{1,0:T(8,128)(2,1)S(1)} %collective-permute-done.4), channel_id=1, source_target_pairs={{0,1},{1,0},{2,3},{3,2},{4,5},{5,4},{6,7},{7,6},{8,9},{9,8},{10,11... | collective-permute-start | bytes 98312 | tf_op jit(solution)/shard_map/ppermute | solution.py:28
  27.8 2.2 %collective-permute-start.12 = (bf16[64,512]{1,0:T(8,128)(2,1)S(1)}, bf16[64,512]{1,0:T(8,128)(2,1)S(1)}, u32[]{:S(2)}, u32[]{:S(2)}) collective-permute-start(bf16[64,512]{1,0:T(8,128)(2,1)S(1)} %get-tuple-element.23), channel_id=1, source_target_pairs={{0,1},{1,0},{2,3},{3,2},{4,5},{5,4},{6,7},{7,6},{8,9},{9,8},{10,11... | collective-permute-start | bytes 196616 | tf_op jit(solution)/shard_map/ppermute | solution.py:28
  28.2 4.8 %collective-permute-start.10 = (bf16[32,512]{1,0:T(8,128)(2,1)S(1)}, bf16[32,512]{1,0:T(8,128)(2,1)S(1)}, u32[]{:S(2)}, u32[]{:S(2)}) collective-permute-start(bf16[32,512]{1,0:T(8,128)(2,1)S(1)} %constant_dynamic-slice_fusion.2), channel_id=1, source_target_pairs={{0,24},{1,25},{2,26},{3,27},{4,28},{5,29},{6,30},{7,31},{8,0},{9,1... | collective-permute-start | bytes 98312 | tf_op jit(solution)/shard_map/ppermute | solution.py:28
  30.1 4.3 %collective-permute-start.14 = (bf16[64,512]{1,0:T(8,128)(2,1)S(1)}, bf16[64,512]{1,0:T(8,128)(2,1)S(1)}, u32[]{:S(2)}, u32[]{:S(2)}) collective-permute-start(bf16[64,512]{1,0:T(8,128)(2,1)S(1)} %add_convert_fusion.4), channel_id=1, source_target_pairs={{0,24},{1,31},{2,26},{3,29},{4,28},{5,27},{6,30},{7,25},{8,0},{9,7... | collective-permute-start | bytes 196616 | tf_op jit(solution)/shard_map/ppermute | solution.py:28
  31.0 5.8 %collective-permute-start.13 = (bf16[64,512]{1,0:T(8,128)(2,1)S(1)}, bf16[64,512]{1,0:T(8,128)(2,1)S(1)}, u32[]{:S(2)}, u32[]{:S(2)}) collective-permute-start(bf16[64,512]{1,0:T(8,128)(2,1)S(1)} %add_convert_fusion.4), channel_id=1, source_target_pairs={{0,26},{1,29},{2,24},{3,31},{4,30},{5,25},{6,28},{7,27},{8,2},{9,5... | collective-permute-start | bytes 196616 | tf_op jit(solution)/shard_map/ppermute | solution.py:28
  33.1 4.9 %collective-permute-start.11 = (bf16[32,512]{1,0:T(8,128)(2,1)S(1)}, bf16[32,512]{1,0:T(8,128)(2,1)S(1)}, u32[]{:S(2)}, u32[]{:S(2)}) collective-permute-start(bf16[32,512]{1,0:T(8,128)(2,1)S(1)} %collective-permute-done.10), channel_id=1, source_target_pairs={{0,1},{1,0},{2,3},{3,2},{4,5},{5,4},{6,7},{7,6},{8,9},{9,8},{10,11... | collective-permute-start | bytes 98312 | tf_op jit(solution)/shard_map/ppermute | solution.py:28
  36.9 2.0 %collective-permute-start.15 = (bf16[64,512]{1,0:T(8,128)(2,1)S(1)}, bf16[64,512]{1,0:T(8,128)(2,1)S(1)}, u32[]{:S(2)}, u32[]{:S(2)}) collective-permute-start(bf16[64,512]{1,0:T(8,128)(2,1)S(1)} %add_convert_fusion.3), channel_id=1, source_target_pairs={{0,1},{1,0},{2,3},{3,2},{4,5},{5,4},{6,7},{7,6},{8,9},{9,8},{10,11... | collective-permute-start | bytes 196616 | tf_op jit(solution)/shard_map/ppermute | solution.py:28
  39.6 2.5 %collective-permute-start.18 = (bf16[64,512]{1,0:T(8,128)(2,1)S(1)}, bf16[64,512]{1,0:T(8,128)(2,1)S(1)}, u32[]{:S(2)}, u32[]{:S(2)}) collective-permute-start(bf16[64,512]{1,0:T(8,128)(2,1)S(1)} %get-tuple-element.25), channel_id=1, source_target_pairs={{0,1},{1,0},{2,3},{3,2},{4,5},{5,4},{6,7},{7,6},{8,9},{9,8},{10,11... | collective-permute-start | bytes 196616 | tf_op jit(solution)/shard_map/ppermute | solution.py:28
  40.1 4.6 %collective-permute-start.16 = (bf16[32,512]{1,0:T(8,128)(2,1)S(1)}, bf16[32,512]{1,0:T(8,128)(2,1)S(1)}, u32[]{:S(2)}, u32[]{:S(2)}) collective-permute-start(bf16[32,512]{1,0:T(8,128)(2,1)S(1)} %constant_dynamic-slice_fusion.1), channel_id=1, source_target_pairs={{0,24},{1,25},{2,26},{3,27},{4,28},{5,29},{6,30},{7,31},{8,0},{9,1... | collective-permute-start | bytes 98312 | tf_op jit(solution)/shard_map/ppermute | solution.py:28
  42.2 4.3 %collective-permute-start.20 = (bf16[64,512]{1,0:T(8,128)(2,1)S(1)}, bf16[64,512]{1,0:T(8,128)(2,1)S(1)}, u32[]{:S(2)}, u32[]{:S(2)}) collective-permute-start(bf16[64,512]{1,0:T(8,128)(2,1)S(1)} %add_convert_fusion.2), channel_id=1, source_target_pairs={{0,24},{1,31},{2,26},{3,29},{4,28},{5,27},{6,30},{7,25},{8,0},{9,7... | collective-permute-start | bytes 196616 | tf_op jit(solution)/shard_map/ppermute | solution.py:28
  43.1 6.0 %collective-permute-start.19 = (bf16[64,512]{1,0:T(8,128)(2,1)S(1)}, bf16[64,512]{1,0:T(8,128)(2,1)S(1)}, u32[]{:S(2)}, u32[]{:S(2)}) collective-permute-start(bf16[64,512]{1,0:T(8,128)(2,1)S(1)} %add_convert_fusion.2), channel_id=1, source_target_pairs={{0,26},{1,29},{2,24},{3,31},{4,30},{5,25},{6,28},{7,27},{8,2},{9,5... | collective-permute-start | bytes 196616 | tf_op jit(solution)/shard_map/ppermute | solution.py:28
  44.6 5.1 %collective-permute-start.17 = (bf16[32,512]{1,0:T(8,128)(2,1)S(1)}, bf16[32,512]{1,0:T(8,128)(2,1)S(1)}, u32[]{:S(2)}, u32[]{:S(2)}) collective-permute-start(bf16[32,512]{1,0:T(8,128)(2,1)S(1)} %collective-permute-done.16), channel_id=1, source_target_pairs={{0,1},{1,0},{2,3},{3,2},{4,5},{5,4},{6,7},{7,6},{8,9},{9,8},{10,11... | collective-permute-start | bytes 98312 | tf_op jit(solution)/shard_map/ppermute | solution.py:28
  52.8 4.7 %collective-permute-start.24 = (bf16[16,512]{1,0:T(8,128)(2,1)S(1)}, bf16[16,512]{1,0:T(8,128)(2,1)S(1)}, u32[]{:S(2)}, u32[]{:S(2)}) collective-permute-start(bf16[16,512]{1,0:T(8,128)(2,1)S(1)} %get-tuple-element.5), channel_id=1, source_target_pairs={{0,26},{1,29},{2,24},{3,31},{4,30},{5,25},{6,28},{7,27},{8,2},{9,5... | collective-permute-start | bytes 49160 | tf_op jit(solution)/shard_map/ppermute | solution.py:28
  54.7 3.7 %collective-permute-start.25 = (bf16[16,512]{1,0:T(8,128)(2,1)S(1)}, bf16[16,512]{1,0:T(8,128)(2,1)S(1)}, u32[]{:S(2)}, u32[]{:S(2)}) collective-permute-start(bf16[16,512]{1,0:T(8,128)(2,1)S(1)} %get-tuple-element.6), channel_id=1, source_target_pairs={{0,24},{1,31},{2,26},{3,29},{4,28},{5,27},{6,30},{7,25},{8,0},{9,7... | collective-permute-start | bytes 49160 | tf_op jit(solution)/shard_map/ppermute | solution.py:28
  55.2 6.8 %collective-permute-start.22 = (bf16[8,512]{1,0:T(8,128)(2,1)S(1)}, bf16[8,512]{1,0:T(8,128)(2,1)S(1)}, u32[]{:S(2)}, u32[]{:S(2)}) collective-permute-start(bf16[8,512]{1,0:T(8,128)(2,1)S(1)} %constant_dynamic-slice_fusion), channel_id=1, source_target_pairs={{0,24},{1,25},{2,26},{3,27},{4,28},{5,29},{6,30},{7,31},{8,0},{9,1... | collective-permute-start | bytes 24584 | tf_op jit(solution)/shard_map/ppermute | solution.py:28
  58.5 3.5 %collective-permute-start.26 = (bf16[8,512]{1,0:T(8,128)(2,1)S(1)}, bf16[8,512]{1,0:T(8,128)(2,1)S(1)}, u32[]{:S(2)}, u32[]{:S(2)}) collective-permute-start(bf16[8,512]{1,0:T(8,128)(2,1)S(1)} %dynamic-slice_convert_fusion), channel_id=1, source_target_pairs={{0,1},{1,0},{2,3},{3,2},{4,5},{5,4},{6,7},{7,6},{8,9},{9,8},{10,11... | collective-permute-start | bytes 24584 | tf_op jit(solution)/shard_map/ppermute | solution.py:28
  (5 other events, 27.2 us)

commit v2 on v1

--- a/solution.py
+++ b/solution.py
@@ -53,19 +53,21 @@
     def rows_of(block, start, count):
         return lax.dynamic_slice_in_dim(block, start, count, 0)
 
-    mine = lax.optimization_barrier(narrow(items))
-    block, bit = mine, 1
-    while bit < top // 2:
+    block = narrow(items)
+    block = in_order(block, swap(block, 1), core)
+    one = jnp.ones((), users.dtype)
+    block, shown, moving, one = lax.optimization_barrier((block, ratings, momentum, one))
+    users = lax.optimization_barrier(users * one)
+    bit = 2
+    while bit < n:
         block = in_order(block, swap(block, bit), me // bit % 2)
         bit *= 2
-    near, far, cross = swap(block, bit), swap(block, top), swap(block, bit + top)
-    side, end = me // bit % 2, me // top
-    whole = in_order(in_order(block, near, side), in_order(far, cross, side), end)
+    whole = lax.optimization_barrier(block)
     tiles = [ratings[:, step, :] for step in range(steps)]
-    tiles[0] = lax.optimization_barrier(tiles[0])
+    tiles[0] = lax.optimization_barrier(shown[:, 0, :])
 
-    owner = lax.broadcasted_iota(jnp.int32, (n, own, rank), 0)
-    share = jnp.where(owner == me, inertia * momentum[None], 0.0).reshape(-1, rank)
+    row = lax.broadcasted_iota(jnp.int32, (n * own, rank), 0) - me * own
+    share = jnp.where((row >= 0) & (row < own), inertia * jnp.tile(moving, (n, 1)), 0.0)
     for step in range(steps):
         last = step == steps - 1
         score = lax.dot_general(

time: 63 us -> 62.8 us (level)
  starting transfers between devices: 30.5 us -> 39.3 us
  waiting for transfers between devices: 20.7 us -> 12.8 us
  other arithmetic: 2.43 us -> 3.67 us
  matrix products: 7.01 us -> 5.79 us
  local copies, waits for them, and re-layouts: 1.1 us -> 0.04 us
    ppermute x27 -> x26, starting transfers between devices: 30.5 us -> 39.3 us  [route(): return lax.ppermute(block, AXES, pairs)]
    ppermute x27 -> x26, waiting for transfers between devices: 20.7 us -> 12.8 us  [route(): return lax.ppermute(block, AXES, pairs)]
    dot_general x4, matrix products: 3 us -> 1.78 us  [local(): lax.dot_general(users, whole, (((1,), (1,)), ((), ())), preferred_element...]
    squeeze x1, local copies, waits for them, and re-layouts: 0.91 us -> 0.01 us  [local(): tiles[0] = lax.optimization_barrier(shown[:, 0, :])]
    select_n x7 -> x6, other arithmetic: 0.07 us -> 0.77 us  [in_order(): jnp.where(late == 0, mine, other)]
    mul x1 -> x2, other arithmetic: 0.72 us -> 1.3 us  [the longest x1 1.29 us: local(): users = lax.optimization_barrier(users * one)]
  transfers between devices with their start and end apart: 27 -> 26, of which waited for: 14 -> 14; matrix products, arithmetic and copies ran while one was open for 8% -> 7% of each run, Pallas kernels for 0% -> 0%
where the time goes in v2:
time: 62.8 us; the launch traced here: 62.4 us
  starting transfers between devices  39.3 us (63%)
  waiting for transfers between devices  12.8 us (20%)
  matrix products  5.79 us (9%)
  other arithmetic  3.67 us (6%)
  between operations  0.84 us (1%)
    ppermute x26, starting transfers between devices, route(): return lax.ppermute(block, AXES, pairs)  39.3 us
    ppermute x26, waiting for transfers between devices, route(): return lax.ppermute(block, AXES, pairs)  12.8 us
    dot_general x4, matrix products, local(): change = jnp.dot(resid, whole, preferred_element_type=jnp.float32)  2.8 us
    dot_general x4, matrix products, local(): lax.dot_general(users, whole, (((1,), (1,)), ((), ())), preferred_element...  1.78 us
    mul x1, other arithmetic, local(): users = lax.optimization_barrier(users * one)  1.29 us
  transfers between devices with their start and end apart: 26, of which 14 were waited for; matrix products, arithmetic and copies ran while one was open for 7% of the time, Pallas kernels for 0%

profile of v2, /device:TPU:0, one launch (start us, length us, event | category | flops | bytes accessed | tf_op | source)
XLA Modules:
  0.0 62.4 jit_solution(3772960514876834136)
XLA Ops:
  3.4 3.0 %collective-permute-start.1 = (bf16[16,512]{1,0:T(8,128)(2,1)S(1)}, bf16[16,512]{1,0:T(8,128)(2,1)S(1)}, u32[]{:S(2)}, u32[]{:S(2)}) collective-permute-start(bf16[16,512]{1,0:T(8,128)(2,1)S(1)} %pad_maximum_fusion.2), channel_id=1, source_target_pairs={{0,2},{1,3},{2,0},{3,1},{4,6},{5,7},{6,4},{7,5},{8,10},{9,11},{10,... | collective-permute-start | bytes 49160 | tf_op jit(solution)/shard_map/ppermute | solution.py:28
  6.4 1.3 %broadcast_multiply_fusion = bf16[1024,512]{1,0:T(8,128)(2,1)S(1)} fusion(bf16[1024,512]{1,0:T(8,128)(2,1)} %param.4, bf16[]{:T(256)} %constant.69.clone.1), kind=kLoop, calls=%fused_computation.25 | loop fusion | flops 524288 | bytes 2097154 | tf_op jit(solution)/shard_map/mul | solution.py:60
  8.1 3.1 %collective-permute-start.2 = (bf16[32,512]{1,0:T(8,128)(2,1)S(1)}, bf16[32,512]{1,0:T(8,128)(2,1)S(1)}, u32[]{:S(2)}, u32[]{:S(2)}) collective-permute-start(bf16[32,512]{1,0:T(8,128)(2,1)S(1)} %pad_maximum_fusion.1), channel_id=1, source_target_pairs={{0,4},{1,5},{2,6},{3,7},{4,0},{5,1},{6,2},{7,3},{8,12},{9,13},{10,... | collective-permute-start | bytes 98312 | tf_op jit(solution)/shard_map/ppermute | solution.py:28
  11.2 1.9 %collective-permute-done.2 = bf16[32,512]{1,0:T(8,128)(2,1)S(1)} collective-permute-done((bf16[32,512]{1,0:T(8,128)(2,1)S(1)}, bf16[32,512]{1,0:T(8,128)(2,1)S(1)}, u32[]{:S(2)}, u32[]{:S(2)}) %collective-permute-start.2) | collective-permute-done | bytes 32800 | tf_op jit(solution)/shard_map/ppermute | solution.py:28
  14.0 2.8 %collective-permute-start.3 = (bf16[32,512]{1,0:T(8,128)(2,1)S(1)}, bf16[32,512]{1,0:T(8,128)(2,1)S(1)}, u32[]{:S(2)}, u32[]{:S(2)}) collective-permute-start(bf16[32,512]{1,0:T(8,128)(2,1)S(1)} %constant_dynamic-slice_fusion.3), channel_id=1, source_target_pairs={{0,24},{1,25},{2,26},{3,27},{4,28},{5,29},{6,30},{7,31},{8,0},{9,1... | collective-permute-start | bytes 98312 | tf_op jit(solution)/shard_map/ppermute | solution.py:28
  16.8 2.2 %collective-permute-start.6 = (bf16[64,512]{1,0:T(8,128)(2,1)S(1)}, bf16[64,512]{1,0:T(8,128)(2,1)S(1)}, u32[]{:S(2)}, u32[]{:S(2)}) collective-permute-start(bf16[64,512]{1,0:T(8,128)(2,1)S(1)} %add_convert_fusion.6), channel_id=1, source_target_pairs={{0,26},{1,29},{2,24},{3,31},{4,30},{5,25},{6,28},{7,27},{8,2},{9,5... | collective-permute-start | bytes 196616 | tf_op jit(solution)/shard_map/ppermute | solution.py:28
  20.4 1.5 %collective-permute-start.4 = (bf16[32,512]{1,0:T(8,128)(2,1)S(1)}, bf16[32,512]{1,0:T(8,128)(2,1)S(1)}, u32[]{:S(2)}, u32[]{:S(2)}) collective-permute-start(bf16[32,512]{1,0:T(8,128)(2,1)S(1)} %collective-permute-done.3), channel_id=1, source_target_pairs={{0,1},{1,0},{2,3},{3,2},{4,5},{5,4},{6,7},{7,6},{8,9},{9,8},{10,11... | collective-permute-start | bytes 98312 | tf_op jit(solution)/shard_map/ppermute | solution.py:28
  23.5 2.5 %collective-permute-start.8 = (bf16[64,512]{1,0:T(8,128)(2,1)S(1)}, bf16[64,512]{1,0:T(8,128)(2,1)S(1)}, u32[]{:S(2)}, u32[]{:S(2)}) collective-permute-start(bf16[64,512]{1,0:T(8,128)(2,1)S(1)} %add_convert_fusion.5), channel_id=1, source_target_pairs={{0,1},{1,0},{2,3},{3,2},{4,5},{5,4},{6,7},{7,6},{8,9},{9,8},{10,11... | collective-permute-start | bytes 196616 | tf_op jit(solution)/shard_map/ppermute | solution.py:28
  28.1 1.7 %collective-permute-start.9 = (bf16[32,512]{1,0:T(8,128)(2,1)S(1)}, bf16[32,512]{1,0:T(8,128)(2,1)S(1)}, u32[]{:S(2)}, u32[]{:S(2)}) collective-permute-start(bf16[32,512]{1,0:T(8,128)(2,1)S(1)} %constant_dynamic-slice_fusion.2), channel_id=1, source_target_pairs={{0,24},{1,25},{2,26},{3,27},{4,28},{5,29},{6,30},{7,31},{8,0},{9,1... | collective-permute-start | bytes 98312 | tf_op jit(solution)/shard_map/ppermute | solution.py:28
  29.8 1.0 %collective-permute-start.12 = (bf16[64,512]{1,0:T(8,128)(2,1)S(1)}, bf16[64,512]{1,0:T(8,128)(2,1)S(1)}, u32[]{:S(2)}, u32[]{:S(2)}) collective-permute-start(bf16[64,512]{1,0:T(8,128)(2,1)S(1)} %add_convert_fusion.4), channel_id=1, source_target_pairs={{0,26},{1,29},{2,24},{3,31},{4,30},{5,25},{6,28},{7,27},{8,2},{9,5... | collective-permute-start | bytes 196616 | tf_op jit(solution)/shard_map/ppermute | solution.py:28
  30.8 2.1 %collective-permute-start.13 = (bf16[64,512]{1,0:T(8,128)(2,1)S(1)}, bf16[64,512]{1,0:T(8,128)(2,1)S(1)}, u32[]{:S(2)}, u32[]{:S(2)}) collective-permute-start(bf16[64,512]{1,0:T(8,128)(2,1)S(1)} %add_convert_fusion.4), channel_id=1, source_target_pairs={{0,24},{1,31},{2,26},{3,29},{4,28},{5,27},{6,30},{7,25},{8,0},{9,7... | collective-permute-start | bytes 196616 | tf_op jit(solution)/shard_map/ppermute | solution.py:28
  33.4 1.2 %collective-permute-start.10 = (bf16[32,512]{1,0:T(8,128)(2,1)S(1)}, bf16[32,512]{1,0:T(8,128)(2,1)S(1)}, u32[]{:S(2)}, u32[]{:S(2)}) collective-permute-start(bf16[32,512]{1,0:T(8,128)(2,1)S(1)} %collective-permute-done.9), channel_id=1, source_target_pairs={{0,1},{1,0},{2,3},{3,2},{4,5},{5,4},{6,7},{7,6},{8,9},{9,8},{10,11... | collective-permute-start | bytes 98312 | tf_op jit(solution)/shard_map/ppermute | solution.py:28
  35.1 1.2 %collective-permute-done.13 = bf16[64,512]{1,0:T(8,128)(2,1)S(1)} collective-permute-done((bf16[64,512]{1,0:T(8,128)(2,1)S(1)}, bf16[64,512]{1,0:T(8,128)(2,1)S(1)}, u32[]{:S(2)}, u32[]{:S(2)}) %collective-permute-start.13) | collective-permute-done | bytes 65568 | tf_op jit(solution)/shard_map/ppermute | solution.py:28
  36.3 1.2 %collective-permute-start.14 = (bf16[64,512]{1,0:T(8,128)(2,1)S(1)}, bf16[64,512]{1,0:T(8,128)(2,1)S(1)}, u32[]{:S(2)}, u32[]{:S(2)}) collective-permute-start(bf16[64,512]{1,0:T(8,128)(2,1)S(1)} %add_convert_fusion.3), channel_id=1, source_target_pairs={{0,1},{1,0},{2,3},{3,2},{4,5},{5,4},{6,7},{7,6},{8,9},{9,8},{10,11... | collective-permute-start | bytes 196616 | tf_op jit(solution)/shard_map/ppermute | solution.py:28
  39.6 2.0 %collective-permute-start.15 = (bf16[32,512]{1,0:T(8,128)(2,1)S(1)}, bf16[32,512]{1,0:T(8,128)(2,1)S(1)}, u32[]{:S(2)}, u32[]{:S(2)}) collective-permute-start(bf16[32,512]{1,0:T(8,128)(2,1)S(1)} %constant_dynamic-slice_fusion.1), channel_id=1, source_target_pairs={{0,24},{1,25},{2,26},{3,27},{4,28},{5,29},{6,30},{7,31},{8,0},{9,1... | collective-permute-start | bytes 98312 | tf_op jit(solution)/shard_map/ppermute | solution.py:28
  41.7 1.1 %collective-permute-start.18 = (bf16[64,512]{1,0:T(8,128)(2,1)S(1)}, bf16[64,512]{1,0:T(8,128)(2,1)S(1)}, u32[]{:S(2)}, u32[]{:S(2)}) collective-permute-start(bf16[64,512]{1,0:T(8,128)(2,1)S(1)} %add_convert_fusion.2), channel_id=1, source_target_pairs={{0,26},{1,29},{2,24},{3,31},{4,30},{5,25},{6,28},{7,27},{8,2},{9,5... | collective-permute-start | bytes 196616 | tf_op jit(solution)/shard_map/ppermute | solution.py:28
  42.7 1.7 %collective-permute-start.19 = (bf16[64,512]{1,0:T(8,128)(2,1)S(1)}, bf16[64,512]{1,0:T(8,128)(2,1)S(1)}, u32[]{:S(2)}, u32[]{:S(2)}) collective-permute-start(bf16[64,512]{1,0:T(8,128)(2,1)S(1)} %add_convert_fusion.2), channel_id=1, source_target_pairs={{0,24},{1,31},{2,26},{3,29},{4,28},{5,27},{6,30},{7,25},{8,0},{9,7... | collective-permute-start | bytes 196616 | tf_op jit(solution)/shard_map/ppermute | solution.py:28
  45.0 1.4 %collective-permute-start.16 = (bf16[32,512]{1,0:T(8,128)(2,1)S(1)}, bf16[32,512]{1,0:T(8,128)(2,1)S(1)}, u32[]{:S(2)}, u32[]{:S(2)}) collective-permute-start(bf16[32,512]{1,0:T(8,128)(2,1)S(1)} %collective-permute-done.15), channel_id=1, source_target_pairs={{0,1},{1,0},{2,3},{3,2},{4,5},{5,4},{6,7},{7,6},{8,9},{9,8},{10,11... | collective-permute-start | bytes 98312 | tf_op jit(solution)/shard_map/ppermute | solution.py:28
  47.0 1.1 %collective-permute-done.19 = bf16[64,512]{1,0:T(8,128)(2,1)S(1)} collective-permute-done((bf16[64,512]{1,0:T(8,128)(2,1)S(1)}, bf16[64,512]{1,0:T(8,128)(2,1)S(1)}, u32[]{:S(2)}, u32[]{:S(2)}) %collective-permute-start.19) | collective-permute-done | bytes 65568 | tf_op jit(solution)/shard_map/ppermute | solution.py:28
  48.1 1.0 %collective-permute-start.20 = (bf16[64,512]{1,0:T(8,128)(2,1)S(1)}, bf16[64,512]{1,0:T(8,128)(2,1)S(1)}, u32[]{:S(2)}, u32[]{:S(2)}) collective-permute-start(bf16[64,512]{1,0:T(8,128)(2,1)S(1)} %add_convert_fusion.1), channel_id=1, source_target_pairs={{0,1},{1,0},{2,3},{3,2},{4,5},{5,4},{6,7},{7,6},{8,9},{9,8},{10,11... | collective-permute-start | bytes 196616 | tf_op jit(solution)/shard_map/ppermute | solution.py:28
  52.2 2.3 %collective-permute-start.23 = (bf16[16,512]{1,0:T(8,128)(2,1)S(1)}, bf16[16,512]{1,0:T(8,128)(2,1)S(1)}, u32[]{:S(2)}, u32[]{:S(2)}) collective-permute-start(bf16[16,512]{1,0:T(8,128)(2,1)S(1)} %get-tuple-element.13), channel_id=1, source_target_pairs={{0,26},{1,29},{2,24},{3,31},{4,30},{5,25},{6,28},{7,27},{8,2},{9,5... | collective-permute-start | bytes 49160 | tf_op jit(solution)/shard_map/ppermute | solution.py:28
  55.3 2.1 %collective-permute-start.21 = (bf16[8,512]{1,0:T(8,128)(2,1)S(1)}, bf16[8,512]{1,0:T(8,128)(2,1)S(1)}, u32[]{:S(2)}, u32[]{:S(2)}) collective-permute-start(bf16[8,512]{1,0:T(8,128)(2,1)S(1)} %constant_dynamic-slice_fusion), channel_id=1, source_target_pairs={{0,24},{1,25},{2,26},{3,27},{4,28},{5,29},{6,30},{7,31},{8,0},{9,1... | collective-permute-start | bytes 24584 | tf_op jit(solution)/shard_map/ppermute | solution.py:28
  58.3 2.1 %collective-permute-start.25 = (bf16[8,512]{1,0:T(8,128)(2,1)S(1)}, bf16[8,512]{1,0:T(8,128)(2,1)S(1)}, u32[]{:S(2)}, u32[]{:S(2)}) collective-permute-start(bf16[8,512]{1,0:T(8,128)(2,1)S(1)} %dynamic-slice_convert_fusion), channel_id=1, source_target_pairs={{0,1},{1,0},{2,3},{3,2},{4,5},{5,4},{6,7},{7,6},{8,9},{9,8},{10,11... | collective-permute-start | bytes 24584 | tf_op jit(solution)/shard_map/ppermute | solution.py:28
  60.4 1.4 %subtract_convert_fusion = bf16[1024,512]{1,0:T(8,128)(2,1)} fusion(bf16[1024,512]{1,0:T(8,128)(2,1)S(1)} %subtract_convert_fusion.1, bf16[1024,64]{0,1:T(8,128)(2,1)S(1)} %fusion.11, bf16[64,512]{1,0:T(8,128)(2,1)S(1)} %subtract_convert_fusion.4), kind=kOutput, calls=%fused_computation | convolution fusion | flops 69206016 | bytes 2293760 | tf_op jit(solution)/shard_map/dot_general | solution.py:104
  (76 shorter events, 18.8 us)
Async XLA Ops:
  3.4 4.7 %collective-permute-start.1 = (bf16[16,512]{1,0:T(8,128)(2,1)S(1)}, bf16[16,512]{1,0:T(8,128)(2,1)S(1)}, u32[]{:S(2)}, u32[]{:S(2)}) collective-permute-start(bf16[16,512]{1,0:T(8,128)(2,1)S(1)} %pad_maximum_fusion.2), channel_id=1, source_target_pairs={{0,2},{1,3},{2,0},{3,1},{4,6},{5,7},{6,4},{7,5},{8,10},{9,11},{10,... | collective-permute-start | bytes 49160 | tf_op jit(solution)/shard_map/ppermute | solution.py:28
  8.1 5.0 %collective-permute-start.2 = (bf16[32,512]{1,0:T(8,128)(2,1)S(1)}, bf16[32,512]{1,0:T(8,128)(2,1)S(1)}, u32[]{:S(2)}, u32[]{:S(2)}) collective-permute-start(bf16[32,512]{1,0:T(8,128)(2,1)S(1)} %pad_maximum_fusion.1), channel_id=1, source_target_pairs={{0,4},{1,5},{2,6},{3,7},{4,0},{5,1},{6,2},{7,3},{8,12},{9,13},{10,... | collective-permute-start | bytes 98312 | tf_op jit(solution)/shard_map/ppermute | solution.py:28
  13.9 2.9 %collective-permute-start.5 = (bf16[64,512]{1,0:T(8,128)(2,1)S(1)}, bf16[64,512]{1,0:T(8,128)(2,1)S(1)}, u32[]{:S(2)}, u32[]{:S(2)}) collective-permute-start(bf16[64,512]{1,0:T(8,128)(2,1)S(1)} %get-tuple-element.27), channel_id=1, source_target_pairs={{0,1},{1,0},{2,3},{3,2},{4,5},{5,4},{6,7},{7,6},{8,9},{9,8},{10,11... | collective-permute-start | bytes 196616 | tf_op jit(solution)/shard_map/ppermute | solution.py:28
  14.0 6.4 %collective-permute-start.3 = (bf16[32,512]{1,0:T(8,128)(2,1)S(1)}, bf16[32,512]{1,0:T(8,128)(2,1)S(1)}, u32[]{:S(2)}, u32[]{:S(2)}) collective-permute-start(bf16[32,512]{1,0:T(8,128)(2,1)S(1)} %constant_dynamic-slice_fusion.3), channel_id=1, source_target_pairs={{0,24},{1,25},{2,26},{3,27},{4,28},{5,29},{6,30},{7,31},{8,0},{9,1... | collective-permute-start | bytes 98312 | tf_op jit(solution)/shard_map/ppermute | solution.py:28
  16.8 5.9 %collective-permute-start.6 = (bf16[64,512]{1,0:T(8,128)(2,1)S(1)}, bf16[64,512]{1,0:T(8,128)(2,1)S(1)}, u32[]{:S(2)}, u32[]{:S(2)}) collective-permute-start(bf16[64,512]{1,0:T(8,128)(2,1)S(1)} %add_convert_fusion.6), channel_id=1, source_target_pairs={{0,26},{1,29},{2,24},{3,31},{4,30},{5,25},{6,28},{7,27},{8,2},{9,5... | collective-permute-start | bytes 196616 | tf_op jit(solution)/shard_map/ppermute | solution.py:28
  19.1 4.4 %collective-permute-start.7 = (bf16[64,512]{1,0:T(8,128)(2,1)S(1)}, bf16[64,512]{1,0:T(8,128)(2,1)S(1)}, u32[]{:S(2)}, u32[]{:S(2)}) collective-permute-start(bf16[64,512]{1,0:T(8,128)(2,1)S(1)} %add_convert_fusion.6), channel_id=1, source_target_pairs={{0,24},{1,31},{2,26},{3,29},{4,28},{5,27},{6,30},{7,25},{8,0},{9,7... | collective-permute-start | bytes 196616 | tf_op jit(solution)/shard_map/ppermute | solution.py:28
  20.4 5.6 %collective-permute-start.4 = (bf16[32,512]{1,0:T(8,128)(2,1)S(1)}, bf16[32,512]{1,0:T(8,128)(2,1)S(1)}, u32[]{:S(2)}, u32[]{:S(2)}) collective-permute-start(bf16[32,512]{1,0:T(8,128)(2,1)S(1)} %collective-permute-done.3), channel_id=1, source_target_pairs={{0,1},{1,0},{2,3},{3,2},{4,5},{5,4},{6,7},{7,6},{8,9},{9,8},{10,11... | collective-permute-start | bytes 98312 | tf_op jit(solution)/shard_map/ppermute | solution.py:28
  23.5 3.4 %collective-permute-start.8 = (bf16[64,512]{1,0:T(8,128)(2,1)S(1)}, bf16[64,512]{1,0:T(8,128)(2,1)S(1)}, u32[]{:S(2)}, u32[]{:S(2)}) collective-permute-start(bf16[64,512]{1,0:T(8,128)(2,1)S(1)} %add_convert_fusion.5), channel_id=1, source_target_pairs={{0,1},{1,0},{2,3},{3,2},{4,5},{5,4},{6,7},{7,6},{8,9},{9,8},{10,11... | collective-permute-start | bytes 196616 | tf_op jit(solution)/shard_map/ppermute | solution.py:28
  27.7 2.1 %collective-permute-start.11 = (bf16[64,512]{1,0:T(8,128)(2,1)S(1)}, bf16[64,512]{1,0:T(8,128)(2,1)S(1)}, u32[]{:S(2)}, u32[]{:S(2)}) collective-permute-start(bf16[64,512]{1,0:T(8,128)(2,1)S(1)} %get-tuple-element.29), channel_id=1, source_target_pairs={{0,1},{1,0},{2,3},{3,2},{4,5},{5,4},{6,7},{7,6},{8,9},{9,8},{10,11... | collective-permute-start | bytes 196616 | tf_op jit(solution)/shard_map/ppermute | solution.py:28
  28.1 5.2 %collective-permute-start.9 = (bf16[32,512]{1,0:T(8,128)(2,1)S(1)}, bf16[32,512]{1,0:T(8,128)(2,1)S(1)}, u32[]{:S(2)}, u32[]{:S(2)}) collective-permute-start(bf16[32,512]{1,0:T(8,128)(2,1)S(1)} %constant_dynamic-slice_fusion.2), channel_id=1, source_target_pairs={{0,24},{1,25},{2,26},{3,27},{4,28},{5,29},{6,30},{7,31},{8,0},{9,1... | collective-permute-start | bytes 98312 | tf_op jit(solution)/shard_map/ppermute | solution.py:28
  29.8 5.3 %collective-permute-start.12 = (bf16[64,512]{1,0:T(8,128)(2,1)S(1)}, bf16[64,512]{1,0:T(8,128)(2,1)S(1)}, u32[]{:S(2)}, u32[]{:S(2)}) collective-permute-start(bf16[64,512]{1,0:T(8,128)(2,1)S(1)} %add_convert_fusion.4), channel_id=1, source_target_pairs={{0,26},{1,29},{2,24},{3,31},{4,30},{5,25},{6,28},{7,27},{8,2},{9,5... | collective-permute-start | bytes 196616 | tf_op jit(solution)/shard_map/ppermute | solution.py:28
  30.8 5.5 %collective-permute-start.13 = (bf16[64,512]{1,0:T(8,128)(2,1)S(1)}, bf16[64,512]{1,0:T(8,128)(2,1)S(1)}, u32[]{:S(2)}, u32[]{:S(2)}) collective-permute-start(bf16[64,512]{1,0:T(8,128)(2,1)S(1)} %add_convert_fusion.4), channel_id=1, source_target_pairs={{0,24},{1,31},{2,26},{3,29},{4,28},{5,27},{6,30},{7,25},{8,0},{9,7... | collective-permute-start | bytes 196616 | tf_op jit(solution)/shard_map/ppermute | solution.py:28
  33.4 4.1 %collective-permute-start.10 = (bf16[32,512]{1,0:T(8,128)(2,1)S(1)}, bf16[32,512]{1,0:T(8,128)(2,1)S(1)}, u32[]{:S(2)}, u32[]{:S(2)}) collective-permute-start(bf16[32,512]{1,0:T(8,128)(2,1)S(1)} %collective-permute-done.9), channel_id=1, source_target_pairs={{0,1},{1,0},{2,3},{3,2},{4,5},{5,4},{6,7},{7,6},{8,9},{9,8},{10,11... | collective-permute-start | bytes 98312 | tf_op jit(solution)/shard_map/ppermute | solution.py:28
  36.3 2.1 %collective-permute-start.14 = (bf16[64,512]{1,0:T(8,128)(2,1)S(1)}, bf16[64,512]{1,0:T(8,128)(2,1)S(1)}, u32[]{:S(2)}, u32[]{:S(2)}) collective-permute-start(bf16[64,512]{1,0:T(8,128)(2,1)S(1)} %add_convert_fusion.3), channel_id=1, source_target_pairs={{0,1},{1,0},{2,3},{3,2},{4,5},{5,4},{6,7},{7,6},{8,9},{9,8},{10,11... | collective-permute-start | bytes 196616 | tf_op jit(solution)/shard_map/ppermute | solution.py:28
  39.2 2.5 %collective-permute-start.17 = (bf16[64,512]{1,0:T(8,128)(2,1)S(1)}, bf16[64,512]{1,0:T(8,128)(2,1)S(1)}, u32[]{:S(2)}, u32[]{:S(2)}) collective-permute-start(bf16[64,512]{1,0:T(8,128)(2,1)S(1)} %get-tuple-element.31), channel_id=1, source_target_pairs={{0,1},{1,0},{2,3},{3,2},{4,5},{5,4},{6,7},{7,6},{8,9},{9,8},{10,11... | collective-permute-start | bytes 196616 | tf_op jit(solution)/shard_map/ppermute | solution.py:28
  39.6 5.3 %collective-permute-start.15 = (bf16[32,512]{1,0:T(8,128)(2,1)S(1)}, bf16[32,512]{1,0:T(8,128)(2,1)S(1)}, u32[]{:S(2)}, u32[]{:S(2)}) collective-permute-start(bf16[32,512]{1,0:T(8,128)(2,1)S(1)} %constant_dynamic-slice_fusion.1), channel_id=1, source_target_pairs={{0,24},{1,25},{2,26},{3,27},{4,28},{5,29},{6,30},{7,31},{8,0},{9,1... | collective-permute-start | bytes 98312 | tf_op jit(solution)/shard_map/ppermute | solution.py:28
  41.7 5.3 %collective-permute-start.18 = (bf16[64,512]{1,0:T(8,128)(2,1)S(1)}, bf16[64,512]{1,0:T(8,128)(2,1)S(1)}, u32[]{:S(2)}, u32[]{:S(2)}) collective-permute-start(bf16[64,512]{1,0:T(8,128)(2,1)S(1)} %add_convert_fusion.2), channel_id=1, source_target_pairs={{0,26},{1,29},{2,24},{3,31},{4,30},{5,25},{6,28},{7,27},{8,2},{9,5... | collective-permute-start | bytes 196616 | tf_op jit(solution)/shard_map/ppermute | solution.py:28
  42.7 5.4 %collective-permute-start.19 = (bf16[64,512]{1,0:T(8,128)(2,1)S(1)}, bf16[64,512]{1,0:T(8,128)(2,1)S(1)}, u32[]{:S(2)}, u32[]{:S(2)}) collective-permute-start(bf16[64,512]{1,0:T(8,128)(2,1)S(1)} %add_convert_fusion.2), channel_id=1, source_target_pairs={{0,24},{1,31},{2,26},{3,29},{4,28},{5,27},{6,30},{7,25},{8,0},{9,7... | collective-permute-start | bytes 196616 | tf_op jit(solution)/shard_map/ppermute | solution.py:28
  45.0 4.2 %collective-permute-start.16 = (bf16[32,512]{1,0:T(8,128)(2,1)S(1)}, bf16[32,512]{1,0:T(8,128)(2,1)S(1)}, u32[]{:S(2)}, u32[]{:S(2)}) collective-permute-start(bf16[32,512]{1,0:T(8,128)(2,1)S(1)} %collective-permute-done.15), channel_id=1, source_target_pairs={{0,1},{1,0},{2,3},{3,2},{4,5},{5,4},{6,7},{7,6},{8,9},{9,8},{10,11... | collective-permute-start | bytes 98312 | tf_op jit(solution)/shard_map/ppermute | solution.py:28
  48.1 1.9 %collective-permute-start.20 = (bf16[64,512]{1,0:T(8,128)(2,1)S(1)}, bf16[64,512]{1,0:T(8,128)(2,1)S(1)}, u32[]{:S(2)}, u32[]{:S(2)}) collective-permute-start(bf16[64,512]{1,0:T(8,128)(2,1)S(1)} %add_convert_fusion.1), channel_id=1, source_target_pairs={{0,1},{1,0},{2,3},{3,2},{4,5},{5,4},{6,7},{7,6},{8,9},{9,8},{10,11... | collective-permute-start | bytes 196616 | tf_op jit(solution)/shard_map/ppermute | solution.py:28
  52.2 5.2 %collective-permute-start.23 = (bf16[16,512]{1,0:T(8,128)(2,1)S(1)}, bf16[16,512]{1,0:T(8,128)(2,1)S(1)}, u32[]{:S(2)}, u32[]{:S(2)}) collective-permute-start(bf16[16,512]{1,0:T(8,128)(2,1)S(1)} %get-tuple-element.13), channel_id=1, source_target_pairs={{0,26},{1,29},{2,24},{3,31},{4,30},{5,25},{6,28},{7,27},{8,2},{9,5... | collective-permute-start | bytes 49160 | tf_op jit(solution)/shard_map/ppermute | solution.py:28
  54.5 3.7 %collective-permute-start.24 = (bf16[16,512]{1,0:T(8,128)(2,1)S(1)}, bf16[16,512]{1,0:T(8,128)(2,1)S(1)}, u32[]{:S(2)}, u32[]{:S(2)}) collective-permute-start(bf16[16,512]{1,0:T(8,128)(2,1)S(1)} %get-tuple-element.14), channel_id=1, source_target_pairs={{0,24},{1,31},{2,26},{3,29},{4,28},{5,27},{6,30},{7,25},{8,0},{9,7... | collective-permute-start | bytes 49160 | tf_op jit(solution)/shard_map/ppermute | solution.py:28
  55.3 6.5 %collective-permute-start.21 = (bf16[8,512]{1,0:T(8,128)(2,1)S(1)}, bf16[8,512]{1,0:T(8,128)(2,1)S(1)}, u32[]{:S(2)}, u32[]{:S(2)}) collective-permute-start(bf16[8,512]{1,0:T(8,128)(2,1)S(1)} %constant_dynamic-slice_fusion), channel_id=1, source_target_pairs={{0,24},{1,25},{2,26},{3,27},{4,28},{5,29},{6,30},{7,31},{8,0},{9,1... | collective-permute-start | bytes 24584 | tf_op jit(solution)/shard_map/ppermute | solution.py:28
  58.3 3.5 %collective-permute-start.25 = (bf16[8,512]{1,0:T(8,128)(2,1)S(1)}, bf16[8,512]{1,0:T(8,128)(2,1)S(1)}, u32[]{:S(2)}, u32[]{:S(2)}) collective-permute-start(bf16[8,512]{1,0:T(8,128)(2,1)S(1)} %dynamic-slice_convert_fusion), channel_id=1, source_target_pairs={{0,1},{1,0},{2,3},{3,2},{4,5},{5,4},{6,7},{7,6},{8,9},{9,8},{10,11... | collective-permute-start | bytes 24584 | tf_op jit(solution)/shard_map/ppermute | solution.py:28
  (4 other events, 14.7 us)

commit v3 on v2

--- a/solution.py
+++ b/solution.py
@@ -53,16 +53,21 @@
     def rows_of(block, start, count):
         return lax.dynamic_slice_in_dim(block, start, count, 0)
 
-    block = narrow(items)
+    block = lax.optimization_barrier(narrow(items))
     block = in_order(block, swap(block, 1), core)
     one = jnp.ones((), users.dtype)
     block, shown, moving, one = lax.optimization_barrier((block, ratings, momentum, one))
     users = lax.optimization_barrier(users * one)
     bit = 2
-    while bit < n:
+    while bit < top // 2:
         block = in_order(block, swap(block, bit), me // bit % 2)
         bit *= 2
-    whole = lax.optimization_barrier(block)
+    near = swap(block, bit)
+    far = swap(block, top)
+    cross = swap(block, bit + top)
+    side, end = me // bit % 2, me // top
+    whole = in_order(in_order(block, near, side), in_order(far, cross, side), end)
+    whole = lax.optimization_barrier(whole)
     tiles = [ratings[:, step, :] for step in range(steps)]
     tiles[0] = lax.optimization_barrier(shown[:, 0, :])
 
@@ -83,8 +88,8 @@
             grads = grads + wide(swap(total, bit))
             total = narrow(grads)
             bit *= 2
-        first = (bit, top)
-        second = (0, bit + top)
+        first = (0, top)
+        second = (bit, bit + top)
 
         def part(flip):
             return rows_of(total, (place ^ flip // 2) * 2 * own, 2 * own)
@@ -99,7 +104,7 @@
         if last:
             value = rows_of(whole, me * own, own)
         else:
-            value = rows_of(whole, core * (n // 2 * own), n // 2 * own)
+            value = whole
         value = back(value, 0, 0)
         change = jnp.dot(resid, whole, preferred_element_type=jnp.float32)
         users = narrow(wide(users) - user_rate * factor * change)
@@ -110,7 +115,6 @@
         else:
             moment = narrow(moment)
             moment = wide(moment) + wide(swap(moment, 1))
-            value = in_order(value, swap(value, 1), core)
         fresh = wide(value) - item_rate * moment
         whole = narrow(fresh)
         share = (inertia / n) * moment

time: 62.8 us -> 59.1 us (0.941)
  starting transfers between devices: 39.3 us -> 23.6 us
  waiting for transfers between devices: 12.8 us -> 24.6 us
  local copies, waits for them, and re-layouts: 0.04 us -> 0.93 us
  other arithmetic: 3.67 us -> 2.94 us
    ppermute x26 -> x24, starting transfers between devices: 39.3 us -> 23.6 us  [route(): return lax.ppermute(block, AXES, pairs)]
    ppermute x26 -> x24, waiting for transfers between devices: 12.8 us -> 24.6 us  [route(): return lax.ppermute(block, AXES, pairs)]
    squeeze x1, local copies, waits for them, and re-layouts: 0.01 us -> 0.91 us  [local(): tiles[0] = lax.optimization_barrier(shown[:, 0, :])]
    select_n x6 -> x4, other arithmetic: 0.77 us -> 0.04 us  [in_order(): jnp.where(late == 0, mine, other)]
  transfers between devices with their start and end apart: 26 -> 24, of which waited for: 14 -> 14; matrix products, arithmetic and copies ran while one was open for 7% -> 9% of each run, Pallas kernels for 0% -> 0%
where the time goes in v3:
time: 59.1 us; the launch traced here: 58.8 us
  waiting for transfers between devices  24.6 us (42%)
  starting transfers between devices  23.6 us (40%)
  matrix products  5.8 us (10%)
  other arithmetic  2.94 us (5%)
  local copies, waits for them, and re-layouts  0.93 us (2%)
  between operations  0.89 us (2%)
    ppermute x24, waiting for transfers between devices, route(): return lax.ppermute(block, AXES, pairs)  24.6 us
    ppermute x24, starting transfers between devices, route(): return lax.ppermute(block, AXES, pairs)  23.6 us
    dot_general x4, matrix products, local(): change = jnp.dot(resid, whole, preferred_element_type=jnp.float32)  2.81 us
    dot_general x4, matrix products, local(): lax.dot_general(users, whole, (((1,), (1,)), ((), ())), preferred_element...  1.78 us
    mul x1, other arithmetic, local(): users = lax.optimization_barrier(users * one)  1.3 us
    dot_general x4, matrix products, local(): lax.dot_general(resid, users, (((0,), (0,)), ((), ())), preferred_element...  1.21 us
  transfers between devices with their start and end apart: 24, of which 14 were waited for; matrix products, arithmetic and copies ran while one was open for 9% of the time, Pallas kernels for 0%

profile of v3, /device:TPU:0, one launch (start us, length us, event | category | flops | bytes accessed | tf_op | source)
XLA Modules:
  0.0 58.8 jit_solution(10404643888160608010)
XLA Ops:
  1.9 0.8 %collective-permute-done = bf16[8,512]{1,0:T(8,128)(2,1)S(1)} collective-permute-done((bf16[8,512]{1,0:T(8,128)(2,1)S(1)}, bf16[8,512]{1,0:T(8,128)(2,1)S(1)}, u32[]{:S(2)}, u32[]{:S(2)}) %collective-permute-start) | collective-permute-done | bytes 8224 | tf_op jit(solution)/shard_map/ppermute | solution.py:28
  2.7 3.0 %collective-permute-start.1 = (bf16[16,512]{1,0:T(8,128)(2,1)S(1)}, bf16[16,512]{1,0:T(8,128)(2,1)S(1)}, u32[]{:S(2)}, u32[]{:S(2)}) collective-permute-start(bf16[16,512]{1,0:T(8,128)(2,1)S(1)} %pad_maximum_fusion.3), channel_id=1, source_target_pairs={{0,2},{1,3},{2,0},{3,1},{4,6},{5,7},{6,4},{7,5},{8,10},{9,11},{10,... | collective-permute-start | bytes 49160 | tf_op jit(solution)/shard_map/ppermute | solution.py:28
  5.7 2.6 %collective-permute-start.2 = (bf16[16,512]{1,0:T(8,128)(2,1)S(1)}, bf16[16,512]{1,0:T(8,128)(2,1)S(1)}, u32[]{:S(2)}, u32[]{:S(2)}) collective-permute-start(bf16[16,512]{1,0:T(8,128)(2,1)S(1)} %pad_maximum_fusion.3), channel_id=1, source_target_pairs={{0,4},{1,5},{2,6},{3,7},{4,0},{5,1},{6,2},{7,3},{8,12},{9,13},{10,... | collective-permute-start | bytes 49160 | tf_op jit(solution)/shard_map/ppermute | solution.py:28
  8.2 0.9 %slice_bitcast_fusion = bf16[1024,64]{0,1:T(8,128)(2,1)S(1)} fusion(bf16[1024,4,64]{0,2,1:T(8,128)(2,1)} %param.7), kind=kLoop, calls=%fused_computation.43 | loop fusion | bytes 262144 | tf_op jit(solution)/shard_map/squeeze | solution.py:72
  9.2 1.3 %broadcast_multiply_fusion = bf16[1024,512]{1,0:T(8,128)(2,1)S(1)} fusion(bf16[1024,512]{1,0:T(8,128)(2,1)} %param.4, bf16[]{:T(256)} %constant.64.clone.1), kind=kLoop, calls=%fused_computation.25 | loop fusion | flops 524288 | bytes 2097154 | tf_op jit(solution)/shard_map/mul | solution.py:60
  10.5 3.2 %collective-permute-done.3 = bf16[16,512]{1,0:T(8,128)(2,1)S(1)} collective-permute-done((bf16[16,512]{1,0:T(8,128)(2,1)S(1)}, bf16[16,512]{1,0:T(8,128)(2,1)S(1)}, u32[]{:S(2)}, u32[]{:S(2)}) %collective-permute-start.3) | collective-permute-done | bytes 16416 | tf_op jit(solution)/shard_map/ppermute | solution.py:28
  14.7 1.2 %collective-permute-done.5 = bf16[64,512]{1,0:T(8,128)(2,1)S(1)} collective-permute-done((bf16[64,512]{1,0:T(8,128)(2,1)S(1)}, bf16[64,512]{1,0:T(8,128)(2,1)S(1)}, u32[]{:S(2)}, u32[]{:S(2)}) %collective-permute-start.5) | collective-permute-done | bytes 65568 | tf_op jit(solution)/shard_map/ppermute | solution.py:28
  15.9 2.5 %collective-permute-start.6 = (bf16[64,512]{1,0:T(8,128)(2,1)S(1)}, bf16[64,512]{1,0:T(8,128)(2,1)S(1)}, u32[]{:S(2)}, u32[]{:S(2)}) collective-permute-start(bf16[64,512]{1,0:T(8,128)(2,1)S(1)} %add_convert_fusion.6), channel_id=1, source_target_pairs={{0,24},{1,29},{2,26},{3,31},{4,28},{5,25},{6,30},{7,27},{8,0},{9,5... | collective-permute-start | bytes 196616 | tf_op jit(solution)/shard_map/ppermute | solution.py:28
  19.0 1.5 %collective-permute-done.6 = bf16[64,512]{1,0:T(8,128)(2,1)S(1)} collective-permute-done((bf16[64,512]{1,0:T(8,128)(2,1)S(1)}, bf16[64,512]{1,0:T(8,128)(2,1)S(1)}, u32[]{:S(2)}, u32[]{:S(2)}) %collective-permute-start.6) | collective-permute-done | bytes 65568 | tf_op jit(solution)/shard_map/ppermute | solution.py:28
  20.4 3.2 %collective-permute-done.7 = bf16[64,512]{1,0:T(8,128)(2,1)S(1)} collective-permute-done((bf16[64,512]{1,0:T(8,128)(2,1)S(1)}, bf16[64,512]{1,0:T(8,128)(2,1)S(1)}, u32[]{:S(2)}, u32[]{:S(2)}) %collective-permute-start.7) | collective-permute-done | bytes 65568 | tf_op jit(solution)/shard_map/ppermute | solution.py:28
  26.0 1.1 %collective-permute-done.10 = bf16[64,512]{1,0:T(8,128)(2,1)S(1)} collective-permute-done((bf16[64,512]{1,0:T(8,128)(2,1)S(1)}, bf16[64,512]{1,0:T(8,128)(2,1)S(1)}, u32[]{:S(2)}, u32[]{:S(2)}) %collective-permute-start.10) | collective-permute-done | bytes 65568 | tf_op jit(solution)/shard_map/ppermute | solution.py:28
  27.1 2.5 %collective-permute-start.11 = (bf16[64,512]{1,0:T(8,128)(2,1)S(1)}, bf16[64,512]{1,0:T(8,128)(2,1)S(1)}, u32[]{:S(2)}, u32[]{:S(2)}) collective-permute-start(bf16[64,512]{1,0:T(8,128)(2,1)S(1)} %add_convert_fusion.4), channel_id=1, source_target_pairs={{0,24},{1,29},{2,26},{3,31},{4,28},{5,25},{6,30},{7,27},{8,0},{9,5... | collective-permute-start | bytes 196616 | tf_op jit(solution)/shard_map/ppermute | solution.py:28
  29.6 2.2 %collective-permute-start.9 = (bf16[64,512]{1,0:T(8,128)(2,1)S(1)}, bf16[64,512]{1,0:T(8,128)(2,1)S(1)}, u32[]{:S(2)}, u32[]{:S(2)}) collective-permute-start(bf16[64,512]{1,0:T(8,128)(2,1)S(1)} %subtract_convert_fusion.6), channel_id=1, source_target_pairs={{0,24},{1,25},{2,26},{3,27},{4,28},{5,29},{6,30},{7,31},{8,0},{9,1... | collective-permute-start | bytes 196616 | tf_op jit(solution)/shard_map/ppermute | solution.py:28
  31.9 3.7 %collective-permute-done.12 = bf16[64,512]{1,0:T(8,128)(2,1)S(1)} collective-permute-done((bf16[64,512]{1,0:T(8,128)(2,1)S(1)}, bf16[64,512]{1,0:T(8,128)(2,1)S(1)}, u32[]{:S(2)}, u32[]{:S(2)}) %collective-permute-start.12) | collective-permute-done | bytes 65568 | tf_op jit(solution)/shard_map/ppermute | solution.py:28
  36.2 0.8 %collective-permute-done.13 = bf16[64,512]{1,0:T(8,128)(2,1)S(1)} collective-permute-done((bf16[64,512]{1,0:T(8,128)(2,1)S(1)}, bf16[64,512]{1,0:T(8,128)(2,1)S(1)}, u32[]{:S(2)}, u32[]{:S(2)}) %collective-permute-start.13) | collective-permute-done | bytes 65568 | tf_op jit(solution)/shard_map/ppermute | solution.py:28
  37.9 1.1 %collective-permute-done.15 = bf16[64,512]{1,0:T(8,128)(2,1)S(1)} collective-permute-done((bf16[64,512]{1,0:T(8,128)(2,1)S(1)}, bf16[64,512]{1,0:T(8,128)(2,1)S(1)}, u32[]{:S(2)}, u32[]{:S(2)}) %collective-permute-start.15) | collective-permute-done | bytes 65568 | tf_op jit(solution)/shard_map/ppermute | solution.py:28
  39.1 1.7 %collective-permute-start.16 = (bf16[64,512]{1,0:T(8,128)(2,1)S(1)}, bf16[64,512]{1,0:T(8,128)(2,1)S(1)}, u32[]{:S(2)}, u32[]{:S(2)}) collective-permute-start(bf16[64,512]{1,0:T(8,128)(2,1)S(1)} %add_convert_fusion.2), channel_id=1, source_target_pairs={{0,24},{1,29},{2,26},{3,31},{4,28},{5,25},{6,30},{7,27},{8,0},{9,5... | collective-permute-start | bytes 196616 | tf_op jit(solution)/shard_map/ppermute | solution.py:28
  40.8 2.6 %collective-permute-start.14 = (bf16[64,512]{1,0:T(8,128)(2,1)S(1)}, bf16[64,512]{1,0:T(8,128)(2,1)S(1)}, u32[]{:S(2)}, u32[]{:S(2)}) collective-permute-start(bf16[64,512]{1,0:T(8,128)(2,1)S(1)} %subtract_convert_fusion.5), channel_id=1, source_target_pairs={{0,24},{1,25},{2,26},{3,27},{4,28},{5,29},{6,30},{7,31},{8,0},{9,1... | collective-permute-start | bytes 196616 | tf_op jit(solution)/shard_map/ppermute | solution.py:28
  43.4 3.3 %collective-permute-done.17 = bf16[64,512]{1,0:T(8,128)(2,1)S(1)} collective-permute-done((bf16[64,512]{1,0:T(8,128)(2,1)S(1)}, bf16[64,512]{1,0:T(8,128)(2,1)S(1)}, u32[]{:S(2)}, u32[]{:S(2)}) %collective-permute-start.17) | collective-permute-done | bytes 65568 | tf_op jit(solution)/shard_map/ppermute | solution.py:28
  49.1 1.1 %collective-permute-done.20 = bf16[64,512]{1,0:T(8,128)(2,1)S(1)} collective-permute-done((bf16[64,512]{1,0:T(8,128)(2,1)S(1)}, bf16[64,512]{1,0:T(8,128)(2,1)S(1)}, u32[]{:S(2)}, u32[]{:S(2)}) %collective-permute-start.20) | collective-permute-done | bytes 65568 | tf_op jit(solution)/shard_map/ppermute | solution.py:28
  50.2 1.7 %collective-permute-start.21 = (bf16[16,512]{1,0:T(8,128)(2,1)S(1)}, bf16[16,512]{1,0:T(8,128)(2,1)S(1)}, u32[]{:S(2)}, u32[]{:S(2)}) collective-permute-start(bf16[16,512]{1,0:T(8,128)(2,1)S(1)} %get-tuple-element.13), channel_id=1, source_target_pairs={{0,24},{1,29},{2,26},{3,31},{4,28},{5,25},{6,30},{7,27},{8,0},{9,5... | collective-permute-start | bytes 49160 | tf_op jit(solution)/shard_map/ppermute | solution.py:28
  52.2 2.4 %collective-permute-start.19 = (bf16[8,512]{1,0:T(8,128)(2,1)S(1)}, bf16[8,512]{1,0:T(8,128)(2,1)S(1)}, u32[]{:S(2)}, u32[]{:S(2)}) collective-permute-start(bf16[8,512]{1,0:T(8,128)(2,1)S(1)} %constant_dynamic-slice_fusion), channel_id=1, source_target_pairs={{0,24},{1,25},{2,26},{3,27},{4,28},{5,29},{6,30},{7,31},{8,0},{9,1... | collective-permute-start | bytes 24584 | tf_op jit(solution)/shard_map/ppermute | solution.py:28
  54.6 2.0 %collective-permute-done.22 = bf16[16,512]{1,0:T(8,128)(2,1)S(1)} collective-permute-done((bf16[16,512]{1,0:T(8,128)(2,1)S(1)}, bf16[16,512]{1,0:T(8,128)(2,1)S(1)}, u32[]{:S(2)}, u32[]{:S(2)}) %collective-permute-start.22) | collective-permute-done | bytes 16416 | tf_op jit(solution)/shard_map/ppermute | solution.py:28
  56.8 1.4 %subtract_convert_fusion = bf16[1024,512]{1,0:T(8,128)(2,1)} fusion(bf16[1024,512]{1,0:T(8,128)(2,1)S(1)} %subtract_convert_fusion.1, bf16[1024,64]{0,1:T(8,128)(2,1)S(1)} %fusion.11, bf16[64,512]{1,0:T(8,128)(2,1)S(1)} %subtract_convert_fusion.4), kind=kOutput, calls=%fused_computation | convolution fusion | flops 69206016 | bytes 2293760 | tf_op jit(solution)/shard_map/dot_general | solution.py:109
  (66 shorter events, 10.0 us)
Async XLA Ops:
  1.4 1.3 %collective-permute-start = (bf16[8,512]{1,0:T(8,128)(2,1)S(1)}, bf16[8,512]{1,0:T(8,128)(2,1)S(1)}, u32[]{:S(2)}, u32[]{:S(2)}) collective-permute-start(bf16[8,512]{1,0:T(8,128)(2,1)S(1)} %convert_element_type.174), channel_id=1, source_target_pairs={{0,1},{1,0},{2,3},{3,2},{4,5},{5,4},{6,7},{7,6},{8,9},{9,8},{10,11... | collective-permute-start | bytes 24584 | tf_op jit(solution)/shard_map/ppermute | solution.py:28
  2.7 7.8 %collective-permute-start.1 = (bf16[16,512]{1,0:T(8,128)(2,1)S(1)}, bf16[16,512]{1,0:T(8,128)(2,1)S(1)}, u32[]{:S(2)}, u32[]{:S(2)}) collective-permute-start(bf16[16,512]{1,0:T(8,128)(2,1)S(1)} %pad_maximum_fusion.3), channel_id=1, source_target_pairs={{0,2},{1,3},{2,0},{3,1},{4,6},{5,7},{6,4},{7,5},{8,10},{9,11},{10,... | collective-permute-start | bytes 49160 | tf_op jit(solution)/shard_map/ppermute | solution.py:28
  5.7 4.9 %collective-permute-start.2 = (bf16[16,512]{1,0:T(8,128)(2,1)S(1)}, bf16[16,512]{1,0:T(8,128)(2,1)S(1)}, u32[]{:S(2)}, u32[]{:S(2)}) collective-permute-start(bf16[16,512]{1,0:T(8,128)(2,1)S(1)} %pad_maximum_fusion.3), channel_id=1, source_target_pairs={{0,4},{1,5},{2,6},{3,7},{4,0},{5,1},{6,2},{7,3},{8,12},{9,13},{10,... | collective-permute-start | bytes 49160 | tf_op jit(solution)/shard_map/ppermute | solution.py:28
  8.2 5.5 %collective-permute-start.3 = (bf16[16,512]{1,0:T(8,128)(2,1)S(1)}, bf16[16,512]{1,0:T(8,128)(2,1)S(1)}, u32[]{:S(2)}, u32[]{:S(2)}) collective-permute-start(bf16[16,512]{1,0:T(8,128)(2,1)S(1)} %pad_maximum_fusion.3), channel_id=1, source_target_pairs={{0,6},{1,7},{2,4},{3,5},{4,2},{5,3},{6,0},{7,1},{8,14},{9,15},{10,... | collective-permute-start | bytes 49160 | tf_op jit(solution)/shard_map/ppermute | solution.py:28
  14.6 1.3 %collective-permute-start.5 = (bf16[64,512]{1,0:T(8,128)(2,1)S(1)}, bf16[64,512]{1,0:T(8,128)(2,1)S(1)}, u32[]{:S(2)}, u32[]{:S(2)}) collective-permute-start(bf16[64,512]{1,0:T(8,128)(2,1)S(1)} %get-tuple-element.23), channel_id=1, source_target_pairs={{0,1},{1,0},{2,3},{3,2},{4,5},{5,4},{6,7},{7,6},{8,9},{9,8},{10,11... | collective-permute-start | bytes 196616 | tf_op jit(solution)/shard_map/ppermute | solution.py:28
  15.9 4.5 %collective-permute-start.6 = (bf16[64,512]{1,0:T(8,128)(2,1)S(1)}, bf16[64,512]{1,0:T(8,128)(2,1)S(1)}, u32[]{:S(2)}, u32[]{:S(2)}) collective-permute-start(bf16[64,512]{1,0:T(8,128)(2,1)S(1)} %add_convert_fusion.6), channel_id=1, source_target_pairs={{0,24},{1,29},{2,26},{3,31},{4,28},{5,25},{6,30},{7,27},{8,0},{9,5... | collective-permute-start | bytes 196616 | tf_op jit(solution)/shard_map/ppermute | solution.py:28
  18.4 5.2 %collective-permute-start.7 = (bf16[64,512]{1,0:T(8,128)(2,1)S(1)}, bf16[64,512]{1,0:T(8,128)(2,1)S(1)}, u32[]{:S(2)}, u32[]{:S(2)}) collective-permute-start(bf16[64,512]{1,0:T(8,128)(2,1)S(1)} %add_convert_fusion.6), channel_id=1, source_target_pairs={{0,26},{1,31},{2,24},{3,29},{4,30},{5,27},{6,28},{7,25},{8,2},{9,7... | collective-permute-start | bytes 196616 | tf_op jit(solution)/shard_map/ppermute | solution.py:28
  18.4 5.8 %collective-permute-start.4 = (bf16[64,512]{1,0:T(8,128)(2,1)S(1)}, bf16[64,512]{1,0:T(8,128)(2,1)S(1)}, u32[]{:S(2)}, u32[]{:S(2)}) collective-permute-start(bf16[64,512]{1,0:T(8,128)(2,1)S(1)} %pad_maximum_fusion), channel_id=1, source_target_pairs={{0,24},{1,25},{2,26},{3,27},{4,28},{5,29},{6,30},{7,31},{8,0},{9,1... | collective-permute-start | bytes 196616 | tf_op jit(solution)/shard_map/ppermute | solution.py:28
  23.7 1.3 %collective-permute-start.8 = (bf16[64,512]{1,0:T(8,128)(2,1)S(1)}, bf16[64,512]{1,0:T(8,128)(2,1)S(1)}, u32[]{:S(2)}, u32[]{:S(2)}) collective-permute-start(bf16[64,512]{1,0:T(8,128)(2,1)S(1)} %add_convert_fusion.5), channel_id=1, source_target_pairs={{0,1},{1,0},{2,3},{3,2},{4,5},{5,4},{6,7},{7,6},{8,9},{9,8},{10,11... | collective-permute-start | bytes 196616 | tf_op jit(solution)/shard_map/ppermute | solution.py:28
  25.8 1.3 %collective-permute-start.10 = (bf16[64,512]{1,0:T(8,128)(2,1)S(1)}, bf16[64,512]{1,0:T(8,128)(2,1)S(1)}, u32[]{:S(2)}, u32[]{:S(2)}) collective-permute-start(bf16[64,512]{1,0:T(8,128)(2,1)S(1)} %get-tuple-element.25), channel_id=1, source_target_pairs={{0,1},{1,0},{2,3},{3,2},{4,5},{5,4},{6,7},{7,6},{8,9},{9,8},{10,11... | collective-permute-start | bytes 196616 | tf_op jit(solution)/shard_map/ppermute | solution.py:28
  27.1 4.7 %collective-permute-start.11 = (bf16[64,512]{1,0:T(8,128)(2,1)S(1)}, bf16[64,512]{1,0:T(8,128)(2,1)S(1)}, u32[]{:S(2)}, u32[]{:S(2)}) collective-permute-start(bf16[64,512]{1,0:T(8,128)(2,1)S(1)} %add_convert_fusion.4), channel_id=1, source_target_pairs={{0,24},{1,29},{2,26},{3,31},{4,28},{5,25},{6,30},{7,27},{8,0},{9,5... | collective-permute-start | bytes 196616 | tf_op jit(solution)/shard_map/ppermute | solution.py:28
  29.6 6.0 %collective-permute-start.12 = (bf16[64,512]{1,0:T(8,128)(2,1)S(1)}, bf16[64,512]{1,0:T(8,128)(2,1)S(1)}, u32[]{:S(2)}, u32[]{:S(2)}) collective-permute-start(bf16[64,512]{1,0:T(8,128)(2,1)S(1)} %add_convert_fusion.4), channel_id=1, source_target_pairs={{0,26},{1,31},{2,24},{3,29},{4,30},{5,27},{6,28},{7,25},{8,2},{9,7... | collective-permute-start | bytes 196616 | tf_op jit(solution)/shard_map/ppermute | solution.py:28
  29.6 6.5 %collective-permute-start.9 = (bf16[64,512]{1,0:T(8,128)(2,1)S(1)}, bf16[64,512]{1,0:T(8,128)(2,1)S(1)}, u32[]{:S(2)}, u32[]{:S(2)}) collective-permute-start(bf16[64,512]{1,0:T(8,128)(2,1)S(1)} %subtract_convert_fusion.6), channel_id=1, source_target_pairs={{0,24},{1,25},{2,26},{3,27},{4,28},{5,29},{6,30},{7,31},{8,0},{9,1... | collective-permute-start | bytes 196616 | tf_op jit(solution)/shard_map/ppermute | solution.py:28
  35.6 1.3 %collective-permute-start.13 = (bf16[64,512]{1,0:T(8,128)(2,1)S(1)}, bf16[64,512]{1,0:T(8,128)(2,1)S(1)}, u32[]{:S(2)}, u32[]{:S(2)}) collective-permute-start(bf16[64,512]{1,0:T(8,128)(2,1)S(1)} %add_convert_fusion.3), channel_id=1, source_target_pairs={{0,1},{1,0},{2,3},{3,2},{4,5},{5,4},{6,7},{7,6},{8,9},{9,8},{10,11... | collective-permute-start | bytes 196616 | tf_op jit(solution)/shard_map/ppermute | solution.py:28
  37.7 1.3 %collective-permute-start.15 = (bf16[64,512]{1,0:T(8,128)(2,1)S(1)}, bf16[64,512]{1,0:T(8,128)(2,1)S(1)}, u32[]{:S(2)}, u32[]{:S(2)}) collective-permute-start(bf16[64,512]{1,0:T(8,128)(2,1)S(1)} %get-tuple-element.27), channel_id=1, source_target_pairs={{0,1},{1,0},{2,3},{3,2},{4,5},{5,4},{6,7},{7,6},{8,9},{9,8},{10,11... | collective-permute-start | bytes 196616 | tf_op jit(solution)/shard_map/ppermute | solution.py:28
  39.1 4.4 %collective-permute-start.16 = (bf16[64,512]{1,0:T(8,128)(2,1)S(1)}, bf16[64,512]{1,0:T(8,128)(2,1)S(1)}, u32[]{:S(2)}, u32[]{:S(2)}) collective-permute-start(bf16[64,512]{1,0:T(8,128)(2,1)S(1)} %add_convert_fusion.2), channel_id=1, source_target_pairs={{0,24},{1,29},{2,26},{3,31},{4,28},{5,25},{6,30},{7,27},{8,0},{9,5... | collective-permute-start | bytes 196616 | tf_op jit(solution)/shard_map/ppermute | solution.py:28
  40.8 6.0 %collective-permute-start.17 = (bf16[64,512]{1,0:T(8,128)(2,1)S(1)}, bf16[64,512]{1,0:T(8,128)(2,1)S(1)}, u32[]{:S(2)}, u32[]{:S(2)}) collective-permute-start(bf16[64,512]{1,0:T(8,128)(2,1)S(1)} %add_convert_fusion.2), channel_id=1, source_target_pairs={{0,26},{1,31},{2,24},{3,29},{4,30},{5,27},{6,28},{7,25},{8,2},{9,7... | collective-permute-start | bytes 196616 | tf_op jit(solution)/shard_map/ppermute | solution.py:28
  40.8 6.5 %collective-permute-start.14 = (bf16[64,512]{1,0:T(8,128)(2,1)S(1)}, bf16[64,512]{1,0:T(8,128)(2,1)S(1)}, u32[]{:S(2)}, u32[]{:S(2)}) collective-permute-start(bf16[64,512]{1,0:T(8,128)(2,1)S(1)} %subtract_convert_fusion.5), channel_id=1, source_target_pairs={{0,24},{1,25},{2,26},{3,27},{4,28},{5,29},{6,30},{7,31},{8,0},{9,1... | collective-permute-start | bytes 196616 | tf_op jit(solution)/shard_map/ppermute | solution.py:28
  46.8 1.3 %collective-permute-start.18 = (bf16[64,512]{1,0:T(8,128)(2,1)S(1)}, bf16[64,512]{1,0:T(8,128)(2,1)S(1)}, u32[]{:S(2)}, u32[]{:S(2)}) collective-permute-start(bf16[64,512]{1,0:T(8,128)(2,1)S(1)} %add_convert_fusion.1), channel_id=1, source_target_pairs={{0,1},{1,0},{2,3},{3,2},{4,5},{5,4},{6,7},{7,6},{8,9},{9,8},{10,11... | collective-permute-start | bytes 196616 | tf_op jit(solution)/shard_map/ppermute | solution.py:28
  48.9 1.3 %collective-permute-start.20 = (bf16[64,512]{1,0:T(8,128)(2,1)S(1)}, bf16[64,512]{1,0:T(8,128)(2,1)S(1)}, u32[]{:S(2)}, u32[]{:S(2)}) collective-permute-start(bf16[64,512]{1,0:T(8,128)(2,1)S(1)} %get-tuple-element.29), channel_id=1, source_target_pairs={{0,1},{1,0},{2,3},{3,2},{4,5},{5,4},{6,7},{7,6},{8,9},{9,8},{10,11... | collective-permute-start | bytes 196616 | tf_op jit(solution)/shard_map/ppermute | solution.py:28
  50.2 4.4 %collective-permute-start.21 = (bf16[16,512]{1,0:T(8,128)(2,1)S(1)}, bf16[16,512]{1,0:T(8,128)(2,1)S(1)}, u32[]{:S(2)}, u32[]{:S(2)}) collective-permute-start(bf16[16,512]{1,0:T(8,128)(2,1)S(1)} %get-tuple-element.13), channel_id=1, source_target_pairs={{0,24},{1,29},{2,26},{3,31},{4,28},{5,25},{6,30},{7,27},{8,0},{9,5... | collective-permute-start | bytes 49160 | tf_op jit(solution)/shard_map/ppermute | solution.py:28
  52.0 4.6 %collective-permute-start.22 = (bf16[16,512]{1,0:T(8,128)(2,1)S(1)}, bf16[16,512]{1,0:T(8,128)(2,1)S(1)}, u32[]{:S(2)}, u32[]{:S(2)}) collective-permute-start(bf16[16,512]{1,0:T(8,128)(2,1)S(1)} %get-tuple-element.14), channel_id=1, source_target_pairs={{0,26},{1,31},{2,24},{3,29},{4,30},{5,27},{6,28},{7,25},{8,2},{9,7... | collective-permute-start | bytes 49160 | tf_op jit(solution)/shard_map/ppermute | solution.py:28
  52.2 6.0 %collective-permute-start.19 = (bf16[8,512]{1,0:T(8,128)(2,1)S(1)}, bf16[8,512]{1,0:T(8,128)(2,1)S(1)}, u32[]{:S(2)}, u32[]{:S(2)}) collective-permute-start(bf16[8,512]{1,0:T(8,128)(2,1)S(1)} %constant_dynamic-slice_fusion), channel_id=1, source_target_pairs={{0,24},{1,25},{2,26},{3,27},{4,28},{5,29},{6,30},{7,31},{8,0},{9,1... | collective-permute-start | bytes 24584 | tf_op jit(solution)/shard_map/ppermute | solution.py:28
  56.6 1.6 %collective-permute-start.23 = (bf16[8,512]{1,0:T(8,128)(2,1)S(1)}, bf16[8,512]{1,0:T(8,128)(2,1)S(1)}, u32[]{:S(2)}, u32[]{:S(2)}) collective-permute-start(bf16[8,512]{1,0:T(8,128)(2,1)S(1)} %dynamic-slice_convert_fusion), channel_id=1, source_target_pairs={{0,1},{1,0},{2,3},{3,2},{4,5},{5,4},{6,7},{7,6},{8,9},{9,8},{10,11... | collective-permute-start | bytes 24584 | tf_op jit(solution)/shard_map/ppermute | solution.py:28
  (2 other events, 2.7 us)

commit v4 on v3

--- a/solution.py
+++ b/solution.py
@@ -62,9 +62,14 @@
     while bit < top // 2:
         block = in_order(block, swap(block, bit), me // bit % 2)
         bit *= 2
-    near = swap(block, bit)
-    far = swap(block, top)
-    cross = swap(block, bit + top)
+    got = route(block, lambda s, u: (s, u ^ (top if u % 2 else bit)))
+    more = route(block, lambda s, u: (s, u ^ (bit + top if u % 2 else bit)))
+    both = jnp.concatenate([got, more], axis=0)
+    other = swap(both, 1)
+    rows = block.shape[0]
+    near = jnp.where(core == 0, got, other[:rows])
+    far = jnp.where(core == 0, other[:rows], got)
+    cross = jnp.where(core == 0, other[rows:], more)
     side, end = me // bit % 2, me // top
     whole = in_order(in_order(block, near, side), in_order(far, cross, side), end)
     whole = lax.optimization_barrier(whole)

time: 59.1 us -> 58.6 us (level)
  starting transfers between devices: 23.6 us -> 27.3 us
  waiting for transfers between devices: 24.6 us -> 21.5 us
  local copies, waits for them, and re-layouts: 0.93 us -> 0.03 us
    ppermute x24, starting transfers between devices: 23.6 us -> 27.3 us  [route(): return lax.ppermute(block, AXES, pairs)]
    ppermute x24, waiting for transfers between devices: 24.6 us -> 21.5 us  [route(): return lax.ppermute(block, AXES, pairs)]
    squeeze x1, local copies, waits for them, and re-layouts: 0.91 us -> 0.01 us  [local(): tiles[0] = lax.optimization_barrier(shown[:, 0, :])]
  transfers between devices with their start and end apart: 24 -> 24, of which waited for: 14 -> 18; matrix products, arithmetic and copies ran while one was open for 9% -> 7% of each run, Pallas kernels for 0% -> 0%
where the time goes in v4:
time: 58.6 us; the launch traced here: 58.3 us
  starting transfers between devices  27.3 us (47%)
  waiting for transfers between devices  21.5 us (37%)
  matrix products  5.78 us (10%)
  other arithmetic  2.93 us (5%)
  between operations  0.82 us (1%)
    ppermute x24, starting transfers between devices, route(): return lax.ppermute(block, AXES, pairs)  27.3 us
    ppermute x24, waiting for transfers between devices, route(): return lax.ppermute(block, AXES, pairs)  21.5 us
    dot_general x4, matrix products, local(): change = jnp.dot(resid, whole, preferred_element_type=jnp.float32)  2.8 us
    dot_general x4, matrix products, local(): lax.dot_general(users, whole, (((1,), (1,)), ((), ())), preferred_element...  1.77 us
    mul x1, other arithmetic, local(): users = lax.optimization_barrier(users * one)  1.29 us
    dot_general x4, matrix products, local(): lax.dot_general(resid, users, (((0,), (0,)), ((), ())), preferred_element...  1.21 us
  transfers between devices with their start and end apart: 24, of which 18 were waited for; matrix products, arithmetic and copies ran while one was open for 7% of the time, Pallas kernels for 0%

profile of v4, /device:TPU:0, one launch (start us, length us, event | category | flops | bytes accessed | tf_op | source)
XLA Modules:
  0.0 58.3 jit_solution(10777616493189626423)
XLA Ops:
  2.7 3.0 %collective-permute-start.1 = (bf16[16,512]{1,0:T(8,128)(2,1)S(1)}, bf16[16,512]{1,0:T(8,128)(2,1)S(1)}, u32[]{:S(2)}, u32[]{:S(2)}) collective-permute-start(bf16[16,512]{1,0:T(8,128)(2,1)S(1)} %pad_maximum_fusion.4), channel_id=1, source_target_pairs={{0,2},{1,5},{2,0},{3,7},{4,6},{5,1},{6,4},{7,3},{8,10},{9,13},{10,... | collective-permute-start | bytes 49160 | tf_op jit(solution)/shard_map/ppermute | solution.py:28
  5.8 1.3 %broadcast_multiply_fusion = bf16[1024,512]{1,0:T(8,128)(2,1)S(1)} fusion(bf16[1024,512]{1,0:T(8,128)(2,1)} %param.4, bf16[]{:T(256)} %constant.64.clone.1), kind=kLoop, calls=%fused_computation.25 | loop fusion | flops 524288 | bytes 2097154 | tf_op jit(solution)/shard_map/mul | solution.py:60
  7.4 2.0 %collective-permute-done.2 = bf16[16,512]{1,0:T(8,128)(2,1)S(1)} collective-permute-done((bf16[16,512]{1,0:T(8,128)(2,1)S(1)}, bf16[16,512]{1,0:T(8,128)(2,1)S(1)}, u32[]{:S(2)}, u32[]{:S(2)}) %collective-permute-start.2) | collective-permute-done | bytes 16416 | tf_op jit(solution)/shard_map/ppermute | solution.py:28
  9.4 1.5 %collective-permute-start.3 = (bf16[32,512]{1,0:T(8,128)(2,1)S(1)}, bf16[32,512]{1,0:T(8,128)(2,1)S(1)}, u32[]{:S(2)}, u32[]{:S(2)}) collective-permute-start(bf16[32,512]{1,0:T(8,128)(2,1)S(1)} %pad_maximum_fusion.1), channel_id=1, source_target_pairs={{0,1},{1,0},{2,3},{3,2},{4,5},{5,4},{6,7},{7,6},{8,9},{9,8},{10,11... | collective-permute-start | bytes 98312 | tf_op jit(solution)/shard_map/ppermute | solution.py:28
  13.0 0.9 %collective-permute-done.5 = bf16[64,512]{1,0:T(8,128)(2,1)S(1)} collective-permute-done((bf16[64,512]{1,0:T(8,128)(2,1)S(1)}, bf16[64,512]{1,0:T(8,128)(2,1)S(1)}, u32[]{:S(2)}, u32[]{:S(2)}) %collective-permute-start.5) | collective-permute-done | bytes 65568 | tf_op jit(solution)/shard_map/ppermute | solution.py:28
  14.0 2.5 %collective-permute-start.6 = (bf16[64,512]{1,0:T(8,128)(2,1)S(1)}, bf16[64,512]{1,0:T(8,128)(2,1)S(1)}, u32[]{:S(2)}, u32[]{:S(2)}) collective-permute-start(bf16[64,512]{1,0:T(8,128)(2,1)S(1)} %add_convert_fusion.6), channel_id=1, source_target_pairs={{0,24},{1,29},{2,26},{3,31},{4,28},{5,25},{6,30},{7,27},{8,0},{9,5... | collective-permute-start | bytes 196616 | tf_op jit(solution)/shard_map/ppermute | solution.py:28
  16.5 1.2 %collective-permute-start.4 = (bf16[64,512]{1,0:T(8,128)(2,1)S(1)}, bf16[64,512]{1,0:T(8,128)(2,1)S(1)}, u32[]{:S(2)}, u32[]{:S(2)}) collective-permute-start(bf16[64,512]{1,0:T(8,128)(2,1)S(1)} %pad_maximum_fusion), channel_id=1, source_target_pairs={{0,24},{1,25},{2,26},{3,27},{4,28},{5,29},{6,30},{7,31},{8,0},{9,1... | collective-permute-start | bytes 196616 | tf_op jit(solution)/shard_map/ppermute | solution.py:28
  18.4 3.4 %collective-permute-done.7 = bf16[64,512]{1,0:T(8,128)(2,1)S(1)} collective-permute-done((bf16[64,512]{1,0:T(8,128)(2,1)S(1)}, bf16[64,512]{1,0:T(8,128)(2,1)S(1)}, u32[]{:S(2)}, u32[]{:S(2)}) %collective-permute-start.7) | collective-permute-done | bytes 65568 | tf_op jit(solution)/shard_map/ppermute | solution.py:28
  21.8 1.3 %collective-permute-start.8 = (bf16[64,512]{1,0:T(8,128)(2,1)S(1)}, bf16[64,512]{1,0:T(8,128)(2,1)S(1)}, u32[]{:S(2)}, u32[]{:S(2)}) collective-permute-start(bf16[64,512]{1,0:T(8,128)(2,1)S(1)} %add_convert_fusion.5), channel_id=1, source_target_pairs={{0,1},{1,0},{2,3},{3,2},{4,5},{5,4},{6,7},{7,6},{8,9},{9,8},{10,11... | collective-permute-start | bytes 196616 | tf_op jit(solution)/shard_map/ppermute | solution.py:28
  25.2 0.9 %collective-permute-done.10 = bf16[64,512]{1,0:T(8,128)(2,1)S(1)} collective-permute-done((bf16[64,512]{1,0:T(8,128)(2,1)S(1)}, bf16[64,512]{1,0:T(8,128)(2,1)S(1)}, u32[]{:S(2)}, u32[]{:S(2)}) %collective-permute-start.10) | collective-permute-done | bytes 65568 | tf_op jit(solution)/shard_map/ppermute | solution.py:28
  26.1 1.6 %collective-permute-start.11 = (bf16[64,512]{1,0:T(8,128)(2,1)S(1)}, bf16[64,512]{1,0:T(8,128)(2,1)S(1)}, u32[]{:S(2)}, u32[]{:S(2)}) collective-permute-start(bf16[64,512]{1,0:T(8,128)(2,1)S(1)} %add_convert_fusion.4), channel_id=1, source_target_pairs={{0,24},{1,29},{2,26},{3,31},{4,28},{5,25},{6,30},{7,27},{8,0},{9,5... | collective-permute-start | bytes 196616 | tf_op jit(solution)/shard_map/ppermute | solution.py:28
  27.7 2.3 %collective-permute-start.9 = (bf16[64,512]{1,0:T(8,128)(2,1)S(1)}, bf16[64,512]{1,0:T(8,128)(2,1)S(1)}, u32[]{:S(2)}, u32[]{:S(2)}) collective-permute-start(bf16[64,512]{1,0:T(8,128)(2,1)S(1)} %subtract_convert_fusion.6), channel_id=1, source_target_pairs={{0,24},{1,25},{2,26},{3,27},{4,28},{5,29},{6,30},{7,31},{8,0},{9,1... | collective-permute-start | bytes 196616 | tf_op jit(solution)/shard_map/ppermute | solution.py:28
  30.4 2.6 %collective-permute-done.12 = bf16[64,512]{1,0:T(8,128)(2,1)S(1)} collective-permute-done((bf16[64,512]{1,0:T(8,128)(2,1)S(1)}, bf16[64,512]{1,0:T(8,128)(2,1)S(1)}, u32[]{:S(2)}, u32[]{:S(2)}) %collective-permute-start.12) | collective-permute-done | bytes 65568 | tf_op jit(solution)/shard_map/ppermute | solution.py:28
  33.0 1.4 %collective-permute-start.13 = (bf16[64,512]{1,0:T(8,128)(2,1)S(1)}, bf16[64,512]{1,0:T(8,128)(2,1)S(1)}, u32[]{:S(2)}, u32[]{:S(2)}) collective-permute-start(bf16[64,512]{1,0:T(8,128)(2,1)S(1)} %add_convert_fusion.3), channel_id=1, source_target_pairs={{0,1},{1,0},{2,3},{3,2},{4,5},{5,4},{6,7},{7,6},{8,9},{9,8},{10,11... | collective-permute-start | bytes 196616 | tf_op jit(solution)/shard_map/ppermute | solution.py:28
  36.6 0.9 %collective-permute-done.15 = bf16[64,512]{1,0:T(8,128)(2,1)S(1)} collective-permute-done((bf16[64,512]{1,0:T(8,128)(2,1)S(1)}, bf16[64,512]{1,0:T(8,128)(2,1)S(1)}, u32[]{:S(2)}, u32[]{:S(2)}) %collective-permute-start.15) | collective-permute-done | bytes 65568 | tf_op jit(solution)/shard_map/ppermute | solution.py:28
  37.5 1.6 %collective-permute-start.16 = (bf16[64,512]{1,0:T(8,128)(2,1)S(1)}, bf16[64,512]{1,0:T(8,128)(2,1)S(1)}, u32[]{:S(2)}, u32[]{:S(2)}) collective-permute-start(bf16[64,512]{1,0:T(8,128)(2,1)S(1)} %add_convert_fusion.2), channel_id=1, source_target_pairs={{0,24},{1,29},{2,26},{3,31},{4,28},{5,25},{6,30},{7,27},{8,0},{9,5... | collective-permute-start | bytes 196616 | tf_op jit(solution)/shard_map/ppermute | solution.py:28
  39.5 1.8 %collective-permute-start.14 = (bf16[64,512]{1,0:T(8,128)(2,1)S(1)}, bf16[64,512]{1,0:T(8,128)(2,1)S(1)}, u32[]{:S(2)}, u32[]{:S(2)}) collective-permute-start(bf16[64,512]{1,0:T(8,128)(2,1)S(1)} %subtract_convert_fusion.5), channel_id=1, source_target_pairs={{0,24},{1,25},{2,26},{3,27},{4,28},{5,29},{6,30},{7,31},{8,0},{9,1... | collective-permute-start | bytes 196616 | tf_op jit(solution)/shard_map/ppermute | solution.py:28
  41.8 2.6 %collective-permute-done.17 = bf16[64,512]{1,0:T(8,128)(2,1)S(1)} collective-permute-done((bf16[64,512]{1,0:T(8,128)(2,1)S(1)}, bf16[64,512]{1,0:T(8,128)(2,1)S(1)}, u32[]{:S(2)}, u32[]{:S(2)}) %collective-permute-start.17) | collective-permute-done | bytes 65568 | tf_op jit(solution)/shard_map/ppermute | solution.py:28
  44.4 1.3 %collective-permute-start.18 = (bf16[64,512]{1,0:T(8,128)(2,1)S(1)}, bf16[64,512]{1,0:T(8,128)(2,1)S(1)}, u32[]{:S(2)}, u32[]{:S(2)}) collective-permute-start(bf16[64,512]{1,0:T(8,128)(2,1)S(1)} %add_convert_fusion.1), channel_id=1, source_target_pairs={{0,1},{1,0},{2,3},{3,2},{4,5},{5,4},{6,7},{7,6},{8,9},{9,8},{10,11... | collective-permute-start | bytes 196616 | tf_op jit(solution)/shard_map/ppermute | solution.py:28
  48.7 1.7 %collective-permute-start.21 = (bf16[16,512]{1,0:T(8,128)(2,1)S(1)}, bf16[16,512]{1,0:T(8,128)(2,1)S(1)}, u32[]{:S(2)}, u32[]{:S(2)}) collective-permute-start(bf16[16,512]{1,0:T(8,128)(2,1)S(1)} %get-tuple-element.13), channel_id=1, source_target_pairs={{0,24},{1,29},{2,26},{3,31},{4,28},{5,25},{6,30},{7,27},{8,0},{9,5... | collective-permute-start | bytes 49160 | tf_op jit(solution)/shard_map/ppermute | solution.py:28
  50.8 1.8 %collective-permute-start.19 = (bf16[8,512]{1,0:T(8,128)(2,1)S(1)}, bf16[8,512]{1,0:T(8,128)(2,1)S(1)}, u32[]{:S(2)}, u32[]{:S(2)}) collective-permute-start(bf16[8,512]{1,0:T(8,128)(2,1)S(1)} %constant_dynamic-slice_fusion), channel_id=1, source_target_pairs={{0,24},{1,25},{2,26},{3,27},{4,28},{5,29},{6,30},{7,31},{8,0},{9,1... | collective-permute-start | bytes 24584 | tf_op jit(solution)/shard_map/ppermute | solution.py:28
  52.6 2.4 %collective-permute-done.22 = bf16[16,512]{1,0:T(8,128)(2,1)S(1)} collective-permute-done((bf16[16,512]{1,0:T(8,128)(2,1)S(1)}, bf16[16,512]{1,0:T(8,128)(2,1)S(1)}, u32[]{:S(2)}, u32[]{:S(2)}) %collective-permute-start.22) | collective-permute-done | bytes 16416 | tf_op jit(solution)/shard_map/ppermute | solution.py:28
  55.1 1.2 %collective-permute-start.23 = (bf16[8,512]{1,0:T(8,128)(2,1)S(1)}, bf16[8,512]{1,0:T(8,128)(2,1)S(1)}, u32[]{:S(2)}, u32[]{:S(2)}) collective-permute-start(bf16[8,512]{1,0:T(8,128)(2,1)S(1)} %dynamic-slice_convert_fusion), channel_id=1, source_target_pairs={{0,1},{1,0},{2,3},{3,2},{4,5},{5,4},{6,7},{7,6},{8,9},{9,8},{10,11... | collective-permute-start | bytes 24584 | tf_op jit(solution)/shard_map/ppermute | solution.py:28
  56.3 1.4 %subtract_convert_fusion = bf16[1024,512]{1,0:T(8,128)(2,1)} fusion(bf16[1024,512]{1,0:T(8,128)(2,1)S(1)} %subtract_convert_fusion.1, bf16[1024,64]{0,1:T(8,128)(2,1)S(1)} %fusion.11, bf16[64,512]{1,0:T(8,128)(2,1)S(1)} %subtract_convert_fusion.4), kind=kOutput, calls=%fused_computation | convolution fusion | flops 69206016 | bytes 2293760 | tf_op jit(solution)/shard_map/dot_general | solution.py:114
  (66 shorter events, 14.8 us)
Async XLA Ops:
  1.4 1.3 %collective-permute-start = (bf16[8,512]{1,0:T(8,128)(2,1)S(1)}, bf16[8,512]{1,0:T(8,128)(2,1)S(1)}, u32[]{:S(2)}, u32[]{:S(2)}) collective-permute-start(bf16[8,512]{1,0:T(8,128)(2,1)S(1)} %convert_element_type.174), channel_id=1, source_target_pairs={{0,1},{1,0},{2,3},{3,2},{4,5},{5,4},{6,7},{7,6},{8,9},{9,8},{10,11... | collective-permute-start | bytes 24584 | tf_op jit(solution)/shard_map/ppermute | solution.py:28
  2.7 4.7 %collective-permute-start.1 = (bf16[16,512]{1,0:T(8,128)(2,1)S(1)}, bf16[16,512]{1,0:T(8,128)(2,1)S(1)}, u32[]{:S(2)}, u32[]{:S(2)}) collective-permute-start(bf16[16,512]{1,0:T(8,128)(2,1)S(1)} %pad_maximum_fusion.4), channel_id=1, source_target_pairs={{0,2},{1,5},{2,0},{3,7},{4,6},{5,1},{6,4},{7,3},{8,10},{9,13},{10,... | collective-permute-start | bytes 49160 | tf_op jit(solution)/shard_map/ppermute | solution.py:28
  5.7 3.7 %collective-permute-start.2 = (bf16[16,512]{1,0:T(8,128)(2,1)S(1)}, bf16[16,512]{1,0:T(8,128)(2,1)S(1)}, u32[]{:S(2)}, u32[]{:S(2)}) collective-permute-start(bf16[16,512]{1,0:T(8,128)(2,1)S(1)} %pad_maximum_fusion.4), channel_id=1, source_target_pairs={{0,2},{1,7},{2,0},{3,5},{4,6},{5,3},{6,4},{7,1},{8,10},{9,15},{10,... | collective-permute-start | bytes 49160 | tf_op jit(solution)/shard_map/ppermute | solution.py:28
  9.4 2.4 %collective-permute-start.3 = (bf16[32,512]{1,0:T(8,128)(2,1)S(1)}, bf16[32,512]{1,0:T(8,128)(2,1)S(1)}, u32[]{:S(2)}, u32[]{:S(2)}) collective-permute-start(bf16[32,512]{1,0:T(8,128)(2,1)S(1)} %pad_maximum_fusion.1), channel_id=1, source_target_pairs={{0,1},{1,0},{2,3},{3,2},{4,5},{5,4},{6,7},{7,6},{8,9},{9,8},{10,11... | collective-permute-start | bytes 98312 | tf_op jit(solution)/shard_map/ppermute | solution.py:28
  12.6 1.3 %collective-permute-start.5 = (bf16[64,512]{1,0:T(8,128)(2,1)S(1)}, bf16[64,512]{1,0:T(8,128)(2,1)S(1)}, u32[]{:S(2)}, u32[]{:S(2)}) collective-permute-start(bf16[64,512]{1,0:T(8,128)(2,1)S(1)} %get-tuple-element.25), channel_id=1, source_target_pairs={{0,1},{1,0},{2,3},{3,2},{4,5},{5,4},{6,7},{7,6},{8,9},{9,8},{10,11... | collective-permute-start | bytes 196616 | tf_op jit(solution)/shard_map/ppermute | solution.py:28
  14.0 4.4 %collective-permute-start.6 = (bf16[64,512]{1,0:T(8,128)(2,1)S(1)}, bf16[64,512]{1,0:T(8,128)(2,1)S(1)}, u32[]{:S(2)}, u32[]{:S(2)}) collective-permute-start(bf16[64,512]{1,0:T(8,128)(2,1)S(1)} %add_convert_fusion.6), channel_id=1, source_target_pairs={{0,24},{1,29},{2,26},{3,31},{4,28},{5,25},{6,30},{7,27},{8,0},{9,5... | collective-permute-start | bytes 196616 | tf_op jit(solution)/shard_map/ppermute | solution.py:28
  16.5 5.3 %collective-permute-start.7 = (bf16[64,512]{1,0:T(8,128)(2,1)S(1)}, bf16[64,512]{1,0:T(8,128)(2,1)S(1)}, u32[]{:S(2)}, u32[]{:S(2)}) collective-permute-start(bf16[64,512]{1,0:T(8,128)(2,1)S(1)} %add_convert_fusion.6), channel_id=1, source_target_pairs={{0,26},{1,31},{2,24},{3,29},{4,30},{5,27},{6,28},{7,25},{8,2},{9,7... | collective-permute-start | bytes 196616 | tf_op jit(solution)/shard_map/ppermute | solution.py:28
  16.5 7.1 %collective-permute-start.4 = (bf16[64,512]{1,0:T(8,128)(2,1)S(1)}, bf16[64,512]{1,0:T(8,128)(2,1)S(1)}, u32[]{:S(2)}, u32[]{:S(2)}) collective-permute-start(bf16[64,512]{1,0:T(8,128)(2,1)S(1)} %pad_maximum_fusion), channel_id=1, source_target_pairs={{0,24},{1,25},{2,26},{3,27},{4,28},{5,29},{6,30},{7,31},{8,0},{9,1... | collective-permute-start | bytes 196616 | tf_op jit(solution)/shard_map/ppermute | solution.py:28
  21.8 2.2 %collective-permute-start.8 = (bf16[64,512]{1,0:T(8,128)(2,1)S(1)}, bf16[64,512]{1,0:T(8,128)(2,1)S(1)}, u32[]{:S(2)}, u32[]{:S(2)}) collective-permute-start(bf16[64,512]{1,0:T(8,128)(2,1)S(1)} %add_convert_fusion.5), channel_id=1, source_target_pairs={{0,1},{1,0},{2,3},{3,2},{4,5},{5,4},{6,7},{7,6},{8,9},{9,8},{10,11... | collective-permute-start | bytes 196616 | tf_op jit(solution)/shard_map/ppermute | solution.py:28
  24.8 1.3 %collective-permute-start.10 = (bf16[64,512]{1,0:T(8,128)(2,1)S(1)}, bf16[64,512]{1,0:T(8,128)(2,1)S(1)}, u32[]{:S(2)}, u32[]{:S(2)}) collective-permute-start(bf16[64,512]{1,0:T(8,128)(2,1)S(1)} %get-tuple-element.27), channel_id=1, source_target_pairs={{0,1},{1,0},{2,3},{3,2},{4,5},{5,4},{6,7},{7,6},{8,9},{9,8},{10,11... | collective-permute-start | bytes 196616 | tf_op jit(solution)/shard_map/ppermute | solution.py:28
  26.1 4.3 %collective-permute-start.11 = (bf16[64,512]{1,0:T(8,128)(2,1)S(1)}, bf16[64,512]{1,0:T(8,128)(2,1)S(1)}, u32[]{:S(2)}, u32[]{:S(2)}) collective-permute-start(bf16[64,512]{1,0:T(8,128)(2,1)S(1)} %add_convert_fusion.4), channel_id=1, source_target_pairs={{0,24},{1,29},{2,26},{3,31},{4,28},{5,25},{6,30},{7,27},{8,0},{9,5... | collective-permute-start | bytes 196616 | tf_op jit(solution)/shard_map/ppermute | solution.py:28
  27.7 5.3 %collective-permute-start.12 = (bf16[64,512]{1,0:T(8,128)(2,1)S(1)}, bf16[64,512]{1,0:T(8,128)(2,1)S(1)}, u32[]{:S(2)}, u32[]{:S(2)}) collective-permute-start(bf16[64,512]{1,0:T(8,128)(2,1)S(1)} %add_convert_fusion.4), channel_id=1, source_target_pairs={{0,26},{1,31},{2,24},{3,29},{4,30},{5,27},{6,28},{7,25},{8,2},{9,7... | collective-permute-start | bytes 196616 | tf_op jit(solution)/shard_map/ppermute | solution.py:28
  27.7 7.2 %collective-permute-start.9 = (bf16[64,512]{1,0:T(8,128)(2,1)S(1)}, bf16[64,512]{1,0:T(8,128)(2,1)S(1)}, u32[]{:S(2)}, u32[]{:S(2)}) collective-permute-start(bf16[64,512]{1,0:T(8,128)(2,1)S(1)} %subtract_convert_fusion.6), channel_id=1, source_target_pairs={{0,24},{1,25},{2,26},{3,27},{4,28},{5,29},{6,30},{7,31},{8,0},{9,1... | collective-permute-start | bytes 196616 | tf_op jit(solution)/shard_map/ppermute | solution.py:28
  33.0 2.3 %collective-permute-start.13 = (bf16[64,512]{1,0:T(8,128)(2,1)S(1)}, bf16[64,512]{1,0:T(8,128)(2,1)S(1)}, u32[]{:S(2)}, u32[]{:S(2)}) collective-permute-start(bf16[64,512]{1,0:T(8,128)(2,1)S(1)} %add_convert_fusion.3), channel_id=1, source_target_pairs={{0,1},{1,0},{2,3},{3,2},{4,5},{5,4},{6,7},{7,6},{8,9},{9,8},{10,11... | collective-permute-start | bytes 196616 | tf_op jit(solution)/shard_map/ppermute | solution.py:28
  36.1 1.3 %collective-permute-start.15 = (bf16[64,512]{1,0:T(8,128)(2,1)S(1)}, bf16[64,512]{1,0:T(8,128)(2,1)S(1)}, u32[]{:S(2)}, u32[]{:S(2)}) collective-permute-start(bf16[64,512]{1,0:T(8,128)(2,1)S(1)} %get-tuple-element.29), channel_id=1, source_target_pairs={{0,1},{1,0},{2,3},{3,2},{4,5},{5,4},{6,7},{7,6},{8,9},{9,8},{10,11... | collective-permute-start | bytes 196616 | tf_op jit(solution)/shard_map/ppermute | solution.py:28
  37.5 4.3 %collective-permute-start.16 = (bf16[64,512]{1,0:T(8,128)(2,1)S(1)}, bf16[64,512]{1,0:T(8,128)(2,1)S(1)}, u32[]{:S(2)}, u32[]{:S(2)}) collective-permute-start(bf16[64,512]{1,0:T(8,128)(2,1)S(1)} %add_convert_fusion.2), channel_id=1, source_target_pairs={{0,24},{1,29},{2,26},{3,31},{4,28},{5,25},{6,30},{7,27},{8,0},{9,5... | collective-permute-start | bytes 196616 | tf_op jit(solution)/shard_map/ppermute | solution.py:28
  39.1 5.3 %collective-permute-start.17 = (bf16[64,512]{1,0:T(8,128)(2,1)S(1)}, bf16[64,512]{1,0:T(8,128)(2,1)S(1)}, u32[]{:S(2)}, u32[]{:S(2)}) collective-permute-start(bf16[64,512]{1,0:T(8,128)(2,1)S(1)} %add_convert_fusion.2), channel_id=1, source_target_pairs={{0,26},{1,31},{2,24},{3,29},{4,30},{5,27},{6,28},{7,25},{8,2},{9,7... | collective-permute-start | bytes 196616 | tf_op jit(solution)/shard_map/ppermute | solution.py:28
  39.5 6.6 %collective-permute-start.14 = (bf16[64,512]{1,0:T(8,128)(2,1)S(1)}, bf16[64,512]{1,0:T(8,128)(2,1)S(1)}, u32[]{:S(2)}, u32[]{:S(2)}) collective-permute-start(bf16[64,512]{1,0:T(8,128)(2,1)S(1)} %subtract_convert_fusion.5), channel_id=1, source_target_pairs={{0,24},{1,25},{2,26},{3,27},{4,28},{5,29},{6,30},{7,31},{8,0},{9,1... | collective-permute-start | bytes 196616 | tf_op jit(solution)/shard_map/ppermute | solution.py:28
  44.4 2.2 %collective-permute-start.18 = (bf16[64,512]{1,0:T(8,128)(2,1)S(1)}, bf16[64,512]{1,0:T(8,128)(2,1)S(1)}, u32[]{:S(2)}, u32[]{:S(2)}) collective-permute-start(bf16[64,512]{1,0:T(8,128)(2,1)S(1)} %add_convert_fusion.1), channel_id=1, source_target_pairs={{0,1},{1,0},{2,3},{3,2},{4,5},{5,4},{6,7},{7,6},{8,9},{9,8},{10,11... | collective-permute-start | bytes 196616 | tf_op jit(solution)/shard_map/ppermute | solution.py:28
  47.4 1.3 %collective-permute-start.20 = (bf16[64,512]{1,0:T(8,128)(2,1)S(1)}, bf16[64,512]{1,0:T(8,128)(2,1)S(1)}, u32[]{:S(2)}, u32[]{:S(2)}) collective-permute-start(bf16[64,512]{1,0:T(8,128)(2,1)S(1)} %get-tuple-element.31), channel_id=1, source_target_pairs={{0,1},{1,0},{2,3},{3,2},{4,5},{5,4},{6,7},{7,6},{8,9},{9,8},{10,11... | collective-permute-start | bytes 196616 | tf_op jit(solution)/shard_map/ppermute | solution.py:28
  48.7 3.9 %collective-permute-start.21 = (bf16[16,512]{1,0:T(8,128)(2,1)S(1)}, bf16[16,512]{1,0:T(8,128)(2,1)S(1)}, u32[]{:S(2)}, u32[]{:S(2)}) collective-permute-start(bf16[16,512]{1,0:T(8,128)(2,1)S(1)} %get-tuple-element.13), channel_id=1, source_target_pairs={{0,24},{1,29},{2,26},{3,31},{4,28},{5,25},{6,30},{7,27},{8,0},{9,5... | collective-permute-start | bytes 49160 | tf_op jit(solution)/shard_map/ppermute | solution.py:28
  50.4 4.6 %collective-permute-start.22 = (bf16[16,512]{1,0:T(8,128)(2,1)S(1)}, bf16[16,512]{1,0:T(8,128)(2,1)S(1)}, u32[]{:S(2)}, u32[]{:S(2)}) collective-permute-start(bf16[16,512]{1,0:T(8,128)(2,1)S(1)} %get-tuple-element.14), channel_id=1, source_target_pairs={{0,26},{1,31},{2,24},{3,29},{4,30},{5,27},{6,28},{7,25},{8,2},{9,7... | collective-permute-start | bytes 49160 | tf_op jit(solution)/shard_map/ppermute | solution.py:28
  50.8 7.0 %collective-permute-start.19 = (bf16[8,512]{1,0:T(8,128)(2,1)S(1)}, bf16[8,512]{1,0:T(8,128)(2,1)S(1)}, u32[]{:S(2)}, u32[]{:S(2)}) collective-permute-start(bf16[8,512]{1,0:T(8,128)(2,1)S(1)} %constant_dynamic-slice_fusion), channel_id=1, source_target_pairs={{0,24},{1,25},{2,26},{3,27},{4,28},{5,29},{6,30},{7,31},{8,0},{9,1... | collective-permute-start | bytes 24584 | tf_op jit(solution)/shard_map/ppermute | solution.py:28
  55.1 2.7 %collective-permute-start.23 = (bf16[8,512]{1,0:T(8,128)(2,1)S(1)}, bf16[8,512]{1,0:T(8,128)(2,1)S(1)}, u32[]{:S(2)}, u32[]{:S(2)}) collective-permute-start(bf16[8,512]{1,0:T(8,128)(2,1)S(1)} %dynamic-slice_convert_fusion), channel_id=1, source_target_pairs={{0,1},{1,0},{2,3},{3,2},{4,5},{5,4},{6,7},{7,6},{8,9},{9,8},{10,11... | collective-permute-start | bytes 24584 | tf_op jit(solution)/shard_map/ppermute | solution.py:28
  (2 other events, 12.6 us)

commit v5 on v4

--- a/solution.py
+++ b/solution.py
@@ -72,7 +72,6 @@
     cross = jnp.where(core == 0, other[rows:], more)
     side, end = me // bit % 2, me // top
     whole = in_order(in_order(block, near, side), in_order(far, cross, side), end)
-    whole = lax.optimization_barrier(whole)
     tiles = [ratings[:, step, :] for step in range(steps)]
     tiles[0] = lax.optimization_barrier(shown[:, 0, :])
 
@@ -93,8 +92,8 @@
             grads = grads + wide(swap(total, bit))
             total = narrow(grads)
             bit *= 2
-        first = (0, top)
-        second = (bit, bit + top)
+        first = (0, top) if not last else (bit, top)
+        second = (bit, bit + top) if not last else (0, bit + top)
 
         def part(flip):
             return rows_of(total, (place ^ flip // 2) * 2 * own, 2 * own)

time: 58.6 us -> 58.6 us (level)
  waiting for transfers between devices: 21.5 us -> 20.3 us
  starting transfers between devices: 27.3 us -> 28.4 us
    ppermute x24, waiting for transfers between devices: 21.5 us -> 20.3 us  [route(): return lax.ppermute(block, AXES, pairs)]
    ppermute x24, starting transfers between devices: 27.3 us -> 28.4 us  [route(): return lax.ppermute(block, AXES, pairs)]
  transfers between devices with their start and end apart: 24 -> 24, of which waited for: 18 -> 19; matrix products, arithmetic and copies ran while one was open for 7% -> 7% of each run, Pallas kernels for 0% -> 0%
where the time goes in v5:
time: 58.6 us; the launch traced here: 58.3 us
  starting transfers between devices  28.4 us (48%)
  waiting for transfers between devices  20.3 us (35%)
  matrix products  5.79 us (10%)
  other arithmetic  2.93 us (5%)
  between operations  0.82 us (1%)
    ppermute x24, starting transfers between devices, route(): return lax.ppermute(block, AXES, pairs)  28.4 us
    ppermute x24, waiting for transfers between devices, route(): return lax.ppermute(block, AXES, pairs)  20.3 us
    dot_general x4, matrix products, local(): change = jnp.dot(resid, whole, preferred_element_type=jnp.float32)  2.81 us
    dot_general x4, matrix products, local(): lax.dot_general(users, whole, (((1,), (1,)), ((), ())), preferred_element...  1.77 us
    mul x1, other arithmetic, local(): users = lax.optimization_barrier(users * one)  1.29 us
    dot_general x4, matrix products, local(): lax.dot_general(resid, users, (((0,), (0,)), ((), ())), preferred_element...  1.21 us
  transfers between devices with their start and end apart: 24, of which 19 were waited for; matrix products, arithmetic and copies ran while one was open for 7% of the time, Pallas kernels for 0%

profile of v5, /device:TPU:0, one launch (start us, length us, event | category | flops | bytes accessed | tf_op | source)
XLA Modules:
  0.0 58.3 jit_solution(15219253798135696887)
XLA Ops:
  2.7 3.0 %collective-permute-start.1 = (bf16[16,512]{1,0:T(8,128)(2,1)S(1)}, bf16[16,512]{1,0:T(8,128)(2,1)S(1)}, u32[]{:S(2)}, u32[]{:S(2)}) collective-permute-start(bf16[16,512]{1,0:T(8,128)(2,1)S(1)} %pad_maximum_fusion.4), channel_id=1, source_target_pairs={{0,2},{1,5},{2,0},{3,7},{4,6},{5,1},{6,4},{7,3},{8,10},{9,13},{10,... | collective-permute-start | bytes 49160 | tf_op jit(solution)/shard_map/ppermute | solution.py:28
  5.8 1.3 %broadcast_multiply_fusion = bf16[1024,512]{1,0:T(8,128)(2,1)S(1)} fusion(bf16[1024,512]{1,0:T(8,128)(2,1)} %param.4, bf16[]{:T(256)} %constant.64.clone.1), kind=kLoop, calls=%fused_computation.25 | loop fusion | flops 524288 | bytes 2097154 | tf_op jit(solution)/shard_map/mul | solution.py:60
  7.4 2.0 %collective-permute-done.2 = bf16[16,512]{1,0:T(8,128)(2,1)S(1)} collective-permute-done((bf16[16,512]{1,0:T(8,128)(2,1)S(1)}, bf16[16,512]{1,0:T(8,128)(2,1)S(1)}, u32[]{:S(2)}, u32[]{:S(2)}) %collective-permute-start.2) | collective-permute-done | bytes 16416 | tf_op jit(solution)/shard_map/ppermute | solution.py:28
  9.4 1.5 %collective-permute-start.3 = (bf16[32,512]{1,0:T(8,128)(2,1)S(1)}, bf16[32,512]{1,0:T(8,128)(2,1)S(1)}, u32[]{:S(2)}, u32[]{:S(2)}) collective-permute-start(bf16[32,512]{1,0:T(8,128)(2,1)S(1)} %pad_maximum_fusion.1), channel_id=1, source_target_pairs={{0,1},{1,0},{2,3},{3,2},{4,5},{5,4},{6,7},{7,6},{8,9},{9,8},{10,11... | collective-permute-start | bytes 98312 | tf_op jit(solution)/shard_map/ppermute | solution.py:28
  13.0 0.9 %collective-permute-done.5 = bf16[64,512]{1,0:T(8,128)(2,1)S(1)} collective-permute-done((bf16[64,512]{1,0:T(8,128)(2,1)S(1)}, bf16[64,512]{1,0:T(8,128)(2,1)S(1)}, u32[]{:S(2)}, u32[]{:S(2)}) %collective-permute-start.5) | collective-permute-done | bytes 65568 | tf_op jit(solution)/shard_map/ppermute | solution.py:28
  14.0 2.5 %collective-permute-start.6 = (bf16[64,512]{1,0:T(8,128)(2,1)S(1)}, bf16[64,512]{1,0:T(8,128)(2,1)S(1)}, u32[]{:S(2)}, u32[]{:S(2)}) collective-permute-start(bf16[64,512]{1,0:T(8,128)(2,1)S(1)} %add_convert_fusion.6), channel_id=1, source_target_pairs={{0,24},{1,29},{2,26},{3,31},{4,28},{5,25},{6,30},{7,27},{8,0},{9,5... | collective-permute-start | bytes 196616 | tf_op jit(solution)/shard_map/ppermute | solution.py:28
  16.5 1.2 %collective-permute-start.4 = (bf16[64,512]{1,0:T(8,128)(2,1)S(1)}, bf16[64,512]{1,0:T(8,128)(2,1)S(1)}, u32[]{:S(2)}, u32[]{:S(2)}) collective-permute-start(bf16[64,512]{1,0:T(8,128)(2,1)S(1)} %pad_maximum_fusion), channel_id=1, source_target_pairs={{0,24},{1,25},{2,26},{3,27},{4,28},{5,29},{6,30},{7,31},{8,0},{9,1... | collective-permute-start | bytes 196616 | tf_op jit(solution)/shard_map/ppermute | solution.py:28
  18.4 3.4 %collective-permute-done.7 = bf16[64,512]{1,0:T(8,128)(2,1)S(1)} collective-permute-done((bf16[64,512]{1,0:T(8,128)(2,1)S(1)}, bf16[64,512]{1,0:T(8,128)(2,1)S(1)}, u32[]{:S(2)}, u32[]{:S(2)}) %collective-permute-start.7) | collective-permute-done | bytes 65568 | tf_op jit(solution)/shard_map/ppermute | solution.py:28
  21.7 1.3 %collective-permute-start.8 = (bf16[64,512]{1,0:T(8,128)(2,1)S(1)}, bf16[64,512]{1,0:T(8,128)(2,1)S(1)}, u32[]{:S(2)}, u32[]{:S(2)}) collective-permute-start(bf16[64,512]{1,0:T(8,128)(2,1)S(1)} %add_convert_fusion.5), channel_id=1, source_target_pairs={{0,1},{1,0},{2,3},{3,2},{4,5},{5,4},{6,7},{7,6},{8,9},{9,8},{10,11... | collective-permute-start | bytes 196616 | tf_op jit(solution)/shard_map/ppermute | solution.py:28
  25.2 0.9 %collective-permute-done.10 = bf16[64,512]{1,0:T(8,128)(2,1)S(1)} collective-permute-done((bf16[64,512]{1,0:T(8,128)(2,1)S(1)}, bf16[64,512]{1,0:T(8,128)(2,1)S(1)}, u32[]{:S(2)}, u32[]{:S(2)}) %collective-permute-start.10) | collective-permute-done | bytes 65568 | tf_op jit(solution)/shard_map/ppermute | solution.py:28
  26.1 1.6 %collective-permute-start.11 = (bf16[64,512]{1,0:T(8,128)(2,1)S(1)}, bf16[64,512]{1,0:T(8,128)(2,1)S(1)}, u32[]{:S(2)}, u32[]{:S(2)}) collective-permute-start(bf16[64,512]{1,0:T(8,128)(2,1)S(1)} %add_convert_fusion.4), channel_id=1, source_target_pairs={{0,24},{1,29},{2,26},{3,31},{4,28},{5,25},{6,30},{7,27},{8,0},{9,5... | collective-permute-start | bytes 196616 | tf_op jit(solution)/shard_map/ppermute | solution.py:28
  27.7 2.3 %collective-permute-start.9 = (bf16[64,512]{1,0:T(8,128)(2,1)S(1)}, bf16[64,512]{1,0:T(8,128)(2,1)S(1)}, u32[]{:S(2)}, u32[]{:S(2)}) collective-permute-start(bf16[64,512]{1,0:T(8,128)(2,1)S(1)} %subtract_convert_fusion.6), channel_id=1, source_target_pairs={{0,24},{1,25},{2,26},{3,27},{4,28},{5,29},{6,30},{7,31},{8,0},{9,1... | collective-permute-start | bytes 196616 | tf_op jit(solution)/shard_map/ppermute | solution.py:28
  30.4 2.6 %collective-permute-done.12 = bf16[64,512]{1,0:T(8,128)(2,1)S(1)} collective-permute-done((bf16[64,512]{1,0:T(8,128)(2,1)S(1)}, bf16[64,512]{1,0:T(8,128)(2,1)S(1)}, u32[]{:S(2)}, u32[]{:S(2)}) %collective-permute-start.12) | collective-permute-done | bytes 65568 | tf_op jit(solution)/shard_map/ppermute | solution.py:28
  33.0 1.4 %collective-permute-start.13 = (bf16[64,512]{1,0:T(8,128)(2,1)S(1)}, bf16[64,512]{1,0:T(8,128)(2,1)S(1)}, u32[]{:S(2)}, u32[]{:S(2)}) collective-permute-start(bf16[64,512]{1,0:T(8,128)(2,1)S(1)} %add_convert_fusion.3), channel_id=1, source_target_pairs={{0,1},{1,0},{2,3},{3,2},{4,5},{5,4},{6,7},{7,6},{8,9},{9,8},{10,11... | collective-permute-start | bytes 196616 | tf_op jit(solution)/shard_map/ppermute | solution.py:28
  36.5 0.9 %collective-permute-done.15 = bf16[64,512]{1,0:T(8,128)(2,1)S(1)} collective-permute-done((bf16[64,512]{1,0:T(8,128)(2,1)S(1)}, bf16[64,512]{1,0:T(8,128)(2,1)S(1)}, u32[]{:S(2)}, u32[]{:S(2)}) %collective-permute-start.15) | collective-permute-done | bytes 65568 | tf_op jit(solution)/shard_map/ppermute | solution.py:28
  37.5 1.6 %collective-permute-start.16 = (bf16[64,512]{1,0:T(8,128)(2,1)S(1)}, bf16[64,512]{1,0:T(8,128)(2,1)S(1)}, u32[]{:S(2)}, u32[]{:S(2)}) collective-permute-start(bf16[64,512]{1,0:T(8,128)(2,1)S(1)} %add_convert_fusion.2), channel_id=1, source_target_pairs={{0,24},{1,29},{2,26},{3,31},{4,28},{5,25},{6,30},{7,27},{8,0},{9,5... | collective-permute-start | bytes 196616 | tf_op jit(solution)/shard_map/ppermute | solution.py:28
  39.5 1.8 %collective-permute-start.14 = (bf16[64,512]{1,0:T(8,128)(2,1)S(1)}, bf16[64,512]{1,0:T(8,128)(2,1)S(1)}, u32[]{:S(2)}, u32[]{:S(2)}) collective-permute-start(bf16[64,512]{1,0:T(8,128)(2,1)S(1)} %subtract_convert_fusion.5), channel_id=1, source_target_pairs={{0,24},{1,25},{2,26},{3,27},{4,28},{5,29},{6,30},{7,31},{8,0},{9,1... | collective-permute-start | bytes 196616 | tf_op jit(solution)/shard_map/ppermute | solution.py:28
  41.8 2.6 %collective-permute-done.17 = bf16[64,512]{1,0:T(8,128)(2,1)S(1)} collective-permute-done((bf16[64,512]{1,0:T(8,128)(2,1)S(1)}, bf16[64,512]{1,0:T(8,128)(2,1)S(1)}, u32[]{:S(2)}, u32[]{:S(2)}) %collective-permute-start.17) | collective-permute-done | bytes 65568 | tf_op jit(solution)/shard_map/ppermute | solution.py:28
  44.4 1.3 %collective-permute-start.18 = (bf16[64,512]{1,0:T(8,128)(2,1)S(1)}, bf16[64,512]{1,0:T(8,128)(2,1)S(1)}, u32[]{:S(2)}, u32[]{:S(2)}) collective-permute-start(bf16[64,512]{1,0:T(8,128)(2,1)S(1)} %add_convert_fusion.1), channel_id=1, source_target_pairs={{0,1},{1,0},{2,3},{3,2},{4,5},{5,4},{6,7},{7,6},{8,9},{9,8},{10,11... | collective-permute-start | bytes 196616 | tf_op jit(solution)/shard_map/ppermute | solution.py:28
  47.8 0.9 %collective-permute-done.20 = bf16[64,512]{1,0:T(8,128)(2,1)S(1)} collective-permute-done((bf16[64,512]{1,0:T(8,128)(2,1)S(1)}, bf16[64,512]{1,0:T(8,128)(2,1)S(1)}, u32[]{:S(2)}, u32[]{:S(2)}) %collective-permute-start.20) | collective-permute-done | bytes 65568 | tf_op jit(solution)/shard_map/ppermute | solution.py:28
  48.7 1.3 %collective-permute-start.21 = (bf16[16,512]{1,0:T(8,128)(2,1)S(1)}, bf16[16,512]{1,0:T(8,128)(2,1)S(1)}, u32[]{:S(2)}, u32[]{:S(2)}) collective-permute-start(bf16[16,512]{1,0:T(8,128)(2,1)S(1)} %get-tuple-element.13), channel_id=1, source_target_pairs={{0,26},{1,29},{2,24},{3,31},{4,30},{5,25},{6,28},{7,27},{8,2},{9,5... | collective-permute-start | bytes 49160 | tf_op jit(solution)/shard_map/ppermute | solution.py:28
  50.7 1.8 %collective-permute-start.19 = (bf16[8,512]{1,0:T(8,128)(2,1)S(1)}, bf16[8,512]{1,0:T(8,128)(2,1)S(1)}, u32[]{:S(2)}, u32[]{:S(2)}) collective-permute-start(bf16[8,512]{1,0:T(8,128)(2,1)S(1)} %constant_dynamic-slice_fusion), channel_id=1, source_target_pairs={{0,24},{1,25},{2,26},{3,27},{4,28},{5,29},{6,30},{7,31},{8,0},{9,1... | collective-permute-start | bytes 24584 | tf_op jit(solution)/shard_map/ppermute | solution.py:28
  53.9 2.4 %collective-permute-start.23 = (bf16[8,512]{1,0:T(8,128)(2,1)S(1)}, bf16[8,512]{1,0:T(8,128)(2,1)S(1)}, u32[]{:S(2)}, u32[]{:S(2)}) collective-permute-start(bf16[8,512]{1,0:T(8,128)(2,1)S(1)} %dynamic-slice_convert_fusion), channel_id=1, source_target_pairs={{0,1},{1,0},{2,3},{3,2},{4,5},{5,4},{6,7},{7,6},{8,9},{9,8},{10,11... | collective-permute-start | bytes 24584 | tf_op jit(solution)/shard_map/ppermute | solution.py:28
  56.3 1.4 %subtract_convert_fusion = bf16[1024,512]{1,0:T(8,128)(2,1)} fusion(bf16[1024,512]{1,0:T(8,128)(2,1)S(1)} %subtract_convert_fusion.1, bf16[1024,64]{0,1:T(8,128)(2,1)S(1)} %fusion.11, bf16[64,512]{1,0:T(8,128)(2,1)S(1)} %subtract_convert_fusion.4), kind=kOutput, calls=%fused_computation | convolution fusion | flops 69206016 | bytes 2293760 | tf_op jit(solution)/shard_map/dot_general | solution.py:113
  (66 shorter events, 15.5 us)
Async XLA Ops:
  1.4 1.3 %collective-permute-start = (bf16[8,512]{1,0:T(8,128)(2,1)S(1)}, bf16[8,512]{1,0:T(8,128)(2,1)S(1)}, u32[]{:S(2)}, u32[]{:S(2)}) collective-permute-start(bf16[8,512]{1,0:T(8,128)(2,1)S(1)} %convert_element_type.174), channel_id=1, source_target_pairs={{0,1},{1,0},{2,3},{3,2},{4,5},{5,4},{6,7},{7,6},{8,9},{9,8},{10,11... | collective-permute-start | bytes 24584 | tf_op jit(solution)/shard_map/ppermute | solution.py:28
  2.7 4.7 %collective-permute-start.1 = (bf16[16,512]{1,0:T(8,128)(2,1)S(1)}, bf16[16,512]{1,0:T(8,128)(2,1)S(1)}, u32[]{:S(2)}, u32[]{:S(2)}) collective-permute-start(bf16[16,512]{1,0:T(8,128)(2,1)S(1)} %pad_maximum_fusion.4), channel_id=1, source_target_pairs={{0,2},{1,5},{2,0},{3,7},{4,6},{5,1},{6,4},{7,3},{8,10},{9,13},{10,... | collective-permute-start | bytes 49160 | tf_op jit(solution)/shard_map/ppermute | solution.py:28
  5.7 3.7 %collective-permute-start.2 = (bf16[16,512]{1,0:T(8,128)(2,1)S(1)}, bf16[16,512]{1,0:T(8,128)(2,1)S(1)}, u32[]{:S(2)}, u32[]{:S(2)}) collective-permute-start(bf16[16,512]{1,0:T(8,128)(2,1)S(1)} %pad_maximum_fusion.4), channel_id=1, source_target_pairs={{0,2},{1,7},{2,0},{3,5},{4,6},{5,3},{6,4},{7,1},{8,10},{9,15},{10,... | collective-permute-start | bytes 49160 | tf_op jit(solution)/shard_map/ppermute | solution.py:28
  9.4 2.4 %collective-permute-start.3 = (bf16[32,512]{1,0:T(8,128)(2,1)S(1)}, bf16[32,512]{1,0:T(8,128)(2,1)S(1)}, u32[]{:S(2)}, u32[]{:S(2)}) collective-permute-start(bf16[32,512]{1,0:T(8,128)(2,1)S(1)} %pad_maximum_fusion.1), channel_id=1, source_target_pairs={{0,1},{1,0},{2,3},{3,2},{4,5},{5,4},{6,7},{7,6},{8,9},{9,8},{10,11... | collective-permute-start | bytes 98312 | tf_op jit(solution)/shard_map/ppermute | solution.py:28
  12.6 1.3 %collective-permute-start.5 = (bf16[64,512]{1,0:T(8,128)(2,1)S(1)}, bf16[64,512]{1,0:T(8,128)(2,1)S(1)}, u32[]{:S(2)}, u32[]{:S(2)}) collective-permute-start(bf16[64,512]{1,0:T(8,128)(2,1)S(1)} %get-tuple-element.25), channel_id=1, source_target_pairs={{0,1},{1,0},{2,3},{3,2},{4,5},{5,4},{6,7},{7,6},{8,9},{9,8},{10,11... | collective-permute-start | bytes 196616 | tf_op jit(solution)/shard_map/ppermute | solution.py:28
  14.0 4.4 %collective-permute-start.6 = (bf16[64,512]{1,0:T(8,128)(2,1)S(1)}, bf16[64,512]{1,0:T(8,128)(2,1)S(1)}, u32[]{:S(2)}, u32[]{:S(2)}) collective-permute-start(bf16[64,512]{1,0:T(8,128)(2,1)S(1)} %add_convert_fusion.6), channel_id=1, source_target_pairs={{0,24},{1,29},{2,26},{3,31},{4,28},{5,25},{6,30},{7,27},{8,0},{9,5... | collective-permute-start | bytes 196616 | tf_op jit(solution)/shard_map/ppermute | solution.py:28
  16.5 5.3 %collective-permute-start.7 = (bf16[64,512]{1,0:T(8,128)(2,1)S(1)}, bf16[64,512]{1,0:T(8,128)(2,1)S(1)}, u32[]{:S(2)}, u32[]{:S(2)}) collective-permute-start(bf16[64,512]{1,0:T(8,128)(2,1)S(1)} %add_convert_fusion.6), channel_id=1, source_target_pairs={{0,26},{1,31},{2,24},{3,29},{4,30},{5,27},{6,28},{7,25},{8,2},{9,7... | collective-permute-start | bytes 196616 | tf_op jit(solution)/shard_map/ppermute | solution.py:28
  16.5 7.1 %collective-permute-start.4 = (bf16[64,512]{1,0:T(8,128)(2,1)S(1)}, bf16[64,512]{1,0:T(8,128)(2,1)S(1)}, u32[]{:S(2)}, u32[]{:S(2)}) collective-permute-start(bf16[64,512]{1,0:T(8,128)(2,1)S(1)} %pad_maximum_fusion), channel_id=1, source_target_pairs={{0,24},{1,25},{2,26},{3,27},{4,28},{5,29},{6,30},{7,31},{8,0},{9,1... | collective-permute-start | bytes 196616 | tf_op jit(solution)/shard_map/ppermute | solution.py:28
  21.7 2.2 %collective-permute-start.8 = (bf16[64,512]{1,0:T(8,128)(2,1)S(1)}, bf16[64,512]{1,0:T(8,128)(2,1)S(1)}, u32[]{:S(2)}, u32[]{:S(2)}) collective-permute-start(bf16[64,512]{1,0:T(8,128)(2,1)S(1)} %add_convert_fusion.5), channel_id=1, source_target_pairs={{0,1},{1,0},{2,3},{3,2},{4,5},{5,4},{6,7},{7,6},{8,9},{9,8},{10,11... | collective-permute-start | bytes 196616 | tf_op jit(solution)/shard_map/ppermute | solution.py:28
  24.8 1.3 %collective-permute-start.10 = (bf16[64,512]{1,0:T(8,128)(2,1)S(1)}, bf16[64,512]{1,0:T(8,128)(2,1)S(1)}, u32[]{:S(2)}, u32[]{:S(2)}) collective-permute-start(bf16[64,512]{1,0:T(8,128)(2,1)S(1)} %get-tuple-element.27), channel_id=1, source_target_pairs={{0,1},{1,0},{2,3},{3,2},{4,5},{5,4},{6,7},{7,6},{8,9},{9,8},{10,11... | collective-permute-start | bytes 196616 | tf_op jit(solution)/shard_map/ppermute | solution.py:28
  26.1 4.3 %collective-permute-start.11 = (bf16[64,512]{1,0:T(8,128)(2,1)S(1)}, bf16[64,512]{1,0:T(8,128)(2,1)S(1)}, u32[]{:S(2)}, u32[]{:S(2)}) collective-permute-start(bf16[64,512]{1,0:T(8,128)(2,1)S(1)} %add_convert_fusion.4), channel_id=1, source_target_pairs={{0,24},{1,29},{2,26},{3,31},{4,28},{5,25},{6,30},{7,27},{8,0},{9,5... | collective-permute-start | bytes 196616 | tf_op jit(solution)/shard_map/ppermute | solution.py:28
  27.7 5.3 %collective-permute-start.12 = (bf16[64,512]{1,0:T(8,128)(2,1)S(1)}, bf16[64,512]{1,0:T(8,128)(2,1)S(1)}, u32[]{:S(2)}, u32[]{:S(2)}) collective-permute-start(bf16[64,512]{1,0:T(8,128)(2,1)S(1)} %add_convert_fusion.4), channel_id=1, source_target_pairs={{0,26},{1,31},{2,24},{3,29},{4,30},{5,27},{6,28},{7,25},{8,2},{9,7... | collective-permute-start | bytes 196616 | tf_op jit(solution)/shard_map/ppermute | solution.py:28
  27.7 7.2 %collective-permute-start.9 = (bf16[64,512]{1,0:T(8,128)(2,1)S(1)}, bf16[64,512]{1,0:T(8,128)(2,1)S(1)}, u32[]{:S(2)}, u32[]{:S(2)}) collective-permute-start(bf16[64,512]{1,0:T(8,128)(2,1)S(1)} %subtract_convert_fusion.6), channel_id=1, source_target_pairs={{0,24},{1,25},{2,26},{3,27},{4,28},{5,29},{6,30},{7,31},{8,0},{9,1... | collective-permute-start | bytes 196616 | tf_op jit(solution)/shard_map/ppermute | solution.py:28
  33.0 2.3 %collective-permute-start.13 = (bf16[64,512]{1,0:T(8,128)(2,1)S(1)}, bf16[64,512]{1,0:T(8,128)(2,1)S(1)}, u32[]{:S(2)}, u32[]{:S(2)}) collective-permute-start(bf16[64,512]{1,0:T(8,128)(2,1)S(1)} %add_convert_fusion.3), channel_id=1, source_target_pairs={{0,1},{1,0},{2,3},{3,2},{4,5},{5,4},{6,7},{7,6},{8,9},{9,8},{10,11... | collective-permute-start | bytes 196616 | tf_op jit(solution)/shard_map/ppermute | solution.py:28
  36.1 1.3 %collective-permute-start.15 = (bf16[64,512]{1,0:T(8,128)(2,1)S(1)}, bf16[64,512]{1,0:T(8,128)(2,1)S(1)}, u32[]{:S(2)}, u32[]{:S(2)}) collective-permute-start(bf16[64,512]{1,0:T(8,128)(2,1)S(1)} %get-tuple-element.29), channel_id=1, source_target_pairs={{0,1},{1,0},{2,3},{3,2},{4,5},{5,4},{6,7},{7,6},{8,9},{9,8},{10,11... | collective-permute-start | bytes 196616 | tf_op jit(solution)/shard_map/ppermute | solution.py:28
  37.5 4.3 %collective-permute-start.16 = (bf16[64,512]{1,0:T(8,128)(2,1)S(1)}, bf16[64,512]{1,0:T(8,128)(2,1)S(1)}, u32[]{:S(2)}, u32[]{:S(2)}) collective-permute-start(bf16[64,512]{1,0:T(8,128)(2,1)S(1)} %add_convert_fusion.2), channel_id=1, source_target_pairs={{0,24},{1,29},{2,26},{3,31},{4,28},{5,25},{6,30},{7,27},{8,0},{9,5... | collective-permute-start | bytes 196616 | tf_op jit(solution)/shard_map/ppermute | solution.py:28
  39.1 5.3 %collective-permute-start.17 = (bf16[64,512]{1,0:T(8,128)(2,1)S(1)}, bf16[64,512]{1,0:T(8,128)(2,1)S(1)}, u32[]{:S(2)}, u32[]{:S(2)}) collective-permute-start(bf16[64,512]{1,0:T(8,128)(2,1)S(1)} %add_convert_fusion.2), channel_id=1, source_target_pairs={{0,26},{1,31},{2,24},{3,29},{4,30},{5,27},{6,28},{7,25},{8,2},{9,7... | collective-permute-start | bytes 196616 | tf_op jit(solution)/shard_map/ppermute | solution.py:28
  39.5 6.6 %collective-permute-start.14 = (bf16[64,512]{1,0:T(8,128)(2,1)S(1)}, bf16[64,512]{1,0:T(8,128)(2,1)S(1)}, u32[]{:S(2)}, u32[]{:S(2)}) collective-permute-start(bf16[64,512]{1,0:T(8,128)(2,1)S(1)} %subtract_convert_fusion.5), channel_id=1, source_target_pairs={{0,24},{1,25},{2,26},{3,27},{4,28},{5,29},{6,30},{7,31},{8,0},{9,1... | collective-permute-start | bytes 196616 | tf_op jit(solution)/shard_map/ppermute | solution.py:28
  44.4 2.2 %collective-permute-start.18 = (bf16[64,512]{1,0:T(8,128)(2,1)S(1)}, bf16[64,512]{1,0:T(8,128)(2,1)S(1)}, u32[]{:S(2)}, u32[]{:S(2)}) collective-permute-start(bf16[64,512]{1,0:T(8,128)(2,1)S(1)} %add_convert_fusion.1), channel_id=1, source_target_pairs={{0,1},{1,0},{2,3},{3,2},{4,5},{5,4},{6,7},{7,6},{8,9},{9,8},{10,11... | collective-permute-start | bytes 196616 | tf_op jit(solution)/shard_map/ppermute | solution.py:28
  47.4 1.3 %collective-permute-start.20 = (bf16[64,512]{1,0:T(8,128)(2,1)S(1)}, bf16[64,512]{1,0:T(8,128)(2,1)S(1)}, u32[]{:S(2)}, u32[]{:S(2)}) collective-permute-start(bf16[64,512]{1,0:T(8,128)(2,1)S(1)} %get-tuple-element.31), channel_id=1, source_target_pairs={{0,1},{1,0},{2,3},{3,2},{4,5},{5,4},{6,7},{7,6},{8,9},{9,8},{10,11... | collective-permute-start | bytes 196616 | tf_op jit(solution)/shard_map/ppermute | solution.py:28
  48.7 4.7 %collective-permute-start.21 = (bf16[16,512]{1,0:T(8,128)(2,1)S(1)}, bf16[16,512]{1,0:T(8,128)(2,1)S(1)}, u32[]{:S(2)}, u32[]{:S(2)}) collective-permute-start(bf16[16,512]{1,0:T(8,128)(2,1)S(1)} %get-tuple-element.13), channel_id=1, source_target_pairs={{0,26},{1,29},{2,24},{3,31},{4,30},{5,25},{6,28},{7,27},{8,2},{9,5... | collective-permute-start | bytes 49160 | tf_op jit(solution)/shard_map/ppermute | solution.py:28
  50.1 3.8 %collective-permute-start.22 = (bf16[16,512]{1,0:T(8,128)(2,1)S(1)}, bf16[16,512]{1,0:T(8,128)(2,1)S(1)}, u32[]{:S(2)}, u32[]{:S(2)}) collective-permute-start(bf16[16,512]{1,0:T(8,128)(2,1)S(1)} %get-tuple-element.14), channel_id=1, source_target_pairs={{0,24},{1,31},{2,26},{3,29},{4,28},{5,27},{6,30},{7,25},{8,0},{9,7... | collective-permute-start | bytes 49160 | tf_op jit(solution)/shard_map/ppermute | solution.py:28
  50.7 7.0 %collective-permute-start.19 = (bf16[8,512]{1,0:T(8,128)(2,1)S(1)}, bf16[8,512]{1,0:T(8,128)(2,1)S(1)}, u32[]{:S(2)}, u32[]{:S(2)}) collective-permute-start(bf16[8,512]{1,0:T(8,128)(2,1)S(1)} %constant_dynamic-slice_fusion), channel_id=1, source_target_pairs={{0,24},{1,25},{2,26},{3,27},{4,28},{5,29},{6,30},{7,31},{8,0},{9,1... | collective-permute-start | bytes 24584 | tf_op jit(solution)/shard_map/ppermute | solution.py:28
  53.9 3.8 %collective-permute-start.23 = (bf16[8,512]{1,0:T(8,128)(2,1)S(1)}, bf16[8,512]{1,0:T(8,128)(2,1)S(1)}, u32[]{:S(2)}, u32[]{:S(2)}) collective-permute-start(bf16[8,512]{1,0:T(8,128)(2,1)S(1)} %dynamic-slice_convert_fusion), channel_id=1, source_target_pairs={{0,1},{1,0},{2,3},{3,2},{4,5},{5,4},{6,7},{7,6},{8,9},{9,8},{10,11... | collective-permute-start | bytes 24584 | tf_op jit(solution)/shard_map/ppermute | solution.py:28
  (2 other events, 12.6 us)
